TPU v7x, 256 devices: a whole 4x4x8 slice. The times are simulated.
256 devices in a mesh: dp: 32 (over y, z), tensor: 8 (over x, core).
Axes of the slice: x: 4, y: 4, z: 8, core: 2. Of those that a mesh axis runs over, the one named last changes fastest.
Arguments:
- queries: bfloat16 [256, 6, 8192], P('dp', None, 'tensor'), may hold values from -150 to 150
- new_keys: bfloat16 [256, 6, 1024], P('dp', None, 'tensor'), may hold values from -6 to 6
- new_values: bfloat16 [256, 6, 1024], P('dp', None, 'tensor'), may hold values from -6 to 6
- key_cache: bfloat16 [256, 256, 1024], P('dp', None, 'tensor'), may hold values from -6 to 6
- value_cache: bfloat16 [256, 256, 1024], P('dp', None, 'tensor'), may hold values from -6 to 6
- cache_lengths: int32 [256], P('dp'), may hold values from 32 to 256, as said below
- accepted: int32 [256], P('tensor'), may hold values from 1 to 6
- residual: bfloat16 [256, 6, 8192], P('tensor', None, 'dp'), may hold values from -6 to 6
- out_weight: bfloat16 [8192, 8192], P('tensor', 'dp'), may hold values from -0.0625 to 0.0625
- draft_weight: bfloat16 [8192, 8192], P('tensor', 'dp'), may hold values from -0.0625 to 0.0625
Outputs:
- verified: bfloat16 [256, 6, 8192], P('tensor', None, 'dp')
- drafted: bfloat16 [5, 256, 8192], P(None, 'tensor', 'dp')
Inputs may be any that keep to these rules, and one draw needn't show every extreme that they name: `cache_lengths`: every draw has a window with all 256 slots live.
All inputs are finite; a program needn't handle non-finite values.
Results may differ from a plain program's by a relative error of at most 0.008.
Values may be sent and summed in bfloat16 or wider, within the bound.
No kernel may reach another device: no remote copies, remote signals or barrier semaphores. Data moves between devices by JAX's collectives and lax.ppermute only.
A program may use at most 64 MiB of HBM per device.

v0:
```python
import jax
import jax.numpy as jnp
from jax import lax
from jax.sharding import PartitionSpec as P

HD = 128
STEPS = 5


def widen(drafted_rows):
    wide_rows = lax.all_gather(drafted_rows, "dp", axis=1, tiled=True)
    return lax.all_to_all(wide_rows, "tensor", split_axis=1, concat_axis=0, tiled=True)


def per_device(
    queries,
    new_keys,
    new_values,
    key_cache,
    value_cache,
    cache_lengths,
    accepted,
    residual,
    out_weight,
    draft_weight,
):
    windows_here, tokens_here, query_width = queries.shape
    cache_size = key_cache.shape[1]
    kv_here = new_keys.shape[2] // HD
    group_size = query_width // HD // kv_here
    query_split = queries.reshape(windows_here, tokens_here, kv_here, group_size, HD)
    keys_cached = key_cache.reshape(windows_here, cache_size, kv_here, HD)
    keys_fresh = new_keys.reshape(windows_here, tokens_here, kv_here, HD)
    score_cache = jnp.einsum(
        "wtkgd,wpkd->wkgtp", query_split, keys_cached, preferred_element_type=jnp.float32
    ) * HD ** (-0.5)
    score_fresh = jnp.einsum(
        "wtkgd,wpkd->wkgtp", query_split, keys_fresh, preferred_element_type=jnp.float32
    ) * HD ** (-0.5)
    live_cache = (jnp.arange(cache_size)[None, :] < cache_lengths[:, None])[:, None, None, None, :]
    live_fresh = jnp.arange(tokens_here)[None, :] <= jnp.arange(tokens_here)[:, None]
    scores = jnp.concatenate(
        [
            jnp.where(live_cache, score_cache, -jnp.inf),
            jnp.where(live_fresh, score_fresh, -jnp.inf),
        ],
        axis=-1,
    )
    largest = jnp.max(scores, axis=-1, keepdims=True)
    powered = jnp.exp(scores - largest)
    weights = (powered / jnp.sum(powered, axis=-1, keepdims=True)).astype(jnp.bfloat16)
    values_cached = value_cache.reshape(windows_here, cache_size, kv_here, HD)
    values_fresh = new_values.reshape(windows_here, tokens_here, kv_here, HD)
    mixed_rows = jnp.einsum(
        "wkgtp,wpkd->wtkgd",
        weights[..., :cache_size],
        values_cached,
        preferred_element_type=jnp.float32,
    )
    mixed_rows = mixed_rows + jnp.einsum(
        "wkgtp,wpkd->wtkgd",
        weights[..., cache_size:],
        values_fresh,
        preferred_element_type=jnp.float32,
    )
    attended = mixed_rows.astype(jnp.bfloat16).reshape(windows_here * tokens_here, query_width)
    partial_out = jnp.dot(
        lax.all_gather(attended, "dp", axis=0, tiled=True),
        out_weight,
        preferred_element_type=jnp.float32,
    )
    summed = lax.psum_scatter(partial_out, "tensor", scatter_dimension=0, tiled=True)
    block_windows, block_tokens, block_cols = residual.shape
    flat_residual = residual.reshape(block_windows * block_tokens, block_cols).astype(jnp.float32)
    verified = (
        (flat_residual + summed)
        .astype(jnp.bfloat16)
        .reshape(block_windows, block_tokens, block_cols)
    )
    chosen = jnp.arange(block_tokens)[None, :] == (accepted - 1)[:, None]
    picked = jnp.sum(
        jnp.where(chosen[:, :, None], verified, jnp.zeros((), jnp.bfloat16)),
        axis=1,
        dtype=jnp.bfloat16,
    )
    results = []
    current = widen(picked)
    row_block = current.shape[0] // lax.axis_size("tensor")
    row_start = lax.axis_index("tensor") * row_block
    for draft_step in range(STEPS):
        everyone = lax.psum(
            jnp.dot(current, draft_weight, preferred_element_type=jnp.float32), "tensor"
        )
        share = lax.dynamic_slice_in_dim(everyone, row_start, row_block, 0)
        drafted_now = jnp.tanh(2.0 * share).astype(jnp.bfloat16)
        results.append(drafted_now)
        if draft_step + 1 < STEPS:
            current = widen(drafted_now)
    return (verified, jnp.stack(results))


def solution(mesh):
    placed = (
        P("dp", None, "tensor"),
        P("dp", None, "tensor"),
        P("dp", None, "tensor"),
        P("dp", None, "tensor"),
        P("dp", None, "tensor"),
        P("dp"),
        P("tensor"),
        P("tensor", None, "dp"),
        P("tensor", "dp"),
        P("tensor", "dp"),
    )
    return jax.shard_map(
        per_device,
        mesh=mesh,
        in_specs=placed,
        out_specs=(P("tensor", None, "dp"), P(None, "tensor", "dp")),
        check_vma=False,
    )
```

profile of v0, /device:TPU:1, one launch (start us, length us, event | category | flops | bytes accessed | tf_op | source)
XLA Modules:
  0.0 743.5 jit_solution(10365520250779408295)
XLA Ops:
  8.1 1.4 fusion.17
  9.5 1.2 fusion.18
  13.0 79.9 %all-gather.2.cloned.1.call-done = bf16[1536,1024]{1,0:T(8,128)(2,1)} async-done(((bf16[48,1024]{1,0:T(8,128)(2,1)}), bf16[1536,1024]{1,0:T(8,128)(2,1)}) %all-gather.2.cloned.1.call-update) | async-done | bytes 3145744 | tf_op jit(solution)/shard_map/all_gather | solution.py:68
  92.9 4.0 fusion.19
  97.2 33.2 %reduce-scatter.2.cloned.1.call-done = f32[192,256]{1,0:T(8,128)} async-done(((f32[1536,256]{1,0:T(8,128)}), f32[192,256]{1,0:T(8,128)}) %reduce-scatter.2.cloned.1.call-update) | async-done | bytes 196624 | tf_op jit(solution)/shard_map/reduce_scatter | solution.py:72
  131.5 35.5 %all_gather.19 = bf16[32,8192]{1,0:T(8,128)(2,1)S(1)} all-gather(bf16[32,256]{1,0:T(8,128)(2,1)S(1)} %select_reduce_fusion), channel_id=1, replica_groups=mesh['dp'=32,'tensor'=8] {'dp'}, dimensions={1}, use_global_device_ids=true | all-gather | bytes 540672 | tf_op jit(solution)/shard_map/all_gather | solution.py:11
  167.0 24.3 %all_to_all.95 = bf16[32,8,1024]{2,0,1:T(8,128)(2,1)S(1)} all-to-all(bf16[32,8,1024]{2,0,1:T(8,128)(2,1)S(1)} %bitcast.106), channel_id=1, replica_groups=mesh['dp'=32,'tensor'=8] {'tensor'}, dimensions={1} | all-to-all | bytes 1048576 | tf_op jit(solution)/shard_map/all_to_all | solution.py:12
  191.4 1.0 fusion.20
  192.4 59.5 %all-reduce.6.cloned.1.call-done = f32[256,256]{1,0:T(8,128)} async-done(((f32[256,256]{1,0:T(8,128)}), f32[256,256]{1,0:T(8,128)}) %all-reduce.6.cloned.1.call-update) | async-done | bytes 262160 | tf_op jit(solution)/shard_map/psum | solution.py:91
  252.7 35.6 %all_gather.20 = bf16[32,8192]{1,0:T(8,128)(2,1)S(1)} all-gather(bf16[32,256]{1,0:T(8,128)(2,1)S(1)} %get-tuple-element.17), channel_id=1, replica_groups=mesh['dp'=32,'tensor'=8] {'dp'}, dimensions={1}, use_global_device_ids=true | all-gather | bytes 540672 | tf_op jit(solution)/shard_map/all_gather | solution.py:11
  288.3 23.8 %all_to_all.96 = bf16[32,8,1024]{2,0,1:T(8,128)(2,1)S(1)} all-to-all(bf16[32,8,1024]{2,0,1:T(8,128)(2,1)S(1)} %bitcast.109), channel_id=1, replica_groups=mesh['dp'=32,'tensor'=8] {'tensor'}, dimensions={1} | all-to-all | bytes 1048576 | tf_op jit(solution)/shard_map/all_to_all | solution.py:12
  312.1 1.0 fusion.21
  313.2 59.6 %all-reduce.8.cloned.1.call-done = f32[256,256]{1,0:T(8,128)} async-done(((f32[256,256]{1,0:T(8,128)}), f32[256,256]{1,0:T(8,128)}) %all-reduce.8.cloned.1.call-update) | async-done | bytes 262160 | tf_op jit(solution)/shard_map/psum | solution.py:91
  373.6 35.6 %all_gather.21 = bf16[32,8192]{1,0:T(8,128)(2,1)S(1)} all-gather(bf16[32,256]{1,0:T(8,128)(2,1)S(1)} %get-tuple-element.15), channel_id=1, replica_groups=mesh['dp'=32,'tensor'=8] {'dp'}, dimensions={1}, use_global_device_ids=true | all-gather | bytes 540672 | tf_op jit(solution)/shard_map/all_gather | solution.py:11
  409.1 23.8 %all_to_all.97 = bf16[32,8,1024]{2,0,1:T(8,128)(2,1)S(1)} all-to-all(bf16[32,8,1024]{2,0,1:T(8,128)(2,1)S(1)} %bitcast.112), channel_id=1, replica_groups=mesh['dp'=32,'tensor'=8] {'tensor'}, dimensions={1} | all-to-all | bytes 1048576 | tf_op jit(solution)/shard_map/all_to_all | solution.py:12
  432.9 1.0 fusion.22
  434.0 59.6 %all-reduce.10.cloned.1.call-done = f32[256,256]{1,0:T(8,128)} async-done(((f32[256,256]{1,0:T(8,128)}), f32[256,256]{1,0:T(8,128)}) %all-reduce.10.cloned.1.call-update) | async-done | bytes 262160 | tf_op jit(solution)/shard_map/psum | solution.py:91
  494.4 35.6 %all_gather.22 = bf16[32,8192]{1,0:T(8,128)(2,1)S(1)} all-gather(bf16[32,256]{1,0:T(8,128)(2,1)S(1)} %get-tuple-element.13), channel_id=1, replica_groups=mesh['dp'=32,'tensor'=8] {'dp'}, dimensions={1}, use_global_device_ids=true | all-gather | bytes 540672 | tf_op jit(solution)/shard_map/all_gather | solution.py:11
  530.0 23.8 %all_to_all.98 = bf16[32,8,1024]{2,0,1:T(8,128)(2,1)S(1)} all-to-all(bf16[32,8,1024]{2,0,1:T(8,128)(2,1)S(1)} %bitcast.115), channel_id=1, replica_groups=mesh['dp'=32,'tensor'=8] {'tensor'}, dimensions={1} | all-to-all | bytes 1048576 | tf_op jit(solution)/shard_map/all_to_all | solution.py:12
  553.7 1.0 fusion.23
  554.8 59.6 %all-reduce.12.cloned.1.call-done = f32[256,256]{1,0:T(8,128)} async-done(((f32[256,256]{1,0:T(8,128)}), f32[256,256]{1,0:T(8,128)}) %all-reduce.12.cloned.1.call-update) | async-done | bytes 262160 | tf_op jit(solution)/shard_map/psum | solution.py:91
  615.2 35.6 %all_gather.23 = bf16[32,8192]{1,0:T(8,128)(2,1)S(1)} all-gather(bf16[32,256]{1,0:T(8,128)(2,1)S(1)} %get-tuple-element.11), channel_id=1, replica_groups=mesh['dp'=32,'tensor'=8] {'dp'}, dimensions={1}, use_global_device_ids=true | all-gather | bytes 540672 | tf_op jit(solution)/shard_map/all_gather | solution.py:11
  650.8 23.8 %all_to_all.99 = bf16[32,8,1024]{2,0,1:T(8,128)(2,1)S(1)} all-to-all(bf16[32,8,1024]{2,0,1:T(8,128)(2,1)S(1)} %bitcast.118), channel_id=1, replica_groups=mesh['dp'=32,'tensor'=8] {'tensor'}, dimensions={1} | all-to-all | bytes 1048576 | tf_op jit(solution)/shard_map/all_to_all | solution.py:12
  676.2 59.0 %all-reduce.14.cloned.1.call-done = f32[256,256]{1,0:T(8,128)} async-done(((f32[256,256]{1,0:T(8,128)}), f32[256,256]{1,0:T(8,128)}) %all-reduce.14.cloned.1.call-update) | async-done | bytes 262160 | tf_op jit(solution)/shard_map/psum | solution.py:91
  (53 shorter events, 11.1 us)
Async XLA Ops:
  7.2 85.7 %copy-start = (bf16[1024,256]{1,0:T(8,128)(2,1)S(1)}, bf16[1024,256]{1,0:T(8,128)(2,1)}, u32[]{:S(2)}) copy-start(bf16[1024,256]{1,0:T(8,128)(2,1)} %param.18) | copy-start | bytes 1572868
  7.2 4.8 copy-start.2
  7.2 85.7 %all-gather.2.cloned.1.call-start = ((), (), s32[]{:S(2)}) async-start(), calls=%async_computation.6 | async-start | bytes 3244032 | tf_op jit(solution)/shard_map/all_gather | solution.py:68
  12.9 84.0 %copy-start.3 = (bf16[32,6,256]{2,0,1:T(8,128)(2,1)S(1)}, bf16[32,6,256]{2,0,1:T(8,128)(2,1)}, u32[]{:S(2)}) copy-start(bf16[32,6,256]{2,0,1:T(8,128)(2,1)} %param.17) | copy-start | bytes 294916
  12.9 84.1 %copy-start.5 = (s32[32]{0:T(128)S(1)}, s32[32]{0:T(128)}, u32[]{:S(2)}) copy-start(s32[32]{0:T(128)} %param.16) | copy-start | bytes 388
  12.9 117.4 %reduce-scatter.2.cloned.1.call-start = ((), (), s32[]{:S(2)}) async-start(), calls=%async_computation.7 | async-start | bytes 1769472 | tf_op jit(solution)/shard_map/reduce_scatter | solution.py:72
  96.9 94.5 %copy-start.1 = (bf16[1024,256]{1,0:T(8,128)(2,1)S(1)}, bf16[1024,256]{1,0:T(8,128)(2,1)}, u32[]{:S(2)}) copy-start(bf16[1024,256]{1,0:T(8,128)(2,1)} %param.19) | copy-start | bytes 1572868
  96.9 155.1 %all-reduce.6.cloned.1.call-start = ((), (), s32[]{:S(2)}) async-start(), calls=%async_computation.8 | async-start | bytes 524288 | tf_op jit(solution)/shard_map/psum | solution.py:91
  192.4 180.4 %all-reduce.8.cloned.1.call-start = ((), (), s32[]{:S(2)}) async-start(), calls=%async_computation.9 | async-start | bytes 524288 | tf_op jit(solution)/shard_map/psum | solution.py:91
  313.1 180.5 %all-reduce.10.cloned.1.call-start = ((), (), s32[]{:S(2)}) async-start(), calls=%async_computation.10 | async-start | bytes 524288 | tf_op jit(solution)/shard_map/psum | solution.py:91
  433.9 180.5 %all-reduce.12.cloned.1.call-start = ((), (), s32[]{:S(2)}) async-start(), calls=%async_computation.11 | async-start | bytes 524288 | tf_op jit(solution)/shard_map/psum | solution.py:91
  554.7 180.5 %all-reduce.14.cloned.1.call-start = ((), (), s32[]{:S(2)}) async-start(), calls=%async_computation.12 | async-start | bytes 524288 | tf_op jit(solution)/shard_map/psum | solution.py:91
  736.0 0.6 copy-start.4
Sparse Core Ops, SparseCore 0:
  13.0 79.7 all-gather.1
  97.0 33.3 reduce-scatter.1
  192.5 59.4 all-reduce.5
  313.2 59.4 all-reduce.7
  434.0 59.5 all-reduce.9
  554.9 59.4 all-reduce.11
  675.7 59.5 all-reduce.13
where the time goes:
time: 745 us; the launch traced here: 743 us
  waiting for transfers between devices  411 us (55%)
  blocking collectives  297 us (40%)
  between operations  14.3 us (2%)
  matrix products  12.6 us (2%)
    psum x5, waiting for transfers between devices, per_device(): lax.psum(jnp.dot(current, draft_weight, preferred_element_type=jnp.float3...  297 us
    all_gather x5, blocking collectives, widen(): wide_rows = lax.all_gather(drafted_rows, 'dp', axis=1, tiled=True)  178 us
    all_to_all x5, blocking collectives, widen(): lax.all_to_all(wide_rows, 'tensor', split_axis=1, concat_axis=0, tiled=True)  119 us
    all_gather x1, waiting for transfers between devices, per_device(): lax.all_gather(attended, 'dp', axis=0, tiled=True)  79.9 us
    reduce_scatter x1, waiting for transfers between devices, per_device(): lax.psum_scatter(partial_out, 'tensor', scatter_dimension=0, tiled=True)  33.2 us
  transfers between devices with their start and end apart: 7, of which 7 were waited for; matrix products, arithmetic and copies ran while one was open for 0% of the time, Pallas kernels for 0%

commit v1 on v0

--- a/solution.py
+++ b/solution.py
@@ -7,9 +7,29 @@
 STEPS = 5
 
 
-def widen(drafted_rows):
-    wide_rows = lax.all_gather(drafted_rows, "dp", axis=1, tiled=True)
-    return lax.all_to_all(wide_rows, "tensor", split_axis=1, concat_axis=0, tiled=True)
+def spread(block, axis):
+    copies = jnp.broadcast_to(block[None], (lax.axis_size(axis),) + block.shape)
+    return lax.all_to_all(copies, axis, split_axis=0, concat_axis=0, tiled=True)
+
+
+def accepted_of_my_windows(accepted):
+    dp_size, tensor_size = lax.axis_size("dp"), lax.axis_size("tensor")
+    ratio = dp_size // tensor_size
+    pairs = []
+    for j in range(dp_size):
+        for i in range(tensor_size):
+            source = (ratio * i + j % ratio) * tensor_size + j // ratio
+            pairs.append((source, j * tensor_size + i))
+    block = lax.ppermute(accepted, ("dp", "tensor"), pairs)
+    rows = accepted.shape[0] // ratio
+    return lax.dynamic_slice_in_dim(block, lax.axis_index("dp") % ratio * rows, rows, 0)
+
+
+def pick(rows, accepted):
+    chosen = jnp.arange(rows.shape[1])[None, :] == (accepted - 1)[:, None]
+    return jnp.sum(
+        jnp.where(chosen[:, :, None], rows, jnp.zeros((), rows.dtype)), axis=1, dtype=rows.dtype
+    )
 
 
 def per_device(
@@ -28,6 +48,10 @@
     cache_size = key_cache.shape[1]
     kv_here = new_keys.shape[2] // HD
     group_size = query_width // HD // kv_here
+    tensor_size = lax.axis_size("tensor")
+    own_accepted = accepted_of_my_windows(accepted)
+    draft_columns = lax.all_gather(draft_weight, "tensor", axis=0, tiled=True)
+
     query_split = queries.reshape(windows_here, tokens_here, kv_here, group_size, HD)
     keys_cached = key_cache.reshape(windows_here, cache_size, kv_here, HD)
     keys_fresh = new_keys.reshape(windows_here, tokens_here, kv_here, HD)
@@ -63,39 +87,44 @@
         values_fresh,
         preferred_element_type=jnp.float32,
     )
-    attended = mixed_rows.astype(jnp.bfloat16).reshape(windows_here * tokens_here, query_width)
+    attended = mixed_rows.astype(jnp.bfloat16).reshape(windows_here, tokens_here, query_width)
+
+    picked_rows = spread(pick(attended, own_accepted), "dp").reshape(-1, query_width)
+    picked_part = jnp.dot(picked_rows, out_weight, preferred_element_type=jnp.float32)
+    block_windows, block_tokens, block_cols = residual.shape
+    shares = lax.all_to_all(
+        picked_part.astype(jnp.bfloat16).reshape(tensor_size, block_windows, block_cols),
+        "tensor",
+        split_axis=0,
+        concat_axis=0,
+        tiled=True,
+    )
+    current = (
+        pick(residual, accepted).astype(jnp.float32) + jnp.sum(shares.astype(jnp.float32), axis=0)
+    ).astype(jnp.bfloat16)
+
     partial_out = jnp.dot(
-        lax.all_gather(attended, "dp", axis=0, tiled=True),
+        lax.all_gather(
+            attended.reshape(windows_here * tokens_here, query_width), "dp", axis=0, tiled=True
+        ),
         out_weight,
         preferred_element_type=jnp.float32,
     )
     summed = lax.psum_scatter(partial_out, "tensor", scatter_dimension=0, tiled=True)
-    block_windows, block_tokens, block_cols = residual.shape
     flat_residual = residual.reshape(block_windows * block_tokens, block_cols).astype(jnp.float32)
     verified = (
         (flat_residual + summed)
         .astype(jnp.bfloat16)
         .reshape(block_windows, block_tokens, block_cols)
     )
-    chosen = jnp.arange(block_tokens)[None, :] == (accepted - 1)[:, None]
-    picked = jnp.sum(
-        jnp.where(chosen[:, :, None], verified, jnp.zeros((), jnp.bfloat16)),
-        axis=1,
-        dtype=jnp.bfloat16,
-    )
+
+    columns = draft_columns.reshape(-1, block_cols, draft_columns.shape[1])
     results = []
-    current = widen(picked)
-    row_block = current.shape[0] // lax.axis_size("tensor")
-    row_start = lax.axis_index("tensor") * row_block
     for draft_step in range(STEPS):
-        everyone = lax.psum(
-            jnp.dot(current, draft_weight, preferred_element_type=jnp.float32), "tensor"
-        )
-        share = lax.dynamic_slice_in_dim(everyone, row_start, row_block, 0)
-        drafted_now = jnp.tanh(2.0 * share).astype(jnp.bfloat16)
-        results.append(drafted_now)
-        if draft_step + 1 < STEPS:
-            current = widen(drafted_now)
+        inputs = spread(current, "dp")
+        product = jnp.einsum("jwk,jkn->wn", inputs, columns, preferred_element_type=jnp.float32)
+        current = jnp.tanh(2.0 * product).astype(jnp.bfloat16)
+        results.append(current)
     return (verified, jnp.stack(results))
 
 

time: 745 us -> 204 us (0.27)
  the two profiles are of different devices: /device:TPU:1 before, /device:TPU:32 now
where the time goes in v1:
time: 204 us; the launch traced here: 203 us
  blocking collectives  71.2 us (35%)
  waiting for transfers between devices  55.3 us (27%)
  starting transfers between devices  34.3 us (17%)
  matrix products  20.8 us (10%)
  between operations  14 us (7%)
  local copies, waits for them, and re-layouts  4.89 us (2%)
  other arithmetic  2.43 us (1%)
    all_to_all x3, blocking collectives, spread(): return lax.all_to_all(copies, axis, split_axis=0, concat_axis=0, tiled=True)  71.2 us
    all_to_all x3, waiting for transfers between devices, spread(): return lax.all_to_all(copies, axis, split_axis=0, concat_axis=0, tiled=True)  29.5 us
    all_to_all x3, starting transfers between devices, spread(): return lax.all_to_all(copies, axis, split_axis=0, concat_axis=0, tiled=True)  29.5 us
    all_gather x1, waiting for transfers between devices, per_device(): lax.all_gather(attended.reshape(windows_here * tokens_here, query_width),...  18.9 us
    dot_general x5, matrix products, per_device(): jnp.einsum('jwk,jkn->wn', inputs, columns, preferred_element_type=jnp.flo...  11 us
    all_to_all x1, waiting for transfers between devices, per_device(): lax.all_to_all(picked_part.astype(jnp.bfloat16).reshape(tensor_size, bloc...  5.94 us
    dot_general x1, matrix products, per_device(): jnp.dot(lax.all_gather(attended.reshape(windows_here * tokens_here, query...  4.12 us
  transfers between devices with their start and end apart: 8, of which 5 were waited for; matrix products, arithmetic and copies ran while one was open for 12% of the time, Pallas kernels for 0%

profile of v1, /device:TPU:32, one launch (start us, length us, event | category | flops | bytes accessed | tf_op | source)
XLA Modules:
  0.0 202.9 jit_solution(7244637274583813440)
XLA Ops:
  8.0 1.3 collective-permute-start
  10.0 1.2 fusion.35
  11.2 1.4 fusion.34
  14.1 1.3 fusion.29
  16.1 0.9 broadcast_in_dim.104
  16.9 19.1 %all-to-all-start = ((bf16[32,8,1024]{2,1,0:T(8,128)(2,1)}), bf16[32,8,1024]{2,1,0:T(8,128)(2,1)S(1)}, u32[]{:S(2)}, u32[]{:S(2)}) async-start(bf16[32,8,1024]{2,1,0:T(8,128)(2,1)} %broadcast_in_dim.104), calls=%async_computation.1 | async-start | bytes 1048576 | tf_op jit(solution)/shard_map/all_to_all | solution.py:12
  36.1 15.0 %all-to-all-done = bf16[32,8,1024]{2,1,0:T(8,128)(2,1)S(1)} async-done(((bf16[32,8,1024]{2,1,0:T(8,128)(2,1)}), bf16[32,8,1024]{2,1,0:T(8,128)(2,1)S(1)}, u32[]{:S(2)}, u32[]{:S(2)}) %all-to-all-start) | async-done | bytes 524320 | tf_op jit(solution)/shard_map/all_to_all | solution.py:12
  51.1 1.0 convolution_convert_fusion
  52.0 3.4 %all-to-all-start.1 = ((bf16[8,32,256]{2,1,0:T(8,128)(2,1)}), bf16[8,32,256]{2,1,0:T(8,128)(2,1)S(1)}, u32[]{:S(2)}, u32[]{:S(2)}) async-start(bf16[8,32,256]{2,1,0:T(8,128)(2,1)} %bitcast.19), calls=%async_computation.2 | async-start | bytes 262144 | tf_op jit(solution)/shard_map/all_to_all | solution.py:95
  55.5 5.9 %all-to-all-done.1 = bf16[8,32,256]{2,1,0:T(8,128)(2,1)S(1)} async-done(((bf16[8,32,256]{2,1,0:T(8,128)(2,1)}), bf16[8,32,256]{2,1,0:T(8,128)(2,1)S(1)}, u32[]{:S(2)}, u32[]{:S(2)}) %all-to-all-start.1) | async-done | bytes 131104 | tf_op jit(solution)/shard_map/all_to_all | solution.py:95
  61.6 23.8 %all_to_all.35 = bf16[32,32,256]{2,1,0:T(8,128)(2,1)S(1)} all-to-all(bf16[32,32,256]{2,1,0:T(8,128)(2,1)S(1)} %broadcast_in_dim.105), channel_id=1, replica_groups=mesh['dp'=32,'tensor'=8] {'dp'}, dimensions={0} | all-to-all | bytes 1048576 | tf_op jit(solution)/shard_map/all_to_all | solution.py:12
  85.4 3.2 %bitcast_dynamic-update-slice_fusion.3 = (bf16[5,32,256]{2,1,0:T(8,128)(2,1)S(1)}, bf16[32,256]{1,0:T(8,128)(2,1)S(1)}) fusion(bf16[32,32,256]{2,1,0:T(8,128)(2,1)S(1)} %all_to_all.35, bf16[32,256,256]{2,1,0:T(8,128)(2,1)} %bitcast.131), kind=kOutput, calls=%fused_computation.55 | convolution fusion | flops 134234112 | bytes 4751360 | tf_op jit(solution)/shard_map/jwk,jkn->wn/dot_general | solution.py:125
  88.6 23.2 %all_to_all.36 = bf16[32,32,256]{2,1,0:T(8,128)(2,1)S(1)} all-to-all(bf16[32,32,256]{2,1,0:T(8,128)(2,1)S(1)} %broadcast_in_dim.106), channel_id=1, replica_groups=mesh['dp'=32,'tensor'=8] {'dp'}, dimensions={0} | all-to-all | bytes 1048576 | tf_op jit(solution)/shard_map/all_to_all | solution.py:12
  112.7 0.9 broadcast_in_dim.107
  113.6 5.5 %all-to-all-start.4 = ((bf16[32,32,256]{2,1,0:T(8,128)(2,1)}), bf16[32,32,256]{2,1,0:T(8,128)(2,1)S(1)}, u32[]{:S(2)}, u32[]{:S(2)}) async-start(bf16[32,32,256]{2,1,0:T(8,128)(2,1)} %broadcast_in_dim.107), calls=%async_computation.5 | async-start | bytes 1048576 | tf_op jit(solution)/shard_map/all_to_all | solution.py:12
  119.2 18.9 %all-gather.3.cloned.1.call-done = bf16[1536,1024]{1,0:T(8,128)(2,1)} async-done(((bf16[48,1024]{1,0:T(8,128)(2,1)}), bf16[1536,1024]{1,0:T(8,128)(2,1)}) %all-gather.3.cloned.1.call-update) | async-done | bytes 3145744 | tf_op jit(solution)/shard_map/all_gather | solution.py:107
  138.1 4.1 %fusion.36 = f32[1536,256]{1,0:T(8,128)} fusion(bf16[1536,1024]{1,0:T(8,128)(2,1)} %all-gather.3.cloned.1.call-done, bf16[1024,256]{1,0:T(8,128)(2,1)S(1)} %copy-done), kind=kOutput, calls=%fused_computation.66 | convolution fusion | flops 805306368 | bytes 5242880 | tf_op jit(solution)/shard_map/dot_general | solution.py:106
  142.2 3.2 %bitcast_dynamic-update-slice_fusion.1 = (bf16[5,32,256]{2,1,0:T(8,128)(2,1)S(1)}, bf16[32,256]{1,0:T(8,128)(2,1)S(1)}) fusion(bf16[5,32,256]{2,1,0:T(8,128)(2,1)S(1)} %get-tuple-element.14, bf16[32,32,256]{2,1,0:T(8,128)(2,1)S(1)} %all-to-all-done.4, bf16[32,256,256]{2,1,0:T(8,128)(2,1)} %bitcast.132), kind=kOutput, calls=%fused_computation.53 | convolution fusion | flops 134234112 | bytes 4751360 | tf_op jit(solution)/shard_map/jwk,jkn->wn/dot_general | solution.py:125
  145.5 24.1 %all_to_all.37 = bf16[32,32,256]{2,1,0:T(8,128)(2,1)S(1)} all-to-all(bf16[32,32,256]{2,1,0:T(8,128)(2,1)S(1)} %broadcast_in_dim.108), channel_id=1, replica_groups=mesh['dp'=32,'tensor'=8] {'dp'}, dimensions={0} | all-to-all | bytes 1048576 | tf_op jit(solution)/shard_map/all_to_all | solution.py:12
  170.4 0.9 broadcast_in_dim.109
  171.3 4.8 %all-to-all-start.6 = ((bf16[32,32,256]{2,1,0:T(8,128)(2,1)}), bf16[32,32,256]{2,1,0:T(8,128)(2,1)S(1)}, u32[]{:S(2)}, u32[]{:S(2)}) async-start(bf16[32,32,256]{2,1,0:T(8,128)(2,1)} %broadcast_in_dim.109), calls=%async_computation.7 | async-start | bytes 1048576 | tf_op jit(solution)/shard_map/all_to_all | solution.py:12
  176.5 0.9 add_convert_fusion
  178.1 14.5 %all-to-all-done.6 = bf16[32,32,256]{2,1,0:T(8,128)(2,1)S(1)} async-done(((bf16[32,32,256]{2,1,0:T(8,128)(2,1)}), bf16[32,32,256]{2,1,0:T(8,128)(2,1)S(1)}, u32[]{:S(2)}, u32[]{:S(2)}) %all-to-all-start.6) | async-done | bytes 524320 | tf_op jit(solution)/shard_map/all_to_all | solution.py:12
  192.7 3.0 %fusion.22 = bf16[5,32,256]{2,1,0:T(8,128)(2,1)S(1)} fusion(bf16[5,32,256]{2,1,0:T(8,128)(2,1)S(1)} %get-tuple-element.18, bf16[32,32,256]{2,1,0:T(8,128)(2,1)S(1)} %all-to-all-done.6, bf16[32,256,256]{2,1,0:T(8,128)(2,1)} %bitcast.133), kind=kOutput, calls=%fused_computation.31 | convolution fusion | flops 134234112 | bytes 4734976 | tf_op jit(solution)/shard_map/jwk,jkn->wn/dot_general | solution.py:125
  (46 shorter events, 7.3 us)
Async XLA Ops:
  7.2 43.9 %copy-start = (bf16[1024,256]{1,0:T(8,128)(2,1)S(1)}, bf16[1024,256]{1,0:T(8,128)(2,1)}, u32[]{:S(2)}) copy-start(bf16[1024,256]{1,0:T(8,128)(2,1)} %param.18) | copy-start | bytes 1572868
  7.2 28.9 %copy-start.5 = (s32[32]{0:T(128)S(1)}, s32[32]{0:T(128)}, u32[]{:S(2)}) copy-start(s32[32]{0:T(128)} %param.16) | copy-start | bytes 388
  7.2 48.2 %copy-start.3 = (bf16[32,6,256]{2,0,1:T(8,128)(2,1)S(1)}, bf16[32,6,256]{2,0,1:T(8,128)(2,1)}, u32[]{:S(2)}) copy-start(bf16[32,6,256]{2,0,1:T(8,128)(2,1)} %param.17) | copy-start | bytes 294916
  7.2 78.2 %all-gather.5.cloned.1.call-start = ((), (), s32[]{:S(2)}) async-start(), calls=%async_computation.10 | async-start | bytes 4718592 | tf_op jit(solution)/shard_map/all_gather | solution.py:53
  7.9 130.1 %all-gather.3.cloned.1.call-start = ((), (), s32[]{:S(2)}) async-start(), calls=%async_computation.8 | async-start | bytes 3244032 | tf_op jit(solution)/shard_map/all_gather | solution.py:107
  8.0 6.0 %collective-permute-start = (s32[32]{0:T(128)}, s32[32]{0:T(128)S(1)}, u32[]{:S(2)}, u32[]{:S(2)}) collective-permute-start(s32[32]{0:T(128)} %param.16), channel_id=1, source_target_pairs={{0,0},{32,1},{64,2},{96,3},{128,4},{160,5},{192,6},{224,7},{8,8},{... | collective-permute-start | bytes 392 | tf_op jit(solution)/shard_map/ppermute | solution.py:23
  16.9 34.2 %all-to-all-start = ((bf16[32,8,1024]{2,1,0:T(8,128)(2,1)}), bf16[32,8,1024]{2,1,0:T(8,128)(2,1)S(1)}, u32[]{:S(2)}, u32[]{:S(2)}) async-start(bf16[32,8,1024]{2,1,0:T(8,128)(2,1)} %broadcast_in_dim.104), calls=%async_computation.1 | async-start | bytes 1048576 | tf_op jit(solution)/shard_map/all_to_all | solution.py:12
  52.0 9.4 %all-to-all-start.1 = ((bf16[8,32,256]{2,1,0:T(8,128)(2,1)}), bf16[8,32,256]{2,1,0:T(8,128)(2,1)S(1)}, u32[]{:S(2)}, u32[]{:S(2)}) async-start(bf16[8,32,256]{2,1,0:T(8,128)(2,1)} %bitcast.19), calls=%async_computation.2 | async-start | bytes 262144 | tf_op jit(solution)/shard_map/all_to_all | solution.py:95
  85.4 26.5 %copy-start.1 = (bf16[8192,256]{1,0:T(8,128)(2,1)S(1)}, bf16[8192,256]{1,0:T(8,128)(2,1)}, u32[]{:S(2)}) copy-start(bf16[8192,256]{1,0:T(8,128)(2,1)} %all-gather.5.cloned.1.call-done) | copy-start | bytes 12582916
  113.6 28.6 %all-to-all-start.4 = ((bf16[32,32,256]{2,1,0:T(8,128)(2,1)}), bf16[32,32,256]{2,1,0:T(8,128)(2,1)S(1)}, u32[]{:S(2)}, u32[]{:S(2)}) async-start(bf16[32,32,256]{2,1,0:T(8,128)(2,1)} %broadcast_in_dim.107), calls=%async_computation.5 | async-start | bytes 1048576 | tf_op jit(solution)/shard_map/all_to_all | solution.py:12
  119.1 57.4 %reduce-scatter.2.cloned.1.call-start = ((), (), s32[]{:S(2)}) async-start(), calls=%async_computation.9 | async-start | bytes 1769472 | tf_op jit(solution)/shard_map/reduce_scatter | solution.py:113
  142.2 27.4 %copy-start.2 = (bf16[8192,256]{1,0:T(8,128)(2,1)S(1)}, bf16[8192,256]{1,0:T(8,128)(2,1)}, u32[]{:S(2)}) copy-start(bf16[8192,256]{1,0:T(8,128)(2,1)} %all-gather.5.cloned.1.call-done) | copy-start | bytes 12582916
  171.3 21.4 %all-to-all-start.6 = ((bf16[32,32,256]{2,1,0:T(8,128)(2,1)}), bf16[32,32,256]{2,1,0:T(8,128)(2,1)S(1)}, u32[]{:S(2)}, u32[]{:S(2)}) async-start(bf16[32,32,256]{2,1,0:T(8,128)(2,1)} %broadcast_in_dim.109), calls=%async_computation.7 | async-start | bytes 1048576 | tf_op jit(solution)/shard_map/all_to_all | solution.py:12
  195.7 0.6 copy-start.4
Sparse Core Ops, SparseCore 0:
  9.9 37.2 all-gather.4
  50.4 87.6 all-gather.2
  142.3 34.1 reduce-scatter.1

commit v2 on v1

--- a/solution.py
+++ b/solution.py
@@ -1,10 +1,13 @@
 import jax
 import jax.numpy as jnp
 from jax import lax
+from jax.experimental import pallas as pl
+from jax.experimental.pallas import tpu as pltpu
 from jax.sharding import PartitionSpec as P
 
 HD = 128
 STEPS = 5
+HOLD = 2
 
 
 def spread(block, axis):
@@ -12,17 +15,86 @@
     return lax.all_to_all(copies, axis, split_axis=0, concat_axis=0, tiled=True)
 
 
+Y, ZH, ZL, X, C = 4, 2, 4, 4, 2
+BLOCKS = [[(y * ZH + zh) * ZL + zl for y in range(Y) for zl in range(ZL)] for zh in range(ZH)]
+
+
+def route(source):
+    pairs = []
+    for y in range(Y):
+        for zh in range(ZH):
+            for zl in range(ZL):
+                for x in range(X):
+                    for c in range(C):
+                        ends = []
+                        for sy, szh, szl, sx, sc in (source(y, zh, zl, x, c), (y, zh, zl, x, c)):
+                            ends.append((((sy * ZH + szh) * ZL + szl) * X + sx) * C + sc)
+                        pairs.append(tuple(ends))
+    return pairs
+
+
+SWAPPED = route(lambda y, zh, zl, x, c: (y, c, zl, x, zh))
+SWAPPED_OTHER = route(lambda y, zh, zl, x, c: (y, c, zl, x, 1 - zh))
+OTHER_CORE = route(lambda y, zh, zl, x, c: (y, zh, zl, x, 1 - c))
+X_BEHIND = [route(lambda y, zh, zl, x, c, s=s: (y, zh, zl, (x - s) % X, c)) for s in range(X)]
+
+
+def move(block, pairs):
+    return lax.ppermute(block, ("dp", "tensor"), pairs)
+
+
+def draft_weights(shard):
+    here = move(shard, SWAPPED)
+    there = move(shard, SWAPPED_OTHER)
+    same = lax.axis_index("dp") // ZL % ZH == lax.axis_index("tensor") % C
+    both = jnp.stack([jnp.where(same, here, there), jnp.where(same, there, here)])
+    return [both] + [move(both, X_BEHIND[s]) for s in range(1, X)]
+
+
+def draft_kernel(own_ref, other_ref, *refs):
+    weight_refs, (drafted_ref, copies_ref) = refs[:X], refs[X:]
+    x = lax.axis_index("tensor") // C
+    total = jnp.zeros(drafted_ref.shape, jnp.float32)
+    depth = own_ref.shape[2]
+    for s in range(X):
+        y = lax.rem(x + X - s, X)
+        for half, rows_ref in enumerate((own_ref, other_ref)):
+            for zl in range(ZL):
+                total += jnp.dot(
+                    rows_ref[y * ZL + zl],
+                    weight_refs[s][half, zl * depth : (zl + 1) * depth, :],
+                    preferred_element_type=jnp.float32,
+                )
+    drafted = jnp.tanh(2.0 * total).astype(drafted_ref.dtype)
+    drafted_ref[...] = drafted
+    for copy in range(copies_ref.shape[0]):
+        copies_ref[copy] = drafted
+
+
+def draft_step(own, other, weights):
+    count, rows, cols = own.shape
+    return pl.pallas_call(
+        draft_kernel,
+        out_shape=(
+            jax.ShapeDtypeStruct((rows, cols), own.dtype),
+            jax.ShapeDtypeStruct((count, rows, cols), own.dtype),
+        ),
+        in_specs=[pl.BlockSpec(memory_space=pltpu.VMEM)] * (2 + X),
+        out_specs=(pl.BlockSpec(memory_space=pltpu.VMEM),) * 2,
+        compiler_params=pltpu.CompilerParams(vmem_limit_bytes=24 << 20),
+        cost_estimate=pl.CostEstimate(
+            flops=4 * count * rows * cols * cols,
+            bytes_accessed=4 * count * cols * cols + 6 * count * rows * cols,
+            transcendentals=rows * cols,
+        ),
+        name="draft_step",
+    )(own, other, *weights)
+
+
 def accepted_of_my_windows(accepted):
-    dp_size, tensor_size = lax.axis_size("dp"), lax.axis_size("tensor")
-    ratio = dp_size // tensor_size
-    pairs = []
-    for j in range(dp_size):
-        for i in range(tensor_size):
-            source = (ratio * i + j % ratio) * tensor_size + j // ratio
-            pairs.append((source, j * tensor_size + i))
-    block = lax.ppermute(accepted, ("dp", "tensor"), pairs)
-    rows = accepted.shape[0] // ratio
-    return lax.dynamic_slice_in_dim(block, lax.axis_index("dp") % ratio * rows, rows, 0)
+    everyone = spread(accepted, "tensor").reshape(-1)
+    rows = everyone.shape[0] // lax.axis_size("dp")
+    return lax.dynamic_slice_in_dim(everyone, lax.axis_index("dp") * rows, rows, 0)
 
 
 def pick(rows, accepted):
@@ -50,7 +122,7 @@
     group_size = query_width // HD // kv_here
     tensor_size = lax.axis_size("tensor")
     own_accepted = accepted_of_my_windows(accepted)
-    draft_columns = lax.all_gather(draft_weight, "tensor", axis=0, tiled=True)
+    weights_moved = draft_weights(draft_weight)
 
     query_split = queries.reshape(windows_here, tokens_here, kv_here, group_size, HD)
     keys_cached = key_cache.reshape(windows_here, cache_size, kv_here, HD)
@@ -103,28 +175,35 @@
         pick(residual, accepted).astype(jnp.float32) + jnp.sum(shares.astype(jnp.float32), axis=0)
     ).astype(jnp.bfloat16)
 
-    partial_out = jnp.dot(
-        lax.all_gather(
-            attended.reshape(windows_here * tokens_here, query_width), "dp", axis=0, tiled=True
+    gathered = lax.all_gather(
+        attended.reshape(windows_here * tokens_here, query_width), "dp", axis=0, tiled=True
+    )
+
+    current = move(current, SWAPPED)
+    copies = jnp.broadcast_to(current[None], (len(BLOCKS[0]),) + current.shape)
+    results = []
+    for step in range(STEPS):
+        own = lax.all_to_all(
+            copies, "dp", split_axis=0, concat_axis=0, tiled=True, axis_index_groups=BLOCKS
+        )
+        other = move(own, OTHER_CORE)
+        drafted, copies = draft_step(own, other, weights_moved)
+        results.append(move(drafted, SWAPPED))
+        if step == HOLD:
+            gathered, copies = lax.optimization_barrier((gathered, copies))
+
+    partial_out = jnp.dot(gathered, out_weight, preferred_element_type=jnp.float32)
+    parts = lax.all_to_all(
+        partial_out.astype(jnp.bfloat16).reshape(
+            tensor_size, block_windows * block_tokens, block_cols
         ),
-        out_weight,
-        preferred_element_type=jnp.float32,
-    )
-    summed = lax.psum_scatter(partial_out, "tensor", scatter_dimension=0, tiled=True)
-    flat_residual = residual.reshape(block_windows * block_tokens, block_cols).astype(jnp.float32)
-    verified = (
-        (flat_residual + summed)
-        .astype(jnp.bfloat16)
-        .reshape(block_windows, block_tokens, block_cols)
-    )
-
-    columns = draft_columns.reshape(-1, block_cols, draft_columns.shape[1])
-    results = []
-    for draft_step in range(STEPS):
-        inputs = spread(current, "dp")
-        product = jnp.einsum("jwk,jkn->wn", inputs, columns, preferred_element_type=jnp.float32)
-        current = jnp.tanh(2.0 * product).astype(jnp.bfloat16)
-        results.append(current)
+        "tensor",
+        split_axis=0,
+        concat_axis=0,
+        tiled=True,
+    )
+    summed = jnp.sum(parts.astype(jnp.float32), axis=0).reshape(residual.shape)
+    verified = (residual.astype(jnp.float32) + summed).astype(jnp.bfloat16)
     return (verified, jnp.stack(results))
 
 

time: 204 us -> 255 us (1.25)
  the two profiles are of different devices: /device:TPU:32 before, /device:TPU:1 now
where the time goes in v2:
time: 255 us; the launch traced here: 254 us
  starting transfers between devices  80.7 us (32%)
  waiting for transfers between devices  70.7 us (28%)
  blocking collectives  53.8 us (21%)
  between operations  14.4 us (6%)
  Pallas kernels  13.3 us (5%)
  matrix products  8.44 us (3%)
  local copies, waits for them, and re-layouts  8.14 us (3%)
  other arithmetic  4.33 us (2%)
    ppermute x16, waiting for transfers between devices, move(): return lax.ppermute(block, ('dp', 'tensor'), pairs)  69 us
    all_to_all x4, blocking collectives, per_device(): lax.all_to_all(copies, 'dp', split_axis=0, concat_axis=0, tiled=True, axi...  53.8 us
    ppermute x16, starting transfers between devices, move(): return lax.ppermute(block, ('dp', 'tensor'), pairs)  44.9 us
    all_to_all x2, starting transfers between devices, spread(): return lax.all_to_all(copies, axis, split_axis=0, concat_axis=0, tiled=True)  17 us
    pallas_call x5, Pallas kernels, draft_step(): pl.pallas_call(draft_kernel, out_shape=(jax.ShapeDtypeStruct((rows, cols)...  13.3 us
    all_to_all x1, starting transfers between devices, per_device(): lax.all_to_all(picked_part.astype(jnp.bfloat16).reshape(tensor_size, bloc...  9.32 us
    all_to_all x1, starting transfers between devices, per_device(): lax.all_to_all(partial_out.astype(jnp.bfloat16).reshape(tensor_size, bloc...  5.94 us
  transfers between devices with their start and end apart: 22, of which 10 were waited for; matrix products, arithmetic and copies ran while one was open for 7% of the time, Pallas kernels for 4%

profile of v2, /device:TPU:1, one launch (start us, length us, event | category | flops | bytes accessed | tf_op | source)
XLA Modules:
  0.0 253.8 jit_solution(17075191474779414462)
XLA Ops:
  8.5 6.5 %all-to-all-start = ((s32[8,1,32]{2,1,0:T(1,128)}), s32[8,1,32]{2,1,0:T(1,128)S(1)}, u32[]{:S(2)}, u32[]{:S(2)}) async-start(s32[8,1,32]{2,1,0:T(1,128)} %broadcast_in_dim.83), calls=%async_computation | async-start | bytes 8192 | tf_op jit(solution)/shard_map/all_to_all | solution.py:15
  22.9 10.5 %all-to-all-start.1 = ((bf16[32,8,1024]{2,1,0:T(8,128)(2,1)}), bf16[32,8,1024]{2,1,0:T(8,128)(2,1)S(1)}, u32[]{:S(2)}, u32[]{:S(2)}) async-start(bf16[32,8,1024]{2,1,0:T(8,128)(2,1)} %broadcast_in_dim.87), calls=%async_computation.1 | async-start | bytes 1048576 | tf_op jit(solution)/shard_map/all_to_all | solution.py:15
  33.5 7.9 %collective-permute-start.2 = (bf16[1024,256]{1,0:T(8,128)(2,1)S(1)}, bf16[1024,256]{1,0:T(8,128)(2,1)S(1)}, u32[]{:S(2)}, u32[]{:S(2)}) collective-permute-start(bf16[1024,256]{1,0:T(8,128)(2,1)S(1)} %copy-done.4), channel_id=1, source_target_pairs={{0,0},{32,1},{2,2},{34,3},{4,4},{36,5},{6,6},{38,7},{8,8},{40,9},{... | collective-permute-start | bytes 1572872 | tf_op jit(solution)/shard_map/ppermute | solution.py:43
  41.7 30.2 %collective-permute-done.2 = bf16[1024,256]{1,0:T(8,128)(2,1)S(1)} collective-permute-done((bf16[1024,256]{1,0:T(8,128)(2,1)S(1)}, bf16[1024,256]{1,0:T(8,128)(2,1)S(1)}, u32[]{:S(2)}, u32[]{:S(2)}) %collective-permute-start.2) | collective-permute-done | bytes 524320 | tf_op jit(solution)/shard_map/ppermute | solution.py:43
  73.0 9.3 %all-to-all-start.2 = ((bf16[8,32,256]{2,1,0:T(8,128)(2,1)}), bf16[8,32,256]{2,1,0:T(8,128)(2,1)S(1)}, u32[]{:S(2)}, u32[]{:S(2)}) async-start(bf16[8,32,256]{2,1,0:T(8,128)(2,1)} %bitcast.19), calls=%async_computation.2 | async-start | bytes 262144 | tf_op jit(solution)/shard_map/all_to_all | solution.py:167
  83.9 2.4 collective-permute-start.5
  89.9 7.4 %collective-permute-done = bf16[32,256]{1,0:T(8,128)(2,1)S(1)} collective-permute-done((bf16[32,256]{1,0:T(8,128)(2,1)S(1)}, bf16[32,256]{1,0:T(8,128)(2,1)S(1)}, u32[]{:S(2)}, u32[]{:S(2)}) %collective-permute-start) | collective-permute-done | bytes 16416 | tf_op jit(solution)/shard_map/ppermute | solution.py:43
  97.3 14.7 %all_to_all.46.own_ref = bf16[16,32,256]{2,1,0:T(8,128)(2,1)S(1)} all-to-all(bf16[16,32,256]{2,1,0:T(8,128)(2,1)S(1)} %broadcast_in_dim.88), channel_id=1, replica_groups={{0,8,16,24,64,72,80,88,128,136,144,152,192,200,208,216},{32,40,48,56,96..., dimensions={0} | all-to-all | bytes 524288 | tf_op jit(solution)/shard_map/all_to_all | solution.py:186
  112.0 20.7 %collective-permute-done.5.refs_2_ = bf16[2,1024,256]{2,1,0:T(8,128)(2,1)} collective-permute-done((bf16[2,1024,256]{2,1,0:T(8,128)(2,1)S(1)}, bf16[2,1024,256]{2,1,0:T(8,128)(2,1)}, u32[]{:S(2)}, u32[]{:S(2)}) %collective-permute-start.5) | collective-permute-done | bytes 1048608 | tf_op jit(solution)/shard_map/ppermute | solution.py:43
  135.1 14.0 %all_to_all.47.own_ref = bf16[16,32,256]{2,1,0:T(8,128)(2,1)S(1)} all-to-all(bf16[16,32,256]{2,1,0:T(8,128)(2,1)S(1)} %get-tuple-element.13), channel_id=1, replica_groups={{0,8,16,24,64,72,80,88,128,136,144,152,192,200,208,216},{32,40,48,56,96..., dimensions={0} | all-to-all | bytes 524288 | tf_op jit(solution)/shard_map/all_to_all | solution.py:186
  154.8 12.6 %all_to_all.48.own_ref = bf16[16,32,256]{2,1,0:T(8,128)(2,1)S(1)} all-to-all(bf16[16,32,256]{2,1,0:T(8,128)(2,1)S(1)} %get-tuple-element.14), channel_id=1, replica_groups={{0,8,16,24,64,72,80,88,128,136,144,152,192,200,208,216},{32,40,48,56,96..., dimensions={0} | all-to-all | bytes 524288 | tf_op jit(solution)/shard_map/all_to_all | solution.py:186
  172.9 12.6 %all_to_all.49.own_ref = bf16[16,32,256]{2,1,0:T(8,128)(2,1)S(1)} all-to-all(bf16[16,32,256]{2,1,0:T(8,128)(2,1)S(1)} %get-tuple-element.20), channel_id=1, replica_groups={{0,8,16,24,64,72,80,88,128,136,144,152,192,200,208,216},{32,40,48,56,96..., dimensions={0} | all-to-all | bytes 524288 | tf_op jit(solution)/shard_map/all_to_all | solution.py:186
  188.5 3.1 %draft_step.8 = (bf16[32,256]{1,0:T(8,128)(2,1)S(1)}, bf16[16,32,256]{2,1,0:T(8,128)(2,1)}) custom-call(bf16[16,32,256]{2,1,0:T(8,128)(2,1)S(1)} %all_to_all.49.own_ref, bf16[16,32,256]{2,1,0:T(8,128)(2,1)S(1)} %collective-permute-done.12.other_ref, bf16[2,1024,256]{2,1,0:T(8,128)(2,1)S(1)} %pad_maximum_fusion.refs_0_, ...), custom_call_target="tpu_custom_call" | custom-call | flops 134217728 | bytes 4980736 | tf_op jit(solution)/shard_map/draft_step/pallas_call | solution.py:76
  191.6 3.5 %all-to-all-start.8 = ((bf16[16,32,256]{2,1,0:T(8,128)(2,1)}), bf16[16,32,256]{2,1,0:T(8,128)(2,1)S(1)}, u32[]{:S(2)}, u32[]{:S(2)}) async-start(bf16[16,32,256]{2,1,0:T(8,128)(2,1)} %get-tuple-element.22), calls=%async_computation.8 | async-start | bytes 524288 | tf_op jit(solution)/shard_map/all_to_all | solution.py:186
  195.2 5.0 %collective-permute-start.9 = (bf16[32,256]{1,0:T(8,128)(2,1)S(1)}, bf16[32,256]{1,0:T(8,128)(2,1)S(1)}, u32[]{:S(2)}, u32[]{:S(2)}) collective-permute-start(bf16[32,256]{1,0:T(8,128)(2,1)S(1)} %get-tuple-element.17), channel_id=1, source_target_pairs={{0,0},{32,1},{2,2},{34,3},{4,4},{36,5},{6,6},{38,7},{8,8},{40,9},{... | collective-permute-start | bytes 49160 | tf_op jit(solution)/shard_map/ppermute | solution.py:43
  200.1 3.8 %convolution_convert_fusion = bf16[1536,256]{1,0:T(8,128)(2,1)} fusion(bf16[1536,1024]{1,0:T(8,128)(2,1)} %all-gather.2.cloned.1.call-done, bf16[1024,256]{1,0:T(8,128)(2,1)S(1)} %copy-done), kind=kOutput, calls=%fused_computation | convolution fusion | flops 805699584 | bytes 4456448 | tf_op jit(solution)/shard_map/dot_general | solution.py:195
  205.1 5.9 %all-to-all-start.6 = ((bf16[8,192,256]{2,1,0:T(8,128)(2,1)}), bf16[8,192,256]{2,1,0:T(8,128)(2,1)}, u32[]{:S(2)}, u32[]{:S(2)}) async-start(bf16[8,192,256]{2,1,0:T(8,128)(2,1)} %bitcast.79), calls=%async_computation.6 | async-start | bytes 1572864 | tf_op jit(solution)/shard_map/all_to_all | solution.py:196
  211.0 4.6 %collective-permute-start.10 = (bf16[32,256]{1,0:T(8,128)(2,1)S(1)}, bf16[32,256]{1,0:T(8,128)(2,1)S(1)}, u32[]{:S(2)}, u32[]{:S(2)}) collective-permute-start(bf16[32,256]{1,0:T(8,128)(2,1)S(1)} %get-tuple-element.18), channel_id=1, source_target_pairs={{0,0},{32,1},{2,2},{34,3},{4,4},{36,5},{6,6},{38,7},{8,8},{40,9},{... | collective-permute-start | bytes 49160 | tf_op jit(solution)/shard_map/ppermute | solution.py:43
  216.2 4.9 %collective-permute-start.11 = (bf16[32,256]{1,0:T(8,128)(2,1)S(1)}, bf16[32,256]{1,0:T(8,128)(2,1)S(1)}, u32[]{:S(2)}, u32[]{:S(2)}) collective-permute-start(bf16[32,256]{1,0:T(8,128)(2,1)S(1)} %get-tuple-element.19), channel_id=1, source_target_pairs={{0,0},{32,1},{2,2},{34,3},{4,4},{36,5},{6,6},{38,7},{8,8},{40,9},{... | collective-permute-start | bytes 49160 | tf_op jit(solution)/shard_map/ppermute | solution.py:43
  221.8 3.4 %collective-permute-done.11 = bf16[32,256]{1,0:T(8,128)(2,1)S(1)} collective-permute-done((bf16[32,256]{1,0:T(8,128)(2,1)S(1)}, bf16[32,256]{1,0:T(8,128)(2,1)S(1)}, u32[]{:S(2)}, u32[]{:S(2)}) %collective-permute-start.11) | collective-permute-done | bytes 16416 | tf_op jit(solution)/shard_map/ppermute | solution.py:43
  228.7 4.9 %collective-permute-start.13 = (bf16[32,256]{1,0:T(8,128)(2,1)S(1)}, bf16[32,256]{1,0:T(8,128)(2,1)S(1)}, u32[]{:S(2)}, u32[]{:S(2)}) collective-permute-start(bf16[32,256]{1,0:T(8,128)(2,1)S(1)} %get-tuple-element.21), channel_id=1, source_target_pairs={{0,0},{32,1},{2,2},{34,3},{4,4},{36,5},{6,6},{38,7},{8,8},{40,9},{... | collective-permute-start | bytes 49160 | tf_op jit(solution)/shard_map/ppermute | solution.py:43
  234.3 3.1 %draft_step.9 = (bf16[32,256]{1,0:T(8,128)(2,1)S(1)}, bf16[16,32,256]{2,1,0:T(8,128)(2,1)}) custom-call(bf16[16,32,256]{2,1,0:T(8,128)(2,1)S(1)} %all-to-all-done.8.own_ref, bf16[16,32,256]{2,1,0:T(8,128)(2,1)S(1)} %collective-permute-done.14.other_ref, bf16[2,1024,256]{2,1,0:T(8,128)(2,1)S(1)} %pad_maximum_fusion.refs_0_, ...), custom_call_target="tpu_custom_call" | custom-call | flops 134217728 | bytes 4980736 | tf_op jit(solution)/shard_map/draft_step/pallas_call | solution.py:76
  237.4 4.6 %collective-permute-start.15 = (bf16[32,256]{1,0:T(8,128)(2,1)S(1)}, bf16[32,256]{1,0:T(8,128)(2,1)S(1)}, u32[]{:S(2)}, u32[]{:S(2)}) collective-permute-start(bf16[32,256]{1,0:T(8,128)(2,1)S(1)} %get-tuple-element.23), channel_id=1, source_target_pairs={{0,0},{32,1},{2,2},{34,3},{4,4},{36,5},{6,6},{38,7},{8,8},{40,9},{... | collective-permute-start | bytes 49160 | tf_op jit(solution)/shard_map/ppermute | solution.py:43
  242.6 3.8 %collective-permute-done.15 = bf16[32,256]{1,0:T(8,128)(2,1)S(1)} collective-permute-done((bf16[32,256]{1,0:T(8,128)(2,1)S(1)}, bf16[32,256]{1,0:T(8,128)(2,1)S(1)}, u32[]{:S(2)}, u32[]{:S(2)}) %collective-permute-start.15) | collective-permute-done | bytes 16416 | tf_op jit(solution)/shard_map/ppermute | solution.py:43
  (77 shorter events, 40.2 us)
Async XLA Ops:
  7.2 64.9 %copy-start = (bf16[1024,256]{1,0:T(8,128)(2,1)S(1)}, bf16[1024,256]{1,0:T(8,128)(2,1)}, u32[]{:S(2)}) copy-start(bf16[1024,256]{1,0:T(8,128)(2,1)} %param.18) | copy-start | bytes 1572868
  8.5 11.2 %all-to-all-start = ((s32[8,1,32]{2,1,0:T(1,128)}), s32[8,1,32]{2,1,0:T(1,128)S(1)}, u32[]{:S(2)}, u32[]{:S(2)}) async-start(s32[8,1,32]{2,1,0:T(1,128)} %broadcast_in_dim.83), calls=%async_computation | async-start | bytes 8192 | tf_op jit(solution)/shard_map/all_to_all | solution.py:15
  15.0 157.9 %all-gather.2.cloned.1.call-start = ((), (), s32[]{:S(2)}) async-start(), calls=%async_computation.9 | async-start | bytes 3244032 | tf_op jit(solution)/shard_map/all_gather | solution.py:178
  15.7 25.9 %copy-start.2 = (bf16[32,6,256]{2,0,1:T(8,128)(2,1)S(1)}, bf16[32,6,256]{2,0,1:T(8,128)(2,1)}, u32[]{:S(2)}) copy-start(bf16[32,6,256]{2,0,1:T(8,128)(2,1)} %param.17) | copy-start | bytes 294916
  22.9 49.1 %all-to-all-start.1 = ((bf16[32,8,1024]{2,1,0:T(8,128)(2,1)}), bf16[32,8,1024]{2,1,0:T(8,128)(2,1)S(1)}, u32[]{:S(2)}, u32[]{:S(2)}) async-start(bf16[32,8,1024]{2,1,0:T(8,128)(2,1)} %broadcast_in_dim.87), calls=%async_computation.1 | async-start | bytes 1048576 | tf_op jit(solution)/shard_map/all_to_all | solution.py:15
  33.5 38.5 %collective-permute-start.2 = (bf16[1024,256]{1,0:T(8,128)(2,1)S(1)}, bf16[1024,256]{1,0:T(8,128)(2,1)S(1)}, u32[]{:S(2)}, u32[]{:S(2)}) collective-permute-start(bf16[1024,256]{1,0:T(8,128)(2,1)S(1)} %copy-done.4), channel_id=1, source_target_pairs={{0,0},{32,1},{2,2},{34,3},{4,4},{36,5},{6,6},{38,7},{8,8},{40,9},{... | collective-permute-start | bytes 1572872 | tf_op jit(solution)/shard_map/ppermute | solution.py:43
  41.4 30.5 %collective-permute-start.3 = (bf16[1024,256]{1,0:T(8,128)(2,1)S(1)}, bf16[1024,256]{1,0:T(8,128)(2,1)S(1)}, u32[]{:S(2)}, u32[]{:S(2)}) collective-permute-start(bf16[1024,256]{1,0:T(8,128)(2,1)S(1)} %copy-done.4), channel_id=1, source_target_pairs={{1,0},{33,1},{3,2},{35,3},{5,4},{37,5},{7,6},{39,7},{9,8},{41,9},{... | collective-permute-start | bytes 1572872 | tf_op jit(solution)/shard_map/ppermute | solution.py:43
  73.0 14.9 %all-to-all-start.2 = ((bf16[8,32,256]{2,1,0:T(8,128)(2,1)}), bf16[8,32,256]{2,1,0:T(8,128)(2,1)S(1)}, u32[]{:S(2)}, u32[]{:S(2)}) async-start(bf16[8,32,256]{2,1,0:T(8,128)(2,1)} %bitcast.19), calls=%async_computation.2 | async-start | bytes 262144 | tf_op jit(solution)/shard_map/all_to_all | solution.py:167
  82.4 29.6 %collective-permute-start.4 = (bf16[2,1024,256]{2,1,0:T(8,128)(2,1)S(1)}, bf16[2,1024,256]{2,1,0:T(8,128)(2,1)S(1)}, u32[]{:S(2)}, u32[]{:S(2)}) collective-permute-start(bf16[2,1024,256]{2,1,0:T(8,128)(2,1)S(1)} %pad_maximum_fusion.refs_0_), channel_id=1, source_target_pairs={{6,0},{7,1},{0,2},{1,3},{2,4},{3,5},{4,6},{5,7},{14,8},{15,9},{8,1... | collective-permute-start | bytes 3145736 | tf_op jit(solution)/shard_map/ppermute | solution.py:43
  83.9 48.8 %collective-permute-start.5 = (bf16[2,1024,256]{2,1,0:T(8,128)(2,1)S(1)}, bf16[2,1024,256]{2,1,0:T(8,128)(2,1)}, u32[]{:S(2)}, u32[]{:S(2)}) collective-permute-start(bf16[2,1024,256]{2,1,0:T(8,128)(2,1)S(1)} %pad_maximum_fusion.refs_0_), channel_id=1, source_target_pairs={{4,0},{5,1},{6,2},{7,3},{0,4},{1,5},{2,6},{3,7},{12,8},{13,9},{14,... | collective-permute-start | bytes 3145736 | tf_op jit(solution)/shard_map/ppermute | solution.py:43
  86.3 46.4 %collective-permute-start.6 = (bf16[2,1024,256]{2,1,0:T(8,128)(2,1)S(1)}, bf16[2,1024,256]{2,1,0:T(8,128)(2,1)}, u32[]{:S(2)}, u32[]{:S(2)}) collective-permute-start(bf16[2,1024,256]{2,1,0:T(8,128)(2,1)S(1)} %pad_maximum_fusion.refs_0_), channel_id=1, source_target_pairs={{2,0},{3,1},{4,2},{5,3},{6,4},{7,5},{0,6},{1,7},{10,8},{11,9},{12,... | collective-permute-start | bytes 3145736 | tf_op jit(solution)/shard_map/ppermute | solution.py:43
  88.0 9.3 %collective-permute-start = (bf16[32,256]{1,0:T(8,128)(2,1)S(1)}, bf16[32,256]{1,0:T(8,128)(2,1)S(1)}, u32[]{:S(2)}, u32[]{:S(2)}) collective-permute-start(bf16[32,256]{1,0:T(8,128)(2,1)S(1)} %add_convert_fusion.1), channel_id=1, source_target_pairs={{0,0},{32,1},{2,2},{34,3},{4,4},{36,5},{6,6},{38,7},{8,8},{40,9},{... | collective-permute-start | bytes 49160 | tf_op jit(solution)/shard_map/ppermute | solution.py:43
  112.0 20.7 %collective-permute-start.1 = (bf16[16,32,256]{2,1,0:T(8,128)(2,1)S(1)}, bf16[16,32,256]{2,1,0:T(8,128)(2,1)S(1)}, u32[]{:S(2)}, u32[]{:S(2)}) collective-permute-start(bf16[16,32,256]{2,1,0:T(8,128)(2,1)S(1)} %all_to_all.46.own_ref), channel_id=1, source_target_pairs={{1,0},{0,1},{3,2},{2,3},{5,4},{4,5},{7,6},{6,7},{9,8},{8,9},{11,10... | collective-permute-start | bytes 786440 | tf_op jit(solution)/shard_map/ppermute | solution.py:43
  149.1 3.3 %collective-permute-start.7 = (bf16[16,32,256]{2,1,0:T(8,128)(2,1)S(1)}, bf16[16,32,256]{2,1,0:T(8,128)(2,1)S(1)}, u32[]{:S(2)}, u32[]{:S(2)}) collective-permute-start(bf16[16,32,256]{2,1,0:T(8,128)(2,1)S(1)} %all_to_all.47.own_ref), channel_id=1, source_target_pairs={{1,0},{0,1},{3,2},{2,3},{5,4},{4,5},{7,6},{6,7},{9,8},{8,9},{11,10... | collective-permute-start | bytes 786440 | tf_op jit(solution)/shard_map/ppermute | solution.py:43
  167.3 3.1 %collective-permute-start.8 = (bf16[16,32,256]{2,1,0:T(8,128)(2,1)S(1)}, bf16[16,32,256]{2,1,0:T(8,128)(2,1)S(1)}, u32[]{:S(2)}, u32[]{:S(2)}) collective-permute-start(bf16[16,32,256]{2,1,0:T(8,128)(2,1)S(1)} %all_to_all.48.own_ref), channel_id=1, source_target_pairs={{1,0},{0,1},{3,2},{2,3},{5,4},{4,5},{7,6},{6,7},{9,8},{8,9},{11,10... | collective-permute-start | bytes 786440 | tf_op jit(solution)/shard_map/ppermute | solution.py:43
  185.4 3.1 %collective-permute-start.12 = (bf16[16,32,256]{2,1,0:T(8,128)(2,1)S(1)}, bf16[16,32,256]{2,1,0:T(8,128)(2,1)S(1)}, u32[]{:S(2)}, u32[]{:S(2)}) collective-permute-start(bf16[16,32,256]{2,1,0:T(8,128)(2,1)S(1)} %all_to_all.49.own_ref), channel_id=1, source_target_pairs={{1,0},{0,1},{3,2},{2,3},{5,4},{4,5},{7,6},{6,7},{9,8},{8,9},{11,10... | collective-permute-start | bytes 786440 | tf_op jit(solution)/shard_map/ppermute | solution.py:43
  191.6 13.5 %all-to-all-start.8 = ((bf16[16,32,256]{2,1,0:T(8,128)(2,1)}), bf16[16,32,256]{2,1,0:T(8,128)(2,1)S(1)}, u32[]{:S(2)}, u32[]{:S(2)}) async-start(bf16[16,32,256]{2,1,0:T(8,128)(2,1)} %get-tuple-element.22), calls=%async_computation.8 | async-start | bytes 524288 | tf_op jit(solution)/shard_map/all_to_all | solution.py:186
  195.2 20.5 %collective-permute-start.9 = (bf16[32,256]{1,0:T(8,128)(2,1)S(1)}, bf16[32,256]{1,0:T(8,128)(2,1)S(1)}, u32[]{:S(2)}, u32[]{:S(2)}) collective-permute-start(bf16[32,256]{1,0:T(8,128)(2,1)S(1)} %get-tuple-element.17), channel_id=1, source_target_pairs={{0,0},{32,1},{2,2},{34,3},{4,4},{36,5},{6,6},{38,7},{8,8},{40,9},{... | collective-permute-start | bytes 49160 | tf_op jit(solution)/shard_map/ppermute | solution.py:43
  205.1 20.7 %all-to-all-start.6 = ((bf16[8,192,256]{2,1,0:T(8,128)(2,1)}), bf16[8,192,256]{2,1,0:T(8,128)(2,1)}, u32[]{:S(2)}, u32[]{:S(2)}) async-start(bf16[8,192,256]{2,1,0:T(8,128)(2,1)} %bitcast.79), calls=%async_computation.6 | async-start | bytes 1572864 | tf_op jit(solution)/shard_map/all_to_all | solution.py:196
  211.0 10.1 %collective-permute-start.10 = (bf16[32,256]{1,0:T(8,128)(2,1)S(1)}, bf16[32,256]{1,0:T(8,128)(2,1)S(1)}, u32[]{:S(2)}, u32[]{:S(2)}) collective-permute-start(bf16[32,256]{1,0:T(8,128)(2,1)S(1)} %get-tuple-element.18), channel_id=1, source_target_pairs={{0,0},{32,1},{2,2},{34,3},{4,4},{36,5},{6,6},{38,7},{8,8},{40,9},{... | collective-permute-start | bytes 49160 | tf_op jit(solution)/shard_map/ppermute | solution.py:43
  216.2 9.0 %collective-permute-start.11 = (bf16[32,256]{1,0:T(8,128)(2,1)S(1)}, bf16[32,256]{1,0:T(8,128)(2,1)S(1)}, u32[]{:S(2)}, u32[]{:S(2)}) collective-permute-start(bf16[32,256]{1,0:T(8,128)(2,1)S(1)} %get-tuple-element.19), channel_id=1, source_target_pairs={{0,0},{32,1},{2,2},{34,3},{4,4},{36,5},{6,6},{38,7},{8,8},{40,9},{... | collective-permute-start | bytes 49160 | tf_op jit(solution)/shard_map/ppermute | solution.py:43
  225.8 8.5 %collective-permute-start.14 = (bf16[16,32,256]{2,1,0:T(8,128)(2,1)S(1)}, bf16[16,32,256]{2,1,0:T(8,128)(2,1)S(1)}, u32[]{:S(2)}, u32[]{:S(2)}) collective-permute-start(bf16[16,32,256]{2,1,0:T(8,128)(2,1)S(1)} %all-to-all-done.8.own_ref), channel_id=1, source_target_pairs={{1,0},{0,1},{3,2},{2,3},{5,4},{4,5},{7,6},{6,7},{9,8},{8,9},{11,10... | collective-permute-start | bytes 786440 | tf_op jit(solution)/shard_map/ppermute | solution.py:43
  228.7 13.3 %collective-permute-start.13 = (bf16[32,256]{1,0:T(8,128)(2,1)S(1)}, bf16[32,256]{1,0:T(8,128)(2,1)S(1)}, u32[]{:S(2)}, u32[]{:S(2)}) collective-permute-start(bf16[32,256]{1,0:T(8,128)(2,1)S(1)} %get-tuple-element.21), channel_id=1, source_target_pairs={{0,0},{32,1},{2,2},{34,3},{4,4},{36,5},{6,6},{38,7},{8,8},{40,9},{... | collective-permute-start | bytes 49160 | tf_op jit(solution)/shard_map/ppermute | solution.py:43
  237.4 9.0 %collective-permute-start.15 = (bf16[32,256]{1,0:T(8,128)(2,1)S(1)}, bf16[32,256]{1,0:T(8,128)(2,1)S(1)}, u32[]{:S(2)}, u32[]{:S(2)}) collective-permute-start(bf16[32,256]{1,0:T(8,128)(2,1)S(1)} %get-tuple-element.23), channel_id=1, source_target_pairs={{0,0},{32,1},{2,2},{34,3},{4,4},{36,5},{6,6},{38,7},{8,8},{40,9},{... | collective-permute-start | bytes 49160 | tf_op jit(solution)/shard_map/ppermute | solution.py:43
  (3 other events, 57.6 us)
Sparse Core Ops, SparseCore 0:
  22.2 93.4 all-gather.1

commit v3 on v1

--- a/solution.py
+++ b/solution.py
@@ -1,10 +1,15 @@
+import functools
+
 import jax
 import jax.numpy as jnp
 from jax import lax
+from jax.experimental import pallas as pl
+from jax.experimental.pallas import tpu as pltpu
 from jax.sharding import PartitionSpec as P
 
 HD = 128
 STEPS = 5
+HOLD = 2
 
 
 def spread(block, axis):
@@ -12,17 +17,113 @@
     return lax.all_to_all(copies, axis, split_axis=0, concat_axis=0, tiled=True)
 
 
-def accepted_of_my_windows(accepted):
-    dp_size, tensor_size = lax.axis_size("dp"), lax.axis_size("tensor")
-    ratio = dp_size // tensor_size
+YH, YL, Z, X, C = 2, 2, 8, 4, 2
+BLOCKS = [list(range(yh * YL * Z, (yh + 1) * YL * Z)) for yh in range(YH)]
+
+
+def route(source):
     pairs = []
-    for j in range(dp_size):
-        for i in range(tensor_size):
-            source = (ratio * i + j % ratio) * tensor_size + j // ratio
-            pairs.append((source, j * tensor_size + i))
-    block = lax.ppermute(accepted, ("dp", "tensor"), pairs)
-    rows = accepted.shape[0] // ratio
-    return lax.dynamic_slice_in_dim(block, lax.axis_index("dp") % ratio * rows, rows, 0)
+    for yh in range(YH):
+        for yl in range(YL):
+            for z in range(Z):
+                for x in range(X):
+                    for c in range(C):
+                        ends = []
+                        for syh, sx, sc in (source(yh, x, c), (yh, x, c)):
+                            ends.append((((syh * YL + yl) * Z + z) * X + sx % X) * C + sc)
+                        pairs.append(tuple(ends))
+    return pairs
+
+
+SWAPPED = route(lambda yh, x, c: (c, x, yh))
+SWAPPED_OTHER = route(lambda yh, x, c: (c, x, 1 - yh))
+OTHER_CORE = route(lambda yh, x, c: (yh, x, 1 - c))
+FROM_LEFT = route(lambda yh, x, c: (yh, x - 1, c))
+FROM_RIGHT = route(lambda yh, x, c: (yh, x + 1, c))
+
+
+def move(block, pairs):
+    return lax.ppermute(block, ("dp", "tensor"), pairs)
+
+
+def draft_kernel(own_ref, other_ref, here_ref, left_ref, right_ref, low_ref, high_ref, *refs, last, to_hbm):
+    place = lax.axis_index("tensor")
+    x, c = place // C, lax.rem(place, C)
+    count, height, cols = own_ref.shape
+    if last:
+        *earlier_refs, stack_ref, rows_ref = refs
+    elif to_hbm:
+        drafted_ref, copies_hbm_ref, rows_ref, copies_ref, sem = refs
+    else:
+        drafted_ref, copies_ref, rows_ref = refs
+    for k in range(count):
+        rows_ref[c * count + k] = own_ref[k]
+        rows_ref[(1 - c) * count + k] = other_ref[k]
+    total = jnp.zeros((height, cols), jnp.float32)
+    per_x = rows_ref.shape[0] // X
+    half = per_x // 2
+    for offset, shift, weight_ref in (
+        (0, 0, here_ref),
+        (X - 1, 0, left_ref),
+        (1, 0, right_ref),
+        (2, 0, low_ref),
+        (2, half, high_ref),
+    ):
+        first = lax.rem(x + offset, X) * per_x + shift
+        wide = jnp.concatenate(
+            [rows_ref[first + k] for k in range(weight_ref.shape[0] // cols)], axis=1
+        )
+        total += jnp.dot(wide, weight_ref[...], preferred_element_type=jnp.float32)
+    drafted = jnp.tanh(2.0 * total).astype(own_ref.dtype)
+    if last:
+        for k, earlier_ref in enumerate(earlier_refs):
+            stack_ref[k] = earlier_ref[...]
+        stack_ref[len(earlier_refs)] = drafted
+        return
+    drafted_ref[...] = drafted
+    for copy in range(count):
+        copies_ref[copy] = drafted
+    if to_hbm:
+        send = pltpu.make_async_copy(copies_ref, copies_hbm_ref, sem)
+        send.start()
+        send.wait()
+
+
+def draft_step(own, other, weights, earlier, last, to_hbm):
+    count, height, cols = own.shape
+    vmem = pl.BlockSpec(memory_space=pltpu.VMEM)
+    rows = pltpu.VMEM((2 * count, height, cols), own.dtype)
+    block = jax.ShapeDtypeStruct((height, cols), own.dtype)
+    copies = jax.ShapeDtypeStruct(own.shape, own.dtype)
+    if last:
+        operands = (own, other, *weights, *earlier)
+        out_shape = jax.ShapeDtypeStruct((len(earlier) + 1, height, cols), own.dtype)
+        out_specs, scratch = vmem, [rows]
+    else:
+        operands = (own, other, *weights)
+        out_shape, out_specs, scratch = (block, copies), (vmem, vmem), [rows]
+        if to_hbm:
+            out_specs = (vmem, pl.BlockSpec(memory_space=pltpu.HBM))
+            scratch = [rows, pltpu.VMEM(own.shape, own.dtype), pltpu.SemaphoreType.DMA]
+    return pl.pallas_call(
+        functools.partial(draft_kernel, last=last, to_hbm=to_hbm),
+        out_shape=out_shape,
+        in_specs=[vmem] * len(operands),
+        out_specs=out_specs,
+        scratch_shapes=scratch,
+        compiler_params=pltpu.CompilerParams(vmem_limit_bytes=24 << 20),
+        cost_estimate=pl.CostEstimate(
+            flops=4 * count * height * cols * cols,
+            bytes_accessed=4 * count * cols * cols + 6 * count * height * cols,
+            transcendentals=height * cols,
+        ),
+        name="draft_step",
+    )(*operands)
+
+
+def accepted_of_my_windows(everyone):
+    rows = everyone.shape[0] // lax.axis_size("dp")
+    return lax.dynamic_slice_in_dim(everyone, lax.axis_index("dp") * rows, rows, 0)
 
 
 def pick(rows, accepted):
@@ -49,8 +150,14 @@
     kv_here = new_keys.shape[2] // HD
     group_size = query_width // HD // kv_here
     tensor_size = lax.axis_size("tensor")
-    own_accepted = accepted_of_my_windows(accepted)
-    draft_columns = lax.all_gather(draft_weight, "tensor", axis=0, tiled=True)
+    everyone, swapped, swapped_other = lax.optimization_barrier(
+        (
+            spread(accepted, "tensor").reshape(-1),
+            move(draft_weight, SWAPPED),
+            move(draft_weight, SWAPPED_OTHER),
+        )
+    )
+    own_accepted = accepted_of_my_windows(everyone)
 
     query_split = queries.reshape(windows_here, tokens_here, kv_here, group_size, HD)
     keys_cached = key_cache.reshape(windows_here, cache_size, kv_here, HD)
@@ -89,7 +196,16 @@
     )
     attended = mixed_rows.astype(jnp.bfloat16).reshape(windows_here, tokens_here, query_width)
 
-    picked_rows = spread(pick(attended, own_accepted), "dp").reshape(-1, query_width)
+    picked = pick(attended, own_accepted)
+    low_half = lax.axis_index("dp") < YL * Z
+    here = jnp.concatenate(
+        [
+            jnp.where(low_half, swapped, swapped_other),
+            jnp.where(low_half, swapped_other, swapped),
+        ]
+    )
+    left, right = move(here, FROM_LEFT), move(here, FROM_RIGHT)
+    picked_rows = spread(picked, "dp").reshape(-1, query_width)
     picked_part = jnp.dot(picked_rows, out_weight, preferred_element_type=jnp.float32)
     block_windows, block_tokens, block_cols = residual.shape
     shares = lax.all_to_all(
@@ -99,33 +215,39 @@
         concat_axis=0,
         tiled=True,
     )
+    shares, left, right = lax.optimization_barrier((shares, left, right))
+    low = move(left[: left.shape[0] // 2], FROM_LEFT)
+    high = move(right[right.shape[0] // 2 :], FROM_RIGHT)
     current = (
         pick(residual, accepted).astype(jnp.float32) + jnp.sum(shares.astype(jnp.float32), axis=0)
     ).astype(jnp.bfloat16)
 
-    partial_out = jnp.dot(
-        lax.all_gather(
-            attended.reshape(windows_here * tokens_here, query_width), "dp", axis=0, tiled=True
-        ),
-        out_weight,
-        preferred_element_type=jnp.float32,
-    )
+    gathered = lax.all_gather(
+        attended.reshape(windows_here * tokens_here, query_width), "dp", axis=0, tiled=True
+    )
+
+    current = move(current, SWAPPED)
+    copies = jnp.broadcast_to(current[None], (len(BLOCKS[0]),) + current.shape)
+    weights = (here, left, right, low, high)
+    results = []
+    for step in range(STEPS):
+        own = lax.all_to_all(
+            copies, "dp", split_axis=0, concat_axis=0, tiled=True, axis_index_groups=BLOCKS
+        )
+        other = move(own, OTHER_CORE)
+        last = step + 1 == STEPS
+        drafted = draft_step(own, other, weights, results, last, step == HOLD)
+        if last:
+            break
+        drafted, copies = drafted
+        results.append(drafted)
+        if step == HOLD:
+            gathered, copies = lax.optimization_barrier((gathered, copies))
+    partial_out = jnp.dot(gathered, out_weight, preferred_element_type=jnp.float32)
     summed = lax.psum_scatter(partial_out, "tensor", scatter_dimension=0, tiled=True)
-    flat_residual = residual.reshape(block_windows * block_tokens, block_cols).astype(jnp.float32)
-    verified = (
-        (flat_residual + summed)
-        .astype(jnp.bfloat16)
-        .reshape(block_windows, block_tokens, block_cols)
-    )
-
-    columns = draft_columns.reshape(-1, block_cols, draft_columns.shape[1])
-    results = []
-    for draft_step in range(STEPS):
-        inputs = spread(current, "dp")
-        product = jnp.einsum("jwk,jkn->wn", inputs, columns, preferred_element_type=jnp.float32)
-        current = jnp.tanh(2.0 * product).astype(jnp.bfloat16)
-        results.append(current)
-    return (verified, jnp.stack(results))
+    drafted, summed = lax.optimization_barrier((drafted, summed))
+    verified = (residual.astype(jnp.float32) + summed.reshape(residual.shape)).astype(jnp.bfloat16)
+    return (verified, move(drafted, SWAPPED))
 
 
 def solution(mesh):

time: 204 us -> 195 us (0.956)
  the two profiles are of different devices: /device:TPU:32 before, /device:TPU:1 now
where the time goes in v3:
time: 195 us; the launch traced here: 194 us
  starting transfers between devices  57.1 us (29%)
  blocking collectives  55.5 us (28%)
  waiting for transfers between devices  35.4 us (18%)
  between operations  14.3 us (7%)
  Pallas kernels  11.1 us (6%)
  local copies, waits for them, and re-layouts  9.08 us (5%)
  matrix products  7.94 us (4%)
  other arithmetic  3.41 us (2%)
    all_to_all x4, blocking collectives, per_device(): lax.all_to_all(copies, 'dp', split_axis=0, concat_axis=0, tiled=True, axi...  55.5 us
    ppermute x13, starting transfers between devices, move(): return lax.ppermute(block, ('dp', 'tensor'), pairs)  26.6 us
    ppermute x13, waiting for transfers between devices, move(): return lax.ppermute(block, ('dp', 'tensor'), pairs)  14.2 us
    all_to_all x2, starting transfers between devices, spread(): return lax.all_to_all(copies, axis, split_axis=0, concat_axis=0, tiled=True)  14 us
    pallas_call x5, Pallas kernels, draft_step(): pl.pallas_call(functools.partial(draft_kernel, last=last, to_hbm=to_hbm),...  11.1 us
    all_to_all x2, waiting for transfers between devices, spread(): return lax.all_to_all(copies, axis, split_axis=0, concat_axis=0, tiled=True)  10.4 us
    all_to_all x1, starting transfers between devices, per_device(): lax.all_to_all(picked_part.astype(jnp.bfloat16).reshape(tensor_size, bloc...  9.05 us
    all_to_all x1, starting transfers between devices, per_device(): lax.all_to_all(copies, 'dp', split_axis=0, concat_axis=0, tiled=True, axi...  7.39 us
  transfers between devices with their start and end apart: 19, of which 14 were waited for; matrix products, arithmetic and copies ran while one was open for 7% of the time, Pallas kernels for 6%

profile of v3, /device:TPU:1, one launch (start us, length us, event | category | flops | bytes accessed | tf_op | source)
XLA Modules:
  0.0 193.8 jit_solution(10717477915148077876)
XLA Ops:
  7.2 3.3 %collective-permute-start.1 = (bf16[1024,256]{1,0:T(8,128)(2,1)}, bf16[1024,256]{1,0:T(8,128)(2,1)S(1)}, u32[]{:S(2)}, u32[]{:S(2)}) collective-permute-start(bf16[1024,256]{1,0:T(8,128)(2,1)} %param.19), channel_id=1, source_target_pairs={{1,0},{129,1},{3,2},{131,3},{5,4},{133,5},{7,6},{135,7},{9,8},{137... | collective-permute-start | bytes 1572872 | tf_op jit(solution)/shard_map/ppermute | solution.py:46
  10.5 3.1 %collective-permute-start = (bf16[1024,256]{1,0:T(8,128)(2,1)}, bf16[1024,256]{1,0:T(8,128)(2,1)S(1)}, u32[]{:S(2)}, u32[]{:S(2)}) collective-permute-start(bf16[1024,256]{1,0:T(8,128)(2,1)} %param.19), channel_id=1, source_target_pairs={{0,0},{128,1},{2,2},{130,3},{4,4},{132,5},{6,6},{134,7},{8,8},{136... | collective-permute-start | bytes 1572872 | tf_op jit(solution)/shard_map/ppermute | solution.py:46
  14.9 4.4 %all-to-all-start = ((s32[8,1,32]{2,1,0:T(1,128)}), s32[8,1,32]{2,1,0:T(1,128)S(1)}, u32[]{:S(2)}, u32[]{:S(2)}) async-start(s32[8,1,32]{2,1,0:T(1,128)} %broadcast_in_dim.83), calls=%async_computation | async-start | bytes 8192 | tf_op jit(solution)/shard_map/all_to_all | solution.py:17
  27.0 9.6 %all-to-all-start.1 = ((bf16[32,8,1024]{2,1,0:T(8,128)(2,1)}), bf16[32,8,1024]{2,1,0:T(8,128)(2,1)S(1)}, u32[]{:S(2)}, u32[]{:S(2)}) async-start(bf16[32,8,1024]{2,1,0:T(8,128)(2,1)} %broadcast_in_dim.87), calls=%async_computation.1 | async-start | bytes 1048576 | tf_op jit(solution)/shard_map/all_to_all | solution.py:17
  39.7 9.9 %all-to-all-done.1 = bf16[32,8,1024]{2,1,0:T(8,128)(2,1)S(1)} async-done(((bf16[32,8,1024]{2,1,0:T(8,128)(2,1)}), bf16[32,8,1024]{2,1,0:T(8,128)(2,1)S(1)}, u32[]{:S(2)}, u32[]{:S(2)}) %all-to-all-start.1) | async-done | bytes 524320 | tf_op jit(solution)/shard_map/all_to_all | solution.py:17
  50.6 9.1 %all-to-all-start.2 = ((bf16[8,32,256]{2,1,0:T(8,128)(2,1)}), bf16[8,32,256]{2,1,0:T(8,128)(2,1)S(1)}, u32[]{:S(2)}, u32[]{:S(2)}) async-start(bf16[8,32,256]{2,1,0:T(8,128)(2,1)} %bitcast.19), calls=%async_computation.2 | async-start | bytes 262144 | tf_op jit(solution)/shard_map/all_to_all | solution.py:211
  60.6 2.0 %collective-permute-done.2.left_ref = bf16[2048,256]{1,0:T(8,128)(2,1)} collective-permute-done((bf16[2048,256]{1,0:T(8,128)(2,1)S(1)}, bf16[2048,256]{1,0:T(8,128)(2,1)}, u32[]{:S(2)}, u32[]{:S(2)}) %collective-permute-start.2) | collective-permute-done | bytes 1048608 | tf_op jit(solution)/shard_map/ppermute | solution.py:46
  62.6 4.7 %all-to-all-done.2 = bf16[8,32,256]{2,1,0:T(8,128)(2,1)S(1)} async-done(((bf16[8,32,256]{2,1,0:T(8,128)(2,1)}), bf16[8,32,256]{2,1,0:T(8,128)(2,1)S(1)}, u32[]{:S(2)}, u32[]{:S(2)}) %all-to-all-start.2) | async-done | bytes 131104 | tf_op jit(solution)/shard_map/all_to_all | solution.py:211
  67.3 5.2 %collective-permute-start.4 = (bf16[32,256]{1,0:T(8,128)(2,1)S(1)}, bf16[32,256]{1,0:T(8,128)(2,1)S(1)}, u32[]{:S(2)}, u32[]{:S(2)}) collective-permute-start(bf16[32,256]{1,0:T(8,128)(2,1)S(1)} %add_convert_fusion.1), channel_id=1, source_target_pairs={{0,0},{128,1},{2,2},{130,3},{4,4},{132,5},{6,6},{134,7},{8,8},{136... | collective-permute-start | bytes 49160 | tf_op jit(solution)/shard_map/ppermute | solution.py:46
  74.6 7.4 %all-to-all-start.3 = ((bf16[16,32,256]{2,1,0:T(8,128)(2,1)}), bf16[16,32,256]{2,1,0:T(8,128)(2,1)S(1)}, u32[]{:S(2)}, u32[]{:S(2)}) async-start(bf16[16,32,256]{2,1,0:T(8,128)(2,1)} %broadcast_in_dim.88), calls=%async_computation.3 | async-start | bytes 524288 | tf_op jit(solution)/shard_map/all_to_all | solution.py:234
  86.3 6.0 %all-to-all-done.3.own_ref = bf16[16,32,256]{2,1,0:T(8,128)(2,1)S(1)} async-done(((bf16[16,32,256]{2,1,0:T(8,128)(2,1)}), bf16[16,32,256]{2,1,0:T(8,128)(2,1)S(1)}, u32[]{:S(2)}, u32[]{:S(2)}) %all-to-all-start.3) | async-done | bytes 262176 | tf_op jit(solution)/shard_map/all_to_all | solution.py:234
  95.8 2.2 %draft_step.5 = (bf16[32,256]{1,0:T(8,128)(2,1)S(1)}, bf16[16,32,256]{2,1,0:T(8,128)(2,1)S(1)}) custom-call(bf16[16,32,256]{2,1,0:T(8,128)(2,1)S(1)} %all-to-all-done.3.own_ref, bf16[16,32,256]{2,1,0:T(8,128)(2,1)S(1)} %collective-permute-done.5.other_ref, bf16[2048,256]{1,0:T(8,128)(2,1)S(1)} %pad_maximum_fusion.here_ref, ...), custom_call_target="tpu_custom_call" | custom-call | flops 134217728 | bytes 4980736 | tf_op jit(solution)/shard_map/draft_step/pallas_call | solution.py:108
  98.1 16.2 %all_to_all.41.own_ref = bf16[16,32,256]{2,1,0:T(8,128)(2,1)S(1)} all-to-all(bf16[16,32,256]{2,1,0:T(8,128)(2,1)S(1)} %get-tuple-element.26), channel_id=1, replica_groups={{0,8,16,24,32,40,48,56,64,72,80,88,96,104,112,120},{128,136,144,152,160..., dimensions={0} | all-to-all | bytes 524288 | tf_op jit(solution)/shard_map/all_to_all | solution.py:234
  115.8 2.2 %draft_step.6 = (bf16[32,256]{1,0:T(8,128)(2,1)S(1)}, bf16[16,32,256]{2,1,0:T(8,128)(2,1)S(1)}) custom-call(bf16[16,32,256]{2,1,0:T(8,128)(2,1)S(1)} %all_to_all.41.own_ref, bf16[16,32,256]{2,1,0:T(8,128)(2,1)S(1)} %collective-permute-done.8.other_ref, bf16[2048,256]{1,0:T(8,128)(2,1)S(1)} %pad_maximum_fusion.here_ref, ...), custom_call_target="tpu_custom_call" | custom-call | flops 134217728 | bytes 4980736 | tf_op jit(solution)/shard_map/draft_step/pallas_call | solution.py:108
  118.0 13.4 %all_to_all.42.own_ref = bf16[16,32,256]{2,1,0:T(8,128)(2,1)S(1)} all-to-all(bf16[16,32,256]{2,1,0:T(8,128)(2,1)S(1)} %get-tuple-element.27), channel_id=1, replica_groups={{0,8,16,24,32,40,48,56,64,72,80,88,96,104,112,120},{128,136,144,152,160..., dimensions={0} | all-to-all | bytes 524288 | tf_op jit(solution)/shard_map/all_to_all | solution.py:234
  134.5 2.3 %draft_step.7 = (bf16[32,256]{1,0:T(8,128)(2,1)S(1)}, bf16[16,32,256]{2,1,0:T(8,128)(2,1)S(1)}) custom-call(bf16[16,32,256]{2,1,0:T(8,128)(2,1)S(1)} %all_to_all.42.own_ref, bf16[16,32,256]{2,1,0:T(8,128)(2,1)S(1)} %collective-permute-done.9.other_ref, bf16[2048,256]{1,0:T(8,128)(2,1)S(1)} %pad_maximum_fusion.here_ref, ...), custom_call_target="tpu_custom_call" | custom-call | flops 134217728 | bytes 4980736 | tf_op jit(solution)/shard_map/draft_step/pallas_call | solution.py:108
  136.8 4.0 %fusion.19 = f32[1536,256]{1,0:T(8,128)} fusion(bf16[1536,1024]{1,0:T(8,128)(2,1)} %all-gather.2.cloned.1.call-done, bf16[1024,256]{1,0:T(8,128)(2,1)S(1)} %copy-done), kind=kOutput, calls=%fused_computation.43 | convolution fusion | flops 805306368 | bytes 5242880 | tf_op jit(solution)/shard_map/dot_general | solution.py:246
  140.8 13.0 %all_to_all.43.own_ref = bf16[16,32,256]{2,1,0:T(8,128)(2,1)S(1)} all-to-all(bf16[16,32,256]{2,1,0:T(8,128)(2,1)S(1)} %get-tuple-element.29), channel_id=1, replica_groups={{0,8,16,24,32,40,48,56,64,72,80,88,96,104,112,120},{128,136,144,152,160..., dimensions={0} | all-to-all | bytes 524288 | tf_op jit(solution)/shard_map/all_to_all | solution.py:234
  153.8 2.2 %collective-permute-start.10 = (bf16[16,32,256]{2,1,0:T(8,128)(2,1)S(1)}, bf16[16,32,256]{2,1,0:T(8,128)(2,1)S(1)}, u32[]{:S(2)}, u32[]{:S(2)}) collective-permute-start(bf16[16,32,256]{2,1,0:T(8,128)(2,1)S(1)} %all_to_all.43.own_ref), channel_id=1, source_target_pairs={{1,0},{0,1},{3,2},{2,3},{5,4},{4,5},{7,6},{6,7},{9,8},{8,9},{11,10... | collective-permute-start | bytes 786440 | tf_op jit(solution)/shard_map/ppermute | solution.py:46
  157.1 2.2 %draft_step.8 = (bf16[32,256]{1,0:T(8,128)(2,1)S(1)}, bf16[16,32,256]{2,1,0:T(8,128)(2,1)S(1)}) custom-call(bf16[16,32,256]{2,1,0:T(8,128)(2,1)S(1)} %all_to_all.43.own_ref, bf16[16,32,256]{2,1,0:T(8,128)(2,1)S(1)} %collective-permute-done.10.other_ref, bf16[2048,256]{1,0:T(8,128)(2,1)S(1)} %pad_maximum_fusion.here_ref, ...), custom_call_target="tpu_custom_call" | custom-call | flops 134217728 | bytes 4980736 | tf_op jit(solution)/shard_map/draft_step/pallas_call | solution.py:108
  159.4 12.9 %all_to_all.44.own_ref = bf16[16,32,256]{2,1,0:T(8,128)(2,1)S(1)} all-to-all(bf16[16,32,256]{2,1,0:T(8,128)(2,1)S(1)} %get-tuple-element.30), channel_id=1, replica_groups={{0,8,16,24,32,40,48,56,64,72,80,88,96,104,112,120},{128,136,144,152,160..., dimensions={0} | all-to-all | bytes 524288 | tf_op jit(solution)/shard_map/all_to_all | solution.py:234
  172.3 2.2 %collective-permute-start.11 = (bf16[16,32,256]{2,1,0:T(8,128)(2,1)S(1)}, bf16[16,32,256]{2,1,0:T(8,128)(2,1)S(1)}, u32[]{:S(2)}, u32[]{:S(2)}) collective-permute-start(bf16[16,32,256]{2,1,0:T(8,128)(2,1)S(1)} %all_to_all.44.own_ref), channel_id=1, source_target_pairs={{1,0},{0,1},{3,2},{2,3},{5,4},{4,5},{7,6},{6,7},{9,8},{8,9},{11,10... | collective-permute-start | bytes 786440 | tf_op jit(solution)/shard_map/ppermute | solution.py:46
  175.6 2.2 %draft_step.9 = bf16[5,32,256]{2,1,0:T(8,128)(2,1)S(1)} custom-call(bf16[16,32,256]{2,1,0:T(8,128)(2,1)S(1)} %all_to_all.44.own_ref, bf16[16,32,256]{2,1,0:T(8,128)(2,1)S(1)} %collective-permute-done.11.other_ref, bf16[2048,256]{1,0:T(8,128)(2,1)S(1)} %pad_maximum_fusion.here_ref, bf16[2048,256]{1,0:T(8,128)(2,1)} %collective-permute-done.2.left_ref, ...), custom_call_target="tpu_custom_call" | custom-call | flops 134217728 | bytes 4980736 | tf_op jit(solution)/shard_map/draft_step/pallas_call | solution.py:108
  178.8 5.4 %collective-permute-start.12 = (bf16[5,32,256]{2,1,0:T(8,128)(2,1)S(1)}, bf16[5,32,256]{2,1,0:T(8,128)(2,1)S(1)}, u32[]{:S(2)}, u32[]{:S(2)}) collective-permute-start(bf16[5,32,256]{2,1,0:T(8,128)(2,1)S(1)} %draft_step.9), channel_id=1, source_target_pairs={{0,0},{128,1},{2,2},{130,3},{4,4},{132,5},{6,6},{134,7},{8,8},{136... | collective-permute-start | bytes 245768 | tf_op jit(solution)/shard_map/ppermute | solution.py:46
  (71 shorter events, 34.5 us)
Async XLA Ops:
  7.2 42.4 %copy-start = (bf16[1024,256]{1,0:T(8,128)(2,1)S(1)}, bf16[1024,256]{1,0:T(8,128)(2,1)}, u32[]{:S(2)}) copy-start(bf16[1024,256]{1,0:T(8,128)(2,1)} %param.18) | copy-start | bytes 1572868
  7.2 15.9 %copy-start.4 = (bf16[8,6,128]{2,0,1:T(8,128)(2,1)S(1)}, bf16[8,6,128]{2,0,1:T(8,128)(2,1)}, u32[]{:S(2)}) copy-start(bf16[8,6,128]{2,0,1:T(8,128)(2,1)} %param.12) | copy-start | bytes 36868
  7.2 18.1 %copy-start.2 = (bf16[8,256,128]{2,1,0:T(8,128)(2,1)S(1)}, bf16[8,256,128]{2,1,0:T(8,128)(2,1)}, u32[]{:S(2)}) copy-start(bf16[8,256,128]{2,1,0:T(8,128)(2,1)} %param.14) | copy-start | bytes 1572868
  7.2 17.9 %collective-permute-start.1 = (bf16[1024,256]{1,0:T(8,128)(2,1)}, bf16[1024,256]{1,0:T(8,128)(2,1)S(1)}, u32[]{:S(2)}, u32[]{:S(2)}) collective-permute-start(bf16[1024,256]{1,0:T(8,128)(2,1)} %param.19), channel_id=1, source_target_pairs={{1,0},{129,1},{3,2},{131,3},{5,4},{133,5},{7,6},{135,7},{9,8},{137... | collective-permute-start | bytes 1572872 | tf_op jit(solution)/shard_map/ppermute | solution.py:46
  10.5 14.5 %collective-permute-start = (bf16[1024,256]{1,0:T(8,128)(2,1)}, bf16[1024,256]{1,0:T(8,128)(2,1)S(1)}, u32[]{:S(2)}, u32[]{:S(2)}) collective-permute-start(bf16[1024,256]{1,0:T(8,128)(2,1)} %param.19), channel_id=1, source_target_pairs={{0,0},{128,1},{2,2},{130,3},{4,4},{132,5},{6,6},{134,7},{8,8},{136... | collective-permute-start | bytes 1572872 | tf_op jit(solution)/shard_map/ppermute | solution.py:46
  14.9 8.9 %all-to-all-start = ((s32[8,1,32]{2,1,0:T(1,128)}), s32[8,1,32]{2,1,0:T(1,128)S(1)}, u32[]{:S(2)}, u32[]{:S(2)}) async-start(s32[8,1,32]{2,1,0:T(1,128)} %broadcast_in_dim.83), calls=%async_computation | async-start | bytes 8192 | tf_op jit(solution)/shard_map/all_to_all | solution.py:17
  19.3 117.4 %all-gather.2.cloned.1.call-start = ((), (), s32[]{:S(2)}) async-start(), calls=%async_computation.9 | async-start | bytes 3244032 | tf_op jit(solution)/shard_map/all_gather | solution.py:225
  27.0 22.6 %all-to-all-start.1 = ((bf16[32,8,1024]{2,1,0:T(8,128)(2,1)}), bf16[32,8,1024]{2,1,0:T(8,128)(2,1)S(1)}, u32[]{:S(2)}, u32[]{:S(2)}) async-start(bf16[32,8,1024]{2,1,0:T(8,128)(2,1)} %broadcast_in_dim.87), calls=%async_computation.1 | async-start | bytes 1048576 | tf_op jit(solution)/shard_map/all_to_all | solution.py:17
  36.6 3.1 %copy-start.5 = (s32[32]{0:T(128)S(1)}, s32[32]{0:T(128)}, u32[]{:S(2)}) copy-start(s32[32]{0:T(128)} %param.16) | copy-start | bytes 388
  37.8 21.9 %copy-start.3 = (bf16[32,6,256]{2,0,1:T(8,128)(2,1)S(1)}, bf16[32,6,256]{2,0,1:T(8,128)(2,1)}, u32[]{:S(2)}) copy-start(bf16[32,6,256]{2,0,1:T(8,128)(2,1)} %param.17) | copy-start | bytes 294916
  37.9 22.7 %collective-permute-start.3 = (bf16[2048,256]{1,0:T(8,128)(2,1)S(1)}, bf16[2048,256]{1,0:T(8,128)(2,1)S(1)}, u32[]{:S(2)}, u32[]{:S(2)}) collective-permute-start(bf16[2048,256]{1,0:T(8,128)(2,1)S(1)} %pad_maximum_fusion.here_ref), channel_id=1, source_target_pairs={{2,0},{3,1},{4,2},{5,3},{6,4},{7,5},{0,6},{1,7},{10,8},{11,9},{12,... | collective-permute-start | bytes 3145736 | tf_op jit(solution)/shard_map/ppermute | solution.py:46
  39.7 22.9 %collective-permute-start.2 = (bf16[2048,256]{1,0:T(8,128)(2,1)S(1)}, bf16[2048,256]{1,0:T(8,128)(2,1)}, u32[]{:S(2)}, u32[]{:S(2)}) collective-permute-start(bf16[2048,256]{1,0:T(8,128)(2,1)S(1)} %pad_maximum_fusion.here_ref), channel_id=1, source_target_pairs={{6,0},{7,1},{0,2},{1,3},{2,4},{3,5},{4,6},{5,7},{14,8},{15,9},{8,1... | collective-permute-start | bytes 3145736 | tf_op jit(solution)/shard_map/ppermute | solution.py:46
  50.6 16.7 %all-to-all-start.2 = ((bf16[8,32,256]{2,1,0:T(8,128)(2,1)}), bf16[8,32,256]{2,1,0:T(8,128)(2,1)S(1)}, u32[]{:S(2)}, u32[]{:S(2)}) async-start(bf16[8,32,256]{2,1,0:T(8,128)(2,1)} %bitcast.19), calls=%async_computation.2 | async-start | bytes 262144 | tf_op jit(solution)/shard_map/all_to_all | solution.py:211
  67.3 6.6 %collective-permute-start.4 = (bf16[32,256]{1,0:T(8,128)(2,1)S(1)}, bf16[32,256]{1,0:T(8,128)(2,1)S(1)}, u32[]{:S(2)}, u32[]{:S(2)}) collective-permute-start(bf16[32,256]{1,0:T(8,128)(2,1)S(1)} %add_convert_fusion.1), channel_id=1, source_target_pairs={{0,0},{128,1},{2,2},{130,3},{4,4},{132,5},{6,6},{134,7},{8,8},{136... | collective-permute-start | bytes 49160 | tf_op jit(solution)/shard_map/ppermute | solution.py:46
  74.6 17.6 %all-to-all-start.3 = ((bf16[16,32,256]{2,1,0:T(8,128)(2,1)}), bf16[16,32,256]{2,1,0:T(8,128)(2,1)S(1)}, u32[]{:S(2)}, u32[]{:S(2)}) async-start(bf16[16,32,256]{2,1,0:T(8,128)(2,1)} %broadcast_in_dim.88), calls=%async_computation.3 | async-start | bytes 524288 | tf_op jit(solution)/shard_map/all_to_all | solution.py:234
  82.0 95.8 %reduce-scatter.2.cloned.1.call-start = ((), (), s32[]{:S(2)}) async-start(), calls=%async_computation.10 | async-start | bytes 1769472 | tf_op jit(solution)/shard_map/reduce_scatter | solution.py:247
  84.8 9.5 %collective-permute-start.7 = (bf16[1024,256]{1,0:T(8,128)(2,1)}, bf16[1024,256]{1,0:T(8,128)(2,1)S(1)}, u32[]{:S(2)}, u32[]{:S(2)}) collective-permute-start(bf16[1024,256]{1,0:T(8,128)(2,1)} %slice.15), channel_id=1, source_target_pairs={{2,0},{3,1},{4,2},{5,3},{6,4},{7,5},{0,6},{1,7},{10,8},{11,9},{12,... | collective-permute-start | bytes 1572872 | tf_op jit(solution)/shard_map/ppermute | solution.py:46
  84.8 11.0 %collective-permute-start.6 = (bf16[1024,256]{1,0:T(8,128)(2,1)}, bf16[1024,256]{1,0:T(8,128)(2,1)}, u32[]{:S(2)}, u32[]{:S(2)}) collective-permute-start(bf16[1024,256]{1,0:T(8,128)(2,1)} %slice.14), channel_id=1, source_target_pairs={{6,0},{7,1},{0,2},{1,3},{2,4},{3,5},{4,6},{5,7},{14,8},{15,9},{8,1... | collective-permute-start | bytes 1572872 | tf_op jit(solution)/shard_map/ppermute | solution.py:46
  92.3 3.6 %collective-permute-start.5 = (bf16[16,32,256]{2,1,0:T(8,128)(2,1)S(1)}, bf16[16,32,256]{2,1,0:T(8,128)(2,1)S(1)}, u32[]{:S(2)}, u32[]{:S(2)}) collective-permute-start(bf16[16,32,256]{2,1,0:T(8,128)(2,1)S(1)} %all-to-all-done.3.own_ref), channel_id=1, source_target_pairs={{1,0},{0,1},{3,2},{2,3},{5,4},{4,5},{7,6},{6,7},{9,8},{8,9},{11,10... | collective-permute-start | bytes 786440 | tf_op jit(solution)/shard_map/ppermute | solution.py:46
  114.3 1.5 collective-permute-start.8
  131.4 3.1 %collective-permute-start.9 = (bf16[16,32,256]{2,1,0:T(8,128)(2,1)S(1)}, bf16[16,32,256]{2,1,0:T(8,128)(2,1)S(1)}, u32[]{:S(2)}, u32[]{:S(2)}) collective-permute-start(bf16[16,32,256]{2,1,0:T(8,128)(2,1)S(1)} %all_to_all.42.own_ref), channel_id=1, source_target_pairs={{1,0},{0,1},{3,2},{2,3},{5,4},{4,5},{7,6},{6,7},{9,8},{8,9},{11,10... | collective-permute-start | bytes 786440 | tf_op jit(solution)/shard_map/ppermute | solution.py:46
  153.8 3.3 %collective-permute-start.10 = (bf16[16,32,256]{2,1,0:T(8,128)(2,1)S(1)}, bf16[16,32,256]{2,1,0:T(8,128)(2,1)S(1)}, u32[]{:S(2)}, u32[]{:S(2)}) collective-permute-start(bf16[16,32,256]{2,1,0:T(8,128)(2,1)S(1)} %all_to_all.43.own_ref), channel_id=1, source_target_pairs={{1,0},{0,1},{3,2},{2,3},{5,4},{4,5},{7,6},{6,7},{9,8},{8,9},{11,10... | collective-permute-start | bytes 786440 | tf_op jit(solution)/shard_map/ppermute | solution.py:46
  172.3 3.4 %collective-permute-start.11 = (bf16[16,32,256]{2,1,0:T(8,128)(2,1)S(1)}, bf16[16,32,256]{2,1,0:T(8,128)(2,1)S(1)}, u32[]{:S(2)}, u32[]{:S(2)}) collective-permute-start(bf16[16,32,256]{2,1,0:T(8,128)(2,1)S(1)} %all_to_all.44.own_ref), channel_id=1, source_target_pairs={{1,0},{0,1},{3,2},{2,3},{5,4},{4,5},{7,6},{6,7},{9,8},{8,9},{11,10... | collective-permute-start | bytes 786440 | tf_op jit(solution)/shard_map/ppermute | solution.py:46
  178.8 7.5 %collective-permute-start.12 = (bf16[5,32,256]{2,1,0:T(8,128)(2,1)S(1)}, bf16[5,32,256]{2,1,0:T(8,128)(2,1)S(1)}, u32[]{:S(2)}, u32[]{:S(2)}) collective-permute-start(bf16[5,32,256]{2,1,0:T(8,128)(2,1)S(1)} %draft_step.9), channel_id=1, source_target_pairs={{0,0},{128,1},{2,2},{130,3},{4,4},{132,5},{6,6},{134,7},{8,8},{136... | collective-permute-start | bytes 245768 | tf_op jit(solution)/shard_map/ppermute | solution.py:46
  (1 other events, 1.9 us)
Sparse Core Ops, SparseCore 0:
  26.3 81.0 all-gather.1
  140.9 29.5 reduce-scatter.1

commit v4 on v3

--- a/solution.py
+++ b/solution.py
@@ -9,7 +9,7 @@
 
 HD = 128
 STEPS = 5
-HOLD = 2
+HOLD = 1
 
 
 def spread(block, axis):
@@ -46,30 +46,30 @@
     return lax.ppermute(block, ("dp", "tensor"), pairs)
 
 
-def draft_kernel(own_ref, other_ref, here_ref, left_ref, right_ref, low_ref, high_ref, *refs, last, to_hbm):
+def exchange_copies(copies):
+    return lax.all_to_all(
+        copies, "dp", split_axis=0, concat_axis=0, tiled=True, axis_index_groups=BLOCKS
+    )
+
+
+def draft_kernel(own_ref, other_ref, *refs, last):
     place = lax.axis_index("tensor")
     x, c = place // C, lax.rem(place, C)
     count, height, cols = own_ref.shape
+    weight_refs, refs = refs[: 2 * X], refs[2 * X :]
     if last:
         *earlier_refs, stack_ref, rows_ref = refs
-    elif to_hbm:
-        drafted_ref, copies_hbm_ref, rows_ref, copies_ref, sem = refs
     else:
-        drafted_ref, copies_ref, rows_ref = refs
+        drafted_ref, copies_ref, *kept_refs, rows_ref = refs
     for k in range(count):
         rows_ref[c * count + k] = own_ref[k]
         rows_ref[(1 - c) * count + k] = other_ref[k]
     total = jnp.zeros((height, cols), jnp.float32)
     per_x = rows_ref.shape[0] // X
     half = per_x // 2
-    for offset, shift, weight_ref in (
-        (0, 0, here_ref),
-        (X - 1, 0, left_ref),
-        (1, 0, right_ref),
-        (2, 0, low_ref),
-        (2, half, high_ref),
-    ):
-        first = lax.rem(x + offset, X) * per_x + shift
+    for piece, weight_ref in enumerate(weight_refs):
+        offset = (0, X - 1, 1, 2)[piece // 2]
+        first = lax.rem(x + offset, X) * per_x + piece % 2 * half
         wide = jnp.concatenate(
             [rows_ref[first + k] for k in range(weight_ref.shape[0] // cols)], axis=1
         )
@@ -83,13 +83,11 @@
     drafted_ref[...] = drafted
     for copy in range(count):
         copies_ref[copy] = drafted
-    if to_hbm:
-        send = pltpu.make_async_copy(copies_ref, copies_hbm_ref, sem)
-        send.start()
-        send.wait()
-
-
-def draft_step(own, other, weights, earlier, last, to_hbm):
+    for kept_ref, weight_ref in zip(kept_refs, weight_refs[X:]):
+        kept_ref[...] = weight_ref[...]
+
+
+def draft_step(own, other, weights, earlier, last, keep):
     count, height, cols = own.shape
     vmem = pl.BlockSpec(memory_space=pltpu.VMEM)
     rows = pltpu.VMEM((2 * count, height, cols), own.dtype)
@@ -101,17 +99,16 @@
         out_specs, scratch = vmem, [rows]
     else:
         operands = (own, other, *weights)
-        out_shape, out_specs, scratch = (block, copies), (vmem, vmem), [rows]
-        if to_hbm:
-            out_specs = (vmem, pl.BlockSpec(memory_space=pltpu.HBM))
-            scratch = [rows, pltpu.VMEM(own.shape, own.dtype), pltpu.SemaphoreType.DMA]
+        kept = [jax.ShapeDtypeStruct(piece.shape, piece.dtype) for piece in weights[X:]]
+        out_shape, scratch = [block, copies] + (kept if keep else []), [rows]
+        out_specs = [vmem] * len(out_shape)
     return pl.pallas_call(
-        functools.partial(draft_kernel, last=last, to_hbm=to_hbm),
+        functools.partial(draft_kernel, last=last),
         out_shape=out_shape,
         in_specs=[vmem] * len(operands),
         out_specs=out_specs,
         scratch_shapes=scratch,
-        compiler_params=pltpu.CompilerParams(vmem_limit_bytes=24 << 20),
+        compiler_params=pltpu.CompilerParams(vmem_limit_bytes=8 << 20),
         cost_estimate=pl.CostEstimate(
             flops=4 * count * height * cols * cols,
             bytes_accessed=4 * count * cols * cols + 6 * count * height * cols,
@@ -198,14 +195,11 @@
 
     picked = pick(attended, own_accepted)
     low_half = lax.axis_index("dp") < YL * Z
-    here = jnp.concatenate(
-        [
-            jnp.where(low_half, swapped, swapped_other),
-            jnp.where(low_half, swapped_other, swapped),
-        ]
-    )
-    left, right = move(here, FROM_LEFT), move(here, FROM_RIGHT)
+    top = jnp.where(low_half, swapped, swapped_other)
+    bottom = jnp.where(low_half, swapped_other, swapped)
+    top_left, bottom_right = move(top, FROM_LEFT), move(bottom, FROM_RIGHT)
     picked_rows = spread(picked, "dp").reshape(-1, query_width)
+    bottom_left, top_right = move(bottom, FROM_LEFT), move(top, FROM_RIGHT)
     picked_part = jnp.dot(picked_rows, out_weight, preferred_element_type=jnp.float32)
     block_windows, block_tokens, block_cols = residual.shape
     shares = lax.all_to_all(
@@ -215,9 +209,13 @@
         concat_axis=0,
         tiled=True,
     )
-    shares, left, right = lax.optimization_barrier((shares, left, right))
-    low = move(left[: left.shape[0] // 2], FROM_LEFT)
-    high = move(right[right.shape[0] // 2 :], FROM_RIGHT)
+    shares, top_left, bottom_left, top_right, bottom_right = lax.optimization_barrier(
+        (shares, top_left, bottom_left, top_right, bottom_right)
+    )
+    top_across, bottom_across = move(top_left, FROM_LEFT), move(bottom_right, FROM_RIGHT)
+    weights = (
+        top, bottom, top_left, bottom_left, top_right, bottom_right, top_across, bottom_across
+    )
     current = (
         pick(residual, accepted).astype(jnp.float32) + jnp.sum(shares.astype(jnp.float32), axis=0)
     ).astype(jnp.bfloat16)
@@ -228,21 +226,20 @@
 
     current = move(current, SWAPPED)
     copies = jnp.broadcast_to(current[None], (len(BLOCKS[0]),) + current.shape)
-    weights = (here, left, right, low, high)
     results = []
     for step in range(STEPS):
-        own = lax.all_to_all(
-            copies, "dp", split_axis=0, concat_axis=0, tiled=True, axis_index_groups=BLOCKS
-        )
+        own = exchange_copies(copies)
+        if step == HOLD:
+            gathered, own = lax.optimization_barrier((gathered, own))
         other = move(own, OTHER_CORE)
         last = step + 1 == STEPS
         drafted = draft_step(own, other, weights, results, last, step == HOLD)
         if last:
             break
-        drafted, copies = drafted
+        drafted, copies, *kept = drafted
+        if kept:
+            weights = (*weights[:X], *kept)
         results.append(drafted)
-        if step == HOLD:
-            gathered, copies = lax.optimization_barrier((gathered, copies))
     partial_out = jnp.dot(gathered, out_weight, preferred_element_type=jnp.float32)
     summed = lax.psum_scatter(partial_out, "tensor", scatter_dimension=0, tiled=True)
     drafted, summed = lax.optimization_barrier((drafted, summed))

time: 195 us -> 190 us (0.974)
  waiting for transfers between devices: 35.4 us -> 31.3 us
  Pallas kernels: 11.1 us -> 7.11 us
  starting transfers between devices: 57.1 us -> 60.5 us
  local copies, waits for them, and re-layouts: 9.08 us -> 6.37 us
    pallas_call x5, Pallas kernels: 11.1 us -> 7.11 us  [draft_step(): pl.pallas_call(functools.partial(draft_kernel, last=last), out_shape=out_...]
    ppermute x13 -> x15, waiting for transfers between devices: 14.2 us -> 11.3 us  [move(): return lax.ppermute(block, ('dp', 'tensor'), pairs)]
    all_to_all x2, waiting for transfers between devices: 10.4 us -> 7.56 us  [spread(): return lax.all_to_all(copies, axis, split_axis=0, concat_axis=0, tiled=True)]
    slice x2 -> x0, local copies, waits for them, and re-layouts: 2.71 us -> none  [the longest x1 1.87 us: per_device(): low = move(left[:left.shape[0] // 2], FROM_LEFT)]
    ppermute x13 -> x15, starting transfers between devices: 26.6 us -> 29 us  [move(): return lax.ppermute(block, ('dp', 'tensor'), pairs)]
    all_to_all x1, waiting for transfers between devices: 5.99 us -> 8.16 us  [exchange_copies(): lax.all_to_all(copies, 'dp', split_axis=0, concat_axis=0, tiled=True, axi...]
  transfers between devices with their start and end apart: 19 -> 21, of which waited for: 14 -> 12; matrix products, arithmetic and copies ran while one was open for 7% -> 6% of each run, Pallas kernels for 6% -> 4%
where the time goes in v4:
time: 190 us; the launch traced here: 189 us
  starting transfers between devices  60.5 us (32%)
  blocking collectives  57.3 us (30%)
  waiting for transfers between devices  31.3 us (16%)
  between operations  14.3 us (8%)
  matrix products  9.68 us (5%)
  Pallas kernels  7.11 us (4%)
  local copies, waits for them, and re-layouts  6.37 us (3%)
  other arithmetic  2.3 us (1%)
    all_to_all x4, blocking collectives, exchange_copies(): lax.all_to_all(copies, 'dp', split_axis=0, concat_axis=0, tiled=True, axi...  57.3 us
    ppermute x15, starting transfers between devices, move(): return lax.ppermute(block, ('dp', 'tensor'), pairs)  29 us
    all_to_all x2, starting transfers between devices, spread(): return lax.all_to_all(copies, axis, split_axis=0, concat_axis=0, tiled=True)  13.9 us
    ppermute x15, waiting for transfers between devices, move(): return lax.ppermute(block, ('dp', 'tensor'), pairs)  11.3 us
    all_to_all x1, starting transfers between devices, per_device(): lax.all_to_all(picked_part.astype(jnp.bfloat16).reshape(tensor_size, bloc...  10.2 us
    all_to_all x1, waiting for transfers between devices, exchange_copies(): lax.all_to_all(copies, 'dp', split_axis=0, concat_axis=0, tiled=True, axi...  8.16 us
    all_to_all x2, waiting for transfers between devices, spread(): return lax.all_to_all(copies, axis, split_axis=0, concat_axis=0, tiled=True)  7.56 us
    all_to_all x1, starting transfers between devices, exchange_copies(): lax.all_to_all(copies, 'dp', split_axis=0, concat_axis=0, tiled=True, axi...  7.26 us
  transfers between devices with their start and end apart: 21, of which 12 were waited for; matrix products, arithmetic and copies ran while one was open for 6% of the time, Pallas kernels for 4%

profile of v4, /device:TPU:1, one launch (start us, length us, event | category | flops | bytes accessed | tf_op | source)
XLA Modules:
  0.0 188.9 jit_solution(12556932940881737946)
XLA Ops:
  7.2 3.3 %collective-permute-start.1 = (bf16[1024,256]{1,0:T(8,128)(2,1)}, bf16[1024,256]{1,0:T(8,128)(2,1)S(1)}, u32[]{:S(2)}, u32[]{:S(2)}) collective-permute-start(bf16[1024,256]{1,0:T(8,128)(2,1)} %param.19), channel_id=1, source_target_pairs={{1,0},{129,1},{3,2},{131,3},{5,4},{133,5},{7,6},{135,7},{9,8},{137... | collective-permute-start | bytes 1572872 | tf_op jit(solution)/shard_map/ppermute | solution.py:46
  10.5 3.1 %collective-permute-start = (bf16[1024,256]{1,0:T(8,128)(2,1)}, bf16[1024,256]{1,0:T(8,128)(2,1)S(1)}, u32[]{:S(2)}, u32[]{:S(2)}) collective-permute-start(bf16[1024,256]{1,0:T(8,128)(2,1)} %param.19), channel_id=1, source_target_pairs={{0,0},{128,1},{2,2},{130,3},{4,4},{132,5},{6,6},{134,7},{8,8},{136... | collective-permute-start | bytes 1572872 | tf_op jit(solution)/shard_map/ppermute | solution.py:46
  14.9 4.4 %all-to-all-start = ((s32[8,1,32]{2,1,0:T(1,128)}), s32[8,1,32]{2,1,0:T(1,128)S(1)}, u32[]{:S(2)}, u32[]{:S(2)}) async-start(s32[8,1,32]{2,1,0:T(1,128)} %broadcast_in_dim.83), calls=%async_computation | async-start | bytes 8192 | tf_op jit(solution)/shard_map/all_to_all | solution.py:17
  27.2 9.5 %all-to-all-start.1 = ((bf16[32,8,1024]{2,1,0:T(8,128)(2,1)}), bf16[32,8,1024]{2,1,0:T(8,128)(2,1)}, u32[]{:S(2)}, u32[]{:S(2)}) async-start(bf16[32,8,1024]{2,1,0:T(8,128)(2,1)} %broadcast_in_dim.87), calls=%async_computation.1 | async-start | bytes 1048576 | tf_op jit(solution)/shard_map/all_to_all | solution.py:17
  36.9 2.6 %collective-permute-start.5 = (bf16[1024,256]{1,0:T(8,128)(2,1)S(1)}, bf16[1024,256]{1,0:T(8,128)(2,1)S(1)}, u32[]{:S(2)}, u32[]{:S(2)}) collective-permute-start(bf16[1024,256]{1,0:T(8,128)(2,1)S(1)} %get-tuple-element.52.refs_1_), channel_id=1, source_target_pairs={{2,0},{3,1},{4,2},{5,3},{6,4},{7,5},{0,6},{1,7},{10,8},{11,9},{12,... | collective-permute-start | bytes 1572872 | tf_op jit(solution)/shard_map/ppermute | solution.py:46
  39.4 2.7 %collective-permute-start.4 = (bf16[1024,256]{1,0:T(8,128)(2,1)S(1)}, bf16[1024,256]{1,0:T(8,128)(2,1)}, u32[]{:S(2)}, u32[]{:S(2)}) collective-permute-start(bf16[1024,256]{1,0:T(8,128)(2,1)S(1)} %get-tuple-element.53.refs_0_), channel_id=1, source_target_pairs={{2,0},{3,1},{4,2},{5,3},{6,4},{7,5},{0,6},{1,7},{10,8},{11,9},{12,... | collective-permute-start | bytes 1572872 | tf_op jit(solution)/shard_map/ppermute | solution.py:46
  42.1 7.6 %all-to-all-done.1 = bf16[32,8,1024]{2,1,0:T(8,128)(2,1)} async-done(((bf16[32,8,1024]{2,1,0:T(8,128)(2,1)}), bf16[32,8,1024]{2,1,0:T(8,128)(2,1)}, u32[]{:S(2)}, u32[]{:S(2)}) %all-to-all-start.1) | async-done | bytes 524320 | tf_op jit(solution)/shard_map/all_to_all | solution.py:17
  51.7 10.2 %all-to-all-start.2 = ((bf16[8,32,256]{2,1,0:T(8,128)(2,1)}), bf16[8,32,256]{2,1,0:T(8,128)(2,1)S(1)}, u32[]{:S(2)}, u32[]{:S(2)}) async-start(bf16[8,32,256]{2,1,0:T(8,128)(2,1)} %bitcast.19), calls=%async_computation.2 | async-start | bytes 262144 | tf_op jit(solution)/shard_map/all_to_all | solution.py:205
  62.9 4.2 %all-to-all-done.2 = bf16[8,32,256]{2,1,0:T(8,128)(2,1)S(1)} async-done(((bf16[8,32,256]{2,1,0:T(8,128)(2,1)}), bf16[8,32,256]{2,1,0:T(8,128)(2,1)S(1)}, u32[]{:S(2)}, u32[]{:S(2)}) %all-to-all-start.2) | async-done | bytes 131104 | tf_op jit(solution)/shard_map/all_to_all | solution.py:205
  67.2 5.1 %collective-permute-start.6 = (bf16[32,256]{1,0:T(8,128)(2,1)S(1)}, bf16[32,256]{1,0:T(8,128)(2,1)S(1)}, u32[]{:S(2)}, u32[]{:S(2)}) collective-permute-start(bf16[32,256]{1,0:T(8,128)(2,1)S(1)} %add_convert_fusion.1), channel_id=1, source_target_pairs={{0,0},{128,1},{2,2},{130,3},{4,4},{132,5},{6,6},{134,7},{8,8},{136... | collective-permute-start | bytes 49160 | tf_op jit(solution)/shard_map/ppermute | solution.py:46
  74.5 7.3 %all-to-all-start.3 = ((bf16[16,32,256]{2,1,0:T(8,128)(2,1)}), bf16[16,32,256]{2,1,0:T(8,128)(2,1)S(1)}, u32[]{:S(2)}, u32[]{:S(2)}) async-start(bf16[16,32,256]{2,1,0:T(8,128)(2,1)} %broadcast_in_dim.88), calls=%async_computation.3 | async-start | bytes 524288 | tf_op jit(solution)/shard_map/all_to_all | solution.py:50
  83.4 8.2 %all-to-all-done.3.own_ref = bf16[16,32,256]{2,1,0:T(8,128)(2,1)S(1)} async-done(((bf16[16,32,256]{2,1,0:T(8,128)(2,1)}), bf16[16,32,256]{2,1,0:T(8,128)(2,1)S(1)}, u32[]{:S(2)}, u32[]{:S(2)}) %all-to-all-start.3) | async-done | bytes 262176 | tf_op jit(solution)/shard_map/all_to_all | solution.py:50
  93.0 2.3 %draft_step.5 = (bf16[32,256]{1,0:T(8,128)(2,1)S(1)}, bf16[16,32,256]{2,1,0:T(8,128)(2,1)S(1)}) custom-call(bf16[16,32,256]{2,1,0:T(8,128)(2,1)S(1)} %all-to-all-done.3.own_ref, bf16[16,32,256]{2,1,0:T(8,128)(2,1)S(1)} %collective-permute-done.7.other_ref, bf16[1024,256]{1,0:T(8,128)(2,1)S(1)} %get-tuple-element.53.refs_0_, ...), custom_call_target="tpu_custom_call" | custom-call | flops 134217728 | bytes 4980736 | tf_op jit(solution)/shard_map/draft_step/pallas_call | solution.py:105
  95.3 18.3 %all_to_all.41.own_ref = bf16[16,32,256]{2,1,0:T(8,128)(2,1)S(1)} all-to-all(bf16[16,32,256]{2,1,0:T(8,128)(2,1)S(1)} %get-tuple-element.34), channel_id=1, replica_groups={{0,8,16,24,32,40,48,56,64,72,80,88,96,104,112,120},{128,136,144,152,160..., dimensions={0} | all-to-all | bytes 524288 | tf_op jit(solution)/shard_map/all_to_all | solution.py:50
  113.6 4.0 %fusion.19 = f32[1536,256]{1,0:T(8,128)} fusion(bf16[1536,1024]{1,0:T(8,128)(2,1)} %all-gather.2.cloned.1.call-done, bf16[1024,256]{1,0:T(8,128)(2,1)S(1)} %copy-done), kind=kOutput, calls=%fused_computation.42 | convolution fusion | flops 805306368 | bytes 5242880 | tf_op jit(solution)/shard_map/dot_general | solution.py:243
  119.3 2.3 %draft_step.6 = (bf16[32,256]{1,0:T(8,128)(2,1)S(1)}, bf16[16,32,256]{2,1,0:T(8,128)(2,1)S(1)}, bf16[1024,256]{1,0:T(8,128)(2,1)S(1)}, bf16[1024,256]{1,0:T(8,12...) custom-call(bf16[16,32,256]{2,1,0:T(8,128)(2,1)S(1)} %all_to_all.41.own_ref, ...), custom_call_target="tpu_custom_call" | custom-call | flops 134217728 | bytes 4980736 | tf_op jit(solution)/shard_map/draft_step/pallas_call | solution.py:105
  121.6 13.1 %all_to_all.42.own_ref = bf16[16,32,256]{2,1,0:T(8,128)(2,1)S(1)} all-to-all(bf16[16,32,256]{2,1,0:T(8,128)(2,1)S(1)} %get-tuple-element.36), channel_id=1, replica_groups={{0,8,16,24,32,40,48,56,64,72,80,88,96,104,112,120},{128,136,144,152,160..., dimensions={0} | all-to-all | bytes 524288 | tf_op jit(solution)/shard_map/all_to_all | solution.py:50
  134.8 2.2 %collective-permute-start.11 = (bf16[16,32,256]{2,1,0:T(8,128)(2,1)S(1)}, bf16[16,32,256]{2,1,0:T(8,128)(2,1)S(1)}, u32[]{:S(2)}, u32[]{:S(2)}) collective-permute-start(bf16[16,32,256]{2,1,0:T(8,128)(2,1)S(1)} %all_to_all.42.own_ref), channel_id=1, source_target_pairs={{1,0},{0,1},{3,2},{2,3},{5,4},{4,5},{7,6},{6,7},{9,8},{8,9},{11,10... | collective-permute-start | bytes 786440 | tf_op jit(solution)/shard_map/ppermute | solution.py:46
  139.0 12.9 %all_to_all.43.own_ref = bf16[16,32,256]{2,1,0:T(8,128)(2,1)S(1)} all-to-all(bf16[16,32,256]{2,1,0:T(8,128)(2,1)S(1)} %get-tuple-element.41), channel_id=1, replica_groups={{0,8,16,24,32,40,48,56,64,72,80,88,96,104,112,120},{128,136,144,152,160..., dimensions={0} | all-to-all | bytes 524288 | tf_op jit(solution)/shard_map/all_to_all | solution.py:50
  151.9 2.2 %collective-permute-start.12 = (bf16[16,32,256]{2,1,0:T(8,128)(2,1)S(1)}, bf16[16,32,256]{2,1,0:T(8,128)(2,1)S(1)}, u32[]{:S(2)}, u32[]{:S(2)}) collective-permute-start(bf16[16,32,256]{2,1,0:T(8,128)(2,1)S(1)} %all_to_all.43.own_ref), channel_id=1, source_target_pairs={{1,0},{0,1},{3,2},{2,3},{5,4},{4,5},{7,6},{6,7},{9,8},{8,9},{11,10... | collective-permute-start | bytes 786440 | tf_op jit(solution)/shard_map/ppermute | solution.py:46
  156.1 12.9 %all_to_all.44.own_ref = bf16[16,32,256]{2,1,0:T(8,128)(2,1)S(1)} all-to-all(bf16[16,32,256]{2,1,0:T(8,128)(2,1)S(1)} %get-tuple-element.42), channel_id=1, replica_groups={{0,8,16,24,32,40,48,56,64,72,80,88,96,104,112,120},{128,136,144,152,160..., dimensions={0} | all-to-all | bytes 524288 | tf_op jit(solution)/shard_map/all_to_all | solution.py:50
  169.0 2.2 %collective-permute-start.13 = (bf16[16,32,256]{2,1,0:T(8,128)(2,1)S(1)}, bf16[16,32,256]{2,1,0:T(8,128)(2,1)S(1)}, u32[]{:S(2)}, u32[]{:S(2)}) collective-permute-start(bf16[16,32,256]{2,1,0:T(8,128)(2,1)S(1)} %all_to_all.44.own_ref), channel_id=1, source_target_pairs={{1,0},{0,1},{3,2},{2,3},{5,4},{4,5},{7,6},{6,7},{9,8},{8,9},{11,10... | collective-permute-start | bytes 786440 | tf_op jit(solution)/shard_map/ppermute | solution.py:46
  174.2 4.1 %collective-permute-start.14 = (bf16[5,32,256]{2,1,0:T(8,128)(2,1)S(1)}, bf16[5,32,256]{2,1,0:T(8,128)(2,1)S(1)}, u32[]{:S(2)}, u32[]{:S(2)}) collective-permute-start(bf16[5,32,256]{2,1,0:T(8,128)(2,1)S(1)} %draft_step.9), channel_id=1, source_target_pairs={{0,0},{128,1},{2,2},{130,3},{4,4},{132,5},{6,6},{134,7},{8,8},{136... | collective-permute-start | bytes 245768 | tf_op jit(solution)/shard_map/ppermute | solution.py:46
  179.1 2.4 %collective-permute-done.14 = bf16[5,32,256]{2,1,0:T(8,128)(2,1)S(1)} collective-permute-done((bf16[5,32,256]{2,1,0:T(8,128)(2,1)S(1)}, bf16[5,32,256]{2,1,0:T(8,128)(2,1)S(1)}, u32[]{:S(2)}, u32[]{:S(2)}) %collective-permute-start.14) | collective-permute-done | bytes 81952 | tf_op jit(solution)/shard_map/ppermute | solution.py:46
  (68 shorter events, 27.5 us)
Async XLA Ops:
  7.2 42.5 %copy-start = (bf16[1024,256]{1,0:T(8,128)(2,1)S(1)}, bf16[1024,256]{1,0:T(8,128)(2,1)}, u32[]{:S(2)}) copy-start(bf16[1024,256]{1,0:T(8,128)(2,1)} %param.18) | copy-start | bytes 1572868
  7.2 18.2 %copy-start.1 = (bf16[8,256,128]{2,1,0:T(8,128)(2,1)S(1)}, bf16[8,256,128]{2,1,0:T(8,128)(2,1)}, u32[]{:S(2)}) copy-start(bf16[8,256,128]{2,1,0:T(8,128)(2,1)} %param.14) | copy-start | bytes 1572868
  7.2 18.1 %collective-permute-start.1 = (bf16[1024,256]{1,0:T(8,128)(2,1)}, bf16[1024,256]{1,0:T(8,128)(2,1)S(1)}, u32[]{:S(2)}, u32[]{:S(2)}) collective-permute-start(bf16[1024,256]{1,0:T(8,128)(2,1)} %param.19), channel_id=1, source_target_pairs={{1,0},{129,1},{3,2},{131,3},{5,4},{133,5},{7,6},{135,7},{9,8},{137... | collective-permute-start | bytes 1572872 | tf_op jit(solution)/shard_map/ppermute | solution.py:46
  10.5 14.7 %collective-permute-start = (bf16[1024,256]{1,0:T(8,128)(2,1)}, bf16[1024,256]{1,0:T(8,128)(2,1)S(1)}, u32[]{:S(2)}, u32[]{:S(2)}) collective-permute-start(bf16[1024,256]{1,0:T(8,128)(2,1)} %param.19), channel_id=1, source_target_pairs={{0,0},{128,1},{2,2},{130,3},{4,4},{132,5},{6,6},{134,7},{8,8},{136... | collective-permute-start | bytes 1572872 | tf_op jit(solution)/shard_map/ppermute | solution.py:46
  14.9 9.1 %all-to-all-start = ((s32[8,1,32]{2,1,0:T(1,128)}), s32[8,1,32]{2,1,0:T(1,128)S(1)}, u32[]{:S(2)}, u32[]{:S(2)}) async-start(s32[8,1,32]{2,1,0:T(1,128)} %broadcast_in_dim.83), calls=%async_computation | async-start | bytes 8192 | tf_op jit(solution)/shard_map/all_to_all | solution.py:17
  19.3 94.3 %all-gather.2.cloned.1.call-start = ((), (), s32[]{:S(2)}) async-start(), calls=%async_computation.9 | async-start | bytes 3244032 | tf_op jit(solution)/shard_map/all_gather | solution.py:223
  25.4 36.5 %copy-start.2 = (bf16[32,6,256]{2,0,1:T(8,128)(2,1)S(1)}, bf16[32,6,256]{2,0,1:T(8,128)(2,1)}, u32[]{:S(2)}) copy-start(bf16[32,6,256]{2,0,1:T(8,128)(2,1)} %param.17) | copy-start | bytes 294916
  27.2 22.5 %all-to-all-start.1 = ((bf16[32,8,1024]{2,1,0:T(8,128)(2,1)}), bf16[32,8,1024]{2,1,0:T(8,128)(2,1)}, u32[]{:S(2)}, u32[]{:S(2)}) async-start(bf16[32,8,1024]{2,1,0:T(8,128)(2,1)} %broadcast_in_dim.87), calls=%async_computation.1 | async-start | bytes 1048576 | tf_op jit(solution)/shard_map/all_to_all | solution.py:17
  36.9 25.1 %collective-permute-start.5 = (bf16[1024,256]{1,0:T(8,128)(2,1)S(1)}, bf16[1024,256]{1,0:T(8,128)(2,1)S(1)}, u32[]{:S(2)}, u32[]{:S(2)}) collective-permute-start(bf16[1024,256]{1,0:T(8,128)(2,1)S(1)} %get-tuple-element.52.refs_1_), channel_id=1, source_target_pairs={{2,0},{3,1},{4,2},{5,3},{6,4},{7,5},{0,6},{1,7},{10,8},{11,9},{12,... | collective-permute-start | bytes 1572872 | tf_op jit(solution)/shard_map/ppermute | solution.py:46
  39.4 22.6 %collective-permute-start.3 = (bf16[1024,256]{1,0:T(8,128)(2,1)S(1)}, bf16[1024,256]{1,0:T(8,128)(2,1)S(1)}, u32[]{:S(2)}, u32[]{:S(2)}) collective-permute-start(bf16[1024,256]{1,0:T(8,128)(2,1)S(1)} %get-tuple-element.52.refs_1_), channel_id=1, source_target_pairs={{6,0},{7,1},{0,2},{1,3},{2,4},{3,5},{4,6},{5,7},{14,8},{15,9},{8,1... | collective-permute-start | bytes 1572872 | tf_op jit(solution)/shard_map/ppermute | solution.py:46
  39.4 22.6 %collective-permute-start.4 = (bf16[1024,256]{1,0:T(8,128)(2,1)S(1)}, bf16[1024,256]{1,0:T(8,128)(2,1)}, u32[]{:S(2)}, u32[]{:S(2)}) collective-permute-start(bf16[1024,256]{1,0:T(8,128)(2,1)S(1)} %get-tuple-element.53.refs_0_), channel_id=1, source_target_pairs={{2,0},{3,1},{4,2},{5,3},{6,4},{7,5},{0,6},{1,7},{10,8},{11,9},{12,... | collective-permute-start | bytes 1572872 | tf_op jit(solution)/shard_map/ppermute | solution.py:46
  42.1 20.8 %collective-permute-start.2 = (bf16[1024,256]{1,0:T(8,128)(2,1)S(1)}, bf16[1024,256]{1,0:T(8,128)(2,1)S(1)}, u32[]{:S(2)}, u32[]{:S(2)}) collective-permute-start(bf16[1024,256]{1,0:T(8,128)(2,1)S(1)} %get-tuple-element.53.refs_0_), channel_id=1, source_target_pairs={{6,0},{7,1},{0,2},{1,3},{2,4},{3,5},{4,6},{5,7},{14,8},{15,9},{8,1... | collective-permute-start | bytes 1572872 | tf_op jit(solution)/shard_map/ppermute | solution.py:46
  51.7 15.5 %all-to-all-start.2 = ((bf16[8,32,256]{2,1,0:T(8,128)(2,1)}), bf16[8,32,256]{2,1,0:T(8,128)(2,1)S(1)}, u32[]{:S(2)}, u32[]{:S(2)}) async-start(bf16[8,32,256]{2,1,0:T(8,128)(2,1)} %bitcast.19), calls=%async_computation.2 | async-start | bytes 262144 | tf_op jit(solution)/shard_map/all_to_all | solution.py:205
  67.2 6.6 %collective-permute-start.6 = (bf16[32,256]{1,0:T(8,128)(2,1)S(1)}, bf16[32,256]{1,0:T(8,128)(2,1)S(1)}, u32[]{:S(2)}, u32[]{:S(2)}) collective-permute-start(bf16[32,256]{1,0:T(8,128)(2,1)S(1)} %add_convert_fusion.1), channel_id=1, source_target_pairs={{0,0},{128,1},{2,2},{130,3},{4,4},{132,5},{6,6},{134,7},{8,8},{136... | collective-permute-start | bytes 49160 | tf_op jit(solution)/shard_map/ppermute | solution.py:46
  74.5 17.0 %all-to-all-start.3 = ((bf16[16,32,256]{2,1,0:T(8,128)(2,1)}), bf16[16,32,256]{2,1,0:T(8,128)(2,1)S(1)}, u32[]{:S(2)}, u32[]{:S(2)}) async-start(bf16[16,32,256]{2,1,0:T(8,128)(2,1)} %broadcast_in_dim.88), calls=%async_computation.3 | async-start | bytes 524288 | tf_op jit(solution)/shard_map/all_to_all | solution.py:50
  81.8 91.4 %reduce-scatter.2.cloned.1.call-start = ((), (), s32[]{:S(2)}) async-start(), calls=%async_computation.10 | async-start | bytes 1769472 | tf_op jit(solution)/shard_map/reduce_scatter | solution.py:244
  81.8 9.7 %collective-permute-start.9 = (bf16[1024,256]{1,0:T(8,128)(2,1)S(1)}, bf16[1024,256]{1,0:T(8,128)(2,1)}, u32[]{:S(2)}, u32[]{:S(2)}) collective-permute-start(bf16[1024,256]{1,0:T(8,128)(2,1)S(1)} %collective-permute-done.5.refs_5_), channel_id=1, source_target_pairs={{2,0},{3,1},{4,2},{5,3},{6,4},{7,5},{0,6},{1,7},{10,8},{11,9},{12,... | collective-permute-start | bytes 1572872 | tf_op jit(solution)/shard_map/ppermute | solution.py:46
  81.9 10.8 %collective-permute-start.8 = (bf16[1024,256]{1,0:T(8,128)(2,1)S(1)}, bf16[1024,256]{1,0:T(8,128)(2,1)}, u32[]{:S(2)}, u32[]{:S(2)}) collective-permute-start(bf16[1024,256]{1,0:T(8,128)(2,1)S(1)} %collective-permute-done.2.refs_2_), channel_id=1, source_target_pairs={{6,0},{7,1},{0,2},{1,3},{2,4},{3,5},{4,6},{5,7},{14,8},{15,9},{8,1... | collective-permute-start | bytes 1572872 | tf_op jit(solution)/shard_map/ppermute | solution.py:46
  91.5 1.5 collective-permute-start.7
  117.7 1.6 collective-permute-start.10
  134.8 3.3 %collective-permute-start.11 = (bf16[16,32,256]{2,1,0:T(8,128)(2,1)S(1)}, bf16[16,32,256]{2,1,0:T(8,128)(2,1)S(1)}, u32[]{:S(2)}, u32[]{:S(2)}) collective-permute-start(bf16[16,32,256]{2,1,0:T(8,128)(2,1)S(1)} %all_to_all.42.own_ref), channel_id=1, source_target_pairs={{1,0},{0,1},{3,2},{2,3},{5,4},{4,5},{7,6},{6,7},{9,8},{8,9},{11,10... | collective-permute-start | bytes 786440 | tf_op jit(solution)/shard_map/ppermute | solution.py:46
  151.9 3.3 %collective-permute-start.12 = (bf16[16,32,256]{2,1,0:T(8,128)(2,1)S(1)}, bf16[16,32,256]{2,1,0:T(8,128)(2,1)S(1)}, u32[]{:S(2)}, u32[]{:S(2)}) collective-permute-start(bf16[16,32,256]{2,1,0:T(8,128)(2,1)S(1)} %all_to_all.43.own_ref), channel_id=1, source_target_pairs={{1,0},{0,1},{3,2},{2,3},{5,4},{4,5},{7,6},{6,7},{9,8},{8,9},{11,10... | collective-permute-start | bytes 786440 | tf_op jit(solution)/shard_map/ppermute | solution.py:46
  169.0 3.3 %collective-permute-start.13 = (bf16[16,32,256]{2,1,0:T(8,128)(2,1)S(1)}, bf16[16,32,256]{2,1,0:T(8,128)(2,1)S(1)}, u32[]{:S(2)}, u32[]{:S(2)}) collective-permute-start(bf16[16,32,256]{2,1,0:T(8,128)(2,1)S(1)} %all_to_all.44.own_ref), channel_id=1, source_target_pairs={{1,0},{0,1},{3,2},{2,3},{5,4},{4,5},{7,6},{6,7},{9,8},{8,9},{11,10... | collective-permute-start | bytes 786440 | tf_op jit(solution)/shard_map/ppermute | solution.py:46
  174.2 7.3 %collective-permute-start.14 = (bf16[5,32,256]{2,1,0:T(8,128)(2,1)S(1)}, bf16[5,32,256]{2,1,0:T(8,128)(2,1)S(1)}, u32[]{:S(2)}, u32[]{:S(2)}) collective-permute-start(bf16[5,32,256]{2,1,0:T(8,128)(2,1)S(1)} %draft_step.9), channel_id=1, source_target_pairs={{0,0},{128,1},{2,2},{130,3},{4,4},{132,5},{6,6},{134,7},{8,8},{136... | collective-permute-start | bytes 245768 | tf_op jit(solution)/shard_map/ppermute | solution.py:46
  (1 other events, 16.7 us)
Sparse Core Ops, SparseCore 0:
  26.4 82.8 all-gather.1
  117.8 30.1 reduce-scatter.1

commit v5 on v4

--- a/solution.py
+++ b/solution.py
@@ -118,9 +118,26 @@
     )(*operands)
 
 
-def accepted_of_my_windows(everyone):
-    rows = everyone.shape[0] // lax.axis_size("dp")
-    return lax.dynamic_slice_in_dim(everyone, lax.axis_index("dp") * rows, rows, 0)
+def near_holders():
+    pairs = []
+    for yh in range(YH):
+        for yl in range(YL):
+            for z in range(Z):
+                for x in range(X):
+                    for c in range(C):
+                        y = yh * YL + yl
+                        near = (z // X * X + 2 * (z % X) - 2 + c) % Z
+                        source = ((x * Z + near) * X + y) * C + z // X
+                        pairs.append((source, ((y * Z + z) * X + x) * C + c))
+    return pairs
+
+
+NEAR_HOLDER = near_holders()
+
+
+def accepted_of_my_windows(block, rows):
+    start = lax.axis_index("dp") * rows % block.shape[0]
+    return lax.dynamic_slice_in_dim(block, start, rows, 0)
 
 
 def pick(rows, accepted):
@@ -147,14 +164,14 @@
     kv_here = new_keys.shape[2] // HD
     group_size = query_width // HD // kv_here
     tensor_size = lax.axis_size("tensor")
-    everyone, swapped, swapped_other = lax.optimization_barrier(
+    holder_block, swapped, swapped_other = lax.optimization_barrier(
         (
-            spread(accepted, "tensor").reshape(-1),
+            move(accepted, NEAR_HOLDER),
             move(draft_weight, SWAPPED),
             move(draft_weight, SWAPPED_OTHER),
         )
     )
-    own_accepted = accepted_of_my_windows(everyone)
+    own_accepted = accepted_of_my_windows(holder_block, windows_here)
 
     query_split = queries.reshape(windows_here, tokens_here, kv_here, group_size, HD)
     keys_cached = key_cache.reshape(windows_here, cache_size, kv_here, HD)

time: 190 us -> 189 us (level)
  starting transfers between devices: 60.5 us -> 63.4 us
    ppermute x15 -> x16, starting transfers between devices: 29 us -> 36.9 us  [move(): return lax.ppermute(block, ('dp', 'tensor'), pairs)]
    all_to_all x2 -> x1, starting transfers between devices: 13.9 us -> 8.73 us  [spread(): return lax.all_to_all(copies, axis, split_axis=0, concat_axis=0, tiled=True)]
    ppermute x15 -> x16, waiting for transfers between devices: 11.3 us -> 10.2 us  [move(): return lax.ppermute(block, ('dp', 'tensor'), pairs)]
    all_to_all x2 -> x1, waiting for transfers between devices: 7.56 us -> 6.74 us  [spread(): return lax.all_to_all(copies, axis, split_axis=0, concat_axis=0, tiled=True)]
  transfers between devices with their start and end apart: 21 -> 21, of which waited for: 12 -> 12; matrix products, arithmetic and copies ran while one was open for 6% -> 5% of each run, Pallas kernels for 4% -> 4%
where the time goes in v5:
time: 189 us; the launch traced here: 188 us
  starting transfers between devices  63.4 us (34%)
  blocking collectives  58.2 us (31%)
  waiting for transfers between devices  29.8 us (16%)
  between operations  14.4 us (8%)
  matrix products  8.99 us (5%)
  Pallas kernels  7.12 us (4%)
  local copies, waits for them, and re-layouts  4.51 us (2%)
    all_to_all x4, blocking collectives, exchange_copies(): lax.all_to_all(copies, 'dp', split_axis=0, concat_axis=0, tiled=True, axi...  58.2 us
    ppermute x16, starting transfers between devices, move(): return lax.ppermute(block, ('dp', 'tensor'), pairs)  36.9 us
    all_to_all x1, starting transfers between devices, per_device(): lax.all_to_all(picked_part.astype(jnp.bfloat16).reshape(tensor_size, bloc...  10.4 us
    ppermute x16, waiting for transfers between devices, move(): return lax.ppermute(block, ('dp', 'tensor'), pairs)  10.2 us
    all_to_all x1, starting transfers between devices, spread(): return lax.all_to_all(copies, axis, split_axis=0, concat_axis=0, tiled=True)  8.73 us
    all_to_all x1, waiting for transfers between devices, exchange_copies(): lax.all_to_all(copies, 'dp', split_axis=0, concat_axis=0, tiled=True, axi...  7.68 us
    all_to_all x1, starting transfers between devices, exchange_copies(): lax.all_to_all(copies, 'dp', split_axis=0, concat_axis=0, tiled=True, axi...  7.29 us
    pallas_call x5, Pallas kernels, draft_step(): pl.pallas_call(functools.partial(draft_kernel, last=last), out_shape=out_...  7.12 us
  transfers between devices with their start and end apart: 21, of which 12 were waited for; matrix products, arithmetic and copies ran while one was open for 5% of the time, Pallas kernels for 4%

profile of v5, /device:TPU:1, one launch (start us, length us, event | category | flops | bytes accessed | tf_op | source)
XLA Modules:
  0.0 188.0 jit_solution(11338659671596157972)
XLA Ops:
  7.2 3.3 %collective-permute-start.2 = (bf16[1024,256]{1,0:T(8,128)(2,1)}, bf16[1024,256]{1,0:T(8,128)(2,1)S(1)}, u32[]{:S(2)}, u32[]{:S(2)}) collective-permute-start(bf16[1024,256]{1,0:T(8,128)(2,1)} %param.19), channel_id=1, source_target_pairs={{1,0},{129,1},{3,2},{131,3},{5,4},{133,5},{7,6},{135,7},{9,8},{137... | collective-permute-start | bytes 1572872 | tf_op jit(solution)/shard_map/ppermute | solution.py:46
  10.6 3.1 %collective-permute-start.1 = (bf16[1024,256]{1,0:T(8,128)(2,1)}, bf16[1024,256]{1,0:T(8,128)(2,1)S(1)}, u32[]{:S(2)}, u32[]{:S(2)}) collective-permute-start(bf16[1024,256]{1,0:T(8,128)(2,1)} %param.19), channel_id=1, source_target_pairs={{0,0},{128,1},{2,2},{130,3},{4,4},{132,5},{6,6},{134,7},{8,8},{136... | collective-permute-start | bytes 1572872 | tf_op jit(solution)/shard_map/ppermute | solution.py:46
  13.7 7.4 %collective-permute-start = (s32[32]{0:T(128)}, s32[32]{0:T(128)S(1)}, u32[]{:S(2)}, u32[]{:S(2)}) collective-permute-start(s32[32]{0:T(128)} %param.16), channel_id=1, source_target_pairs={{48,0},{56,1},{112,2},{120,3},{176,4},{184,5},{240,6},{248,7},{0,8... | collective-permute-start | bytes 392 | tf_op jit(solution)/shard_map/ppermute | solution.py:46
  27.0 8.7 %all-to-all-start = ((bf16[32,8,1024]{2,1,0:T(8,128)(2,1)}), bf16[32,8,1024]{2,1,0:T(8,128)(2,1)}, u32[]{:S(2)}, u32[]{:S(2)}) async-start(bf16[32,8,1024]{2,1,0:T(8,128)(2,1)} %broadcast_in_dim.80), calls=%async_computation | async-start | bytes 1048576 | tf_op jit(solution)/shard_map/all_to_all | solution.py:17
  35.9 2.3 %collective-permute-start.6 = (bf16[1024,256]{1,0:T(8,128)(2,1)S(1)}, bf16[1024,256]{1,0:T(8,128)(2,1)S(1)}, u32[]{:S(2)}, u32[]{:S(2)}) collective-permute-start(bf16[1024,256]{1,0:T(8,128)(2,1)S(1)} %get-tuple-element.52.refs_1_), channel_id=1, source_target_pairs={{2,0},{3,1},{4,2},{5,3},{6,4},{7,5},{0,6},{1,7},{10,8},{11,9},{12,... | collective-permute-start | bytes 1572872 | tf_op jit(solution)/shard_map/ppermute | solution.py:46
  38.2 2.7 %collective-permute-start.5 = (bf16[1024,256]{1,0:T(8,128)(2,1)S(1)}, bf16[1024,256]{1,0:T(8,128)(2,1)}, u32[]{:S(2)}, u32[]{:S(2)}) collective-permute-start(bf16[1024,256]{1,0:T(8,128)(2,1)S(1)} %get-tuple-element.53.refs_0_), channel_id=1, source_target_pairs={{2,0},{3,1},{4,2},{5,3},{6,4},{7,5},{0,6},{1,7},{10,8},{11,9},{12,... | collective-permute-start | bytes 1572872 | tf_op jit(solution)/shard_map/ppermute | solution.py:46
  40.8 6.7 %all-to-all-done = bf16[32,8,1024]{2,1,0:T(8,128)(2,1)} async-done(((bf16[32,8,1024]{2,1,0:T(8,128)(2,1)}), bf16[32,8,1024]{2,1,0:T(8,128)(2,1)}, u32[]{:S(2)}, u32[]{:S(2)}) %all-to-all-start) | async-done | bytes 524320 | tf_op jit(solution)/shard_map/all_to_all | solution.py:17
  49.6 10.4 %all-to-all-start.1 = ((bf16[8,32,256]{2,1,0:T(8,128)(2,1)}), bf16[8,32,256]{2,1,0:T(8,128)(2,1)S(1)}, u32[]{:S(2)}, u32[]{:S(2)}) async-start(bf16[8,32,256]{2,1,0:T(8,128)(2,1)} %bitcast.19), calls=%async_computation.1 | async-start | bytes 262144 | tf_op jit(solution)/shard_map/all_to_all | solution.py:222
  60.3 5.1 %all-to-all-done.1 = bf16[8,32,256]{2,1,0:T(8,128)(2,1)S(1)} async-done(((bf16[8,32,256]{2,1,0:T(8,128)(2,1)}), bf16[8,32,256]{2,1,0:T(8,128)(2,1)S(1)}, u32[]{:S(2)}, u32[]{:S(2)}) %all-to-all-start.1) | async-done | bytes 131104 | tf_op jit(solution)/shard_map/all_to_all | solution.py:222
  65.5 5.4 %collective-permute-start.7 = (bf16[32,256]{1,0:T(8,128)(2,1)S(1)}, bf16[32,256]{1,0:T(8,128)(2,1)S(1)}, u32[]{:S(2)}, u32[]{:S(2)}) collective-permute-start(bf16[32,256]{1,0:T(8,128)(2,1)S(1)} %add_convert_fusion.1), channel_id=1, source_target_pairs={{0,0},{128,1},{2,2},{130,3},{4,4},{132,5},{6,6},{134,7},{8,8},{136... | collective-permute-start | bytes 49160 | tf_op jit(solution)/shard_map/ppermute | solution.py:46
  73.0 7.3 %all-to-all-start.2 = ((bf16[16,32,256]{2,1,0:T(8,128)(2,1)}), bf16[16,32,256]{2,1,0:T(8,128)(2,1)S(1)}, u32[]{:S(2)}, u32[]{:S(2)}) async-start(bf16[16,32,256]{2,1,0:T(8,128)(2,1)} %broadcast_in_dim.81), calls=%async_computation.2 | async-start | bytes 524288 | tf_op jit(solution)/shard_map/all_to_all | solution.py:50
  81.9 7.7 %all-to-all-done.2.own_ref = bf16[16,32,256]{2,1,0:T(8,128)(2,1)S(1)} async-done(((bf16[16,32,256]{2,1,0:T(8,128)(2,1)}), bf16[16,32,256]{2,1,0:T(8,128)(2,1)S(1)}, u32[]{:S(2)}, u32[]{:S(2)}) %all-to-all-start.2) | async-done | bytes 262176 | tf_op jit(solution)/shard_map/all_to_all | solution.py:50
  91.3 2.3 %draft_step.5 = (bf16[32,256]{1,0:T(8,128)(2,1)S(1)}, bf16[16,32,256]{2,1,0:T(8,128)(2,1)S(1)}) custom-call(bf16[16,32,256]{2,1,0:T(8,128)(2,1)S(1)} %all-to-all-done.2.own_ref, bf16[16,32,256]{2,1,0:T(8,128)(2,1)S(1)} %collective-permute-done.8.other_ref, bf16[1024,256]{1,0:T(8,128)(2,1)S(1)} %get-tuple-element.53.refs_0_, ...), custom_call_target="tpu_custom_call" | custom-call | flops 134217728 | bytes 4980736 | tf_op jit(solution)/shard_map/draft_step/pallas_call | solution.py:105
  93.5 18.6 %all_to_all.35.own_ref = bf16[16,32,256]{2,1,0:T(8,128)(2,1)S(1)} all-to-all(bf16[16,32,256]{2,1,0:T(8,128)(2,1)S(1)} %get-tuple-element.34), channel_id=1, replica_groups={{0,8,16,24,32,40,48,56,64,72,80,88,96,104,112,120},{128,136,144,152,160..., dimensions={0} | all-to-all | bytes 524288 | tf_op jit(solution)/shard_map/all_to_all | solution.py:50
  112.2 4.0 %fusion.19 = f32[1536,256]{1,0:T(8,128)} fusion(bf16[1536,1024]{1,0:T(8,128)(2,1)} %all-gather.2.cloned.1.call-done, bf16[1024,256]{1,0:T(8,128)(2,1)S(1)} %copy-done), kind=kOutput, calls=%fused_computation.42 | convolution fusion | flops 805306368 | bytes 5242880 | tf_op jit(solution)/shard_map/dot_general | solution.py:260
  117.8 2.3 %draft_step.6 = (bf16[32,256]{1,0:T(8,128)(2,1)S(1)}, bf16[16,32,256]{2,1,0:T(8,128)(2,1)S(1)}, bf16[1024,256]{1,0:T(8,128)(2,1)S(1)}, bf16[1024,256]{1,0:T(8,12...) custom-call(bf16[16,32,256]{2,1,0:T(8,128)(2,1)S(1)} %all_to_all.35.own_ref, ...), custom_call_target="tpu_custom_call" | custom-call | flops 134217728 | bytes 4980736 | tf_op jit(solution)/shard_map/draft_step/pallas_call | solution.py:105
  120.2 13.7 %all_to_all.36.own_ref = bf16[16,32,256]{2,1,0:T(8,128)(2,1)S(1)} all-to-all(bf16[16,32,256]{2,1,0:T(8,128)(2,1)S(1)} %get-tuple-element.36), channel_id=1, replica_groups={{0,8,16,24,32,40,48,56,64,72,80,88,96,104,112,120},{128,136,144,152,160..., dimensions={0} | all-to-all | bytes 524288 | tf_op jit(solution)/shard_map/all_to_all | solution.py:50
  133.9 2.2 %collective-permute-start.12 = (bf16[16,32,256]{2,1,0:T(8,128)(2,1)S(1)}, bf16[16,32,256]{2,1,0:T(8,128)(2,1)S(1)}, u32[]{:S(2)}, u32[]{:S(2)}) collective-permute-start(bf16[16,32,256]{2,1,0:T(8,128)(2,1)S(1)} %all_to_all.36.own_ref), channel_id=1, source_target_pairs={{1,0},{0,1},{3,2},{2,3},{5,4},{4,5},{7,6},{6,7},{9,8},{8,9},{11,10... | collective-permute-start | bytes 786440 | tf_op jit(solution)/shard_map/ppermute | solution.py:46
  138.1 13.0 %all_to_all.37.own_ref = bf16[16,32,256]{2,1,0:T(8,128)(2,1)S(1)} all-to-all(bf16[16,32,256]{2,1,0:T(8,128)(2,1)S(1)} %get-tuple-element.41), channel_id=1, replica_groups={{0,8,16,24,32,40,48,56,64,72,80,88,96,104,112,120},{128,136,144,152,160..., dimensions={0} | all-to-all | bytes 524288 | tf_op jit(solution)/shard_map/all_to_all | solution.py:50
  151.0 2.2 %collective-permute-start.13 = (bf16[16,32,256]{2,1,0:T(8,128)(2,1)S(1)}, bf16[16,32,256]{2,1,0:T(8,128)(2,1)S(1)}, u32[]{:S(2)}, u32[]{:S(2)}) collective-permute-start(bf16[16,32,256]{2,1,0:T(8,128)(2,1)S(1)} %all_to_all.37.own_ref), channel_id=1, source_target_pairs={{1,0},{0,1},{3,2},{2,3},{5,4},{4,5},{7,6},{6,7},{9,8},{8,9},{11,10... | collective-permute-start | bytes 786440 | tf_op jit(solution)/shard_map/ppermute | solution.py:46
  155.2 12.9 %all_to_all.38.own_ref = bf16[16,32,256]{2,1,0:T(8,128)(2,1)S(1)} all-to-all(bf16[16,32,256]{2,1,0:T(8,128)(2,1)S(1)} %get-tuple-element.42), channel_id=1, replica_groups={{0,8,16,24,32,40,48,56,64,72,80,88,96,104,112,120},{128,136,144,152,160..., dimensions={0} | all-to-all | bytes 524288 | tf_op jit(solution)/shard_map/all_to_all | solution.py:50
  168.1 2.2 %collective-permute-start.14 = (bf16[16,32,256]{2,1,0:T(8,128)(2,1)S(1)}, bf16[16,32,256]{2,1,0:T(8,128)(2,1)S(1)}, u32[]{:S(2)}, u32[]{:S(2)}) collective-permute-start(bf16[16,32,256]{2,1,0:T(8,128)(2,1)S(1)} %all_to_all.38.own_ref), channel_id=1, source_target_pairs={{1,0},{0,1},{3,2},{2,3},{5,4},{4,5},{7,6},{6,7},{9,8},{8,9},{11,10... | collective-permute-start | bytes 786440 | tf_op jit(solution)/shard_map/ppermute | solution.py:46
  173.3 4.2 %collective-permute-start.15 = (bf16[5,32,256]{2,1,0:T(8,128)(2,1)S(1)}, bf16[5,32,256]{2,1,0:T(8,128)(2,1)S(1)}, u32[]{:S(2)}, u32[]{:S(2)}) collective-permute-start(bf16[5,32,256]{2,1,0:T(8,128)(2,1)S(1)} %draft_step.9), channel_id=1, source_target_pairs={{0,0},{128,1},{2,2},{130,3},{4,4},{132,5},{6,6},{134,7},{8,8},{136... | collective-permute-start | bytes 245768 | tf_op jit(solution)/shard_map/ppermute | solution.py:46
  178.3 2.3 %collective-permute-done.15 = bf16[5,32,256]{2,1,0:T(8,128)(2,1)S(1)} collective-permute-done((bf16[5,32,256]{2,1,0:T(8,128)(2,1)S(1)}, bf16[5,32,256]{2,1,0:T(8,128)(2,1)S(1)}, u32[]{:S(2)}, u32[]{:S(2)}) %collective-permute-start.15) | collective-permute-done | bytes 81952 | tf_op jit(solution)/shard_map/ppermute | solution.py:46
  (66 shorter events, 23.7 us)
Async XLA Ops:
  7.2 40.4 %copy-start = (bf16[1024,256]{1,0:T(8,128)(2,1)S(1)}, bf16[1024,256]{1,0:T(8,128)(2,1)}, u32[]{:S(2)}) copy-start(bf16[1024,256]{1,0:T(8,128)(2,1)} %param.18) | copy-start | bytes 1572868
  7.2 18.1 %copy-start.1 = (bf16[8,256,128]{2,1,0:T(8,128)(2,1)S(1)}, bf16[8,256,128]{2,1,0:T(8,128)(2,1)}, u32[]{:S(2)}) copy-start(bf16[8,256,128]{2,1,0:T(8,128)(2,1)} %param.14) | copy-start | bytes 1572868
  7.2 105.0 %all-gather.2.cloned.1.call-start = ((), (), s32[]{:S(2)}) async-start(), calls=%async_computation.8 | async-start | bytes 3244032 | tf_op jit(solution)/shard_map/all_gather | solution.py:240
  7.2 17.9 %collective-permute-start.2 = (bf16[1024,256]{1,0:T(8,128)(2,1)}, bf16[1024,256]{1,0:T(8,128)(2,1)S(1)}, u32[]{:S(2)}, u32[]{:S(2)}) collective-permute-start(bf16[1024,256]{1,0:T(8,128)(2,1)} %param.19), channel_id=1, source_target_pairs={{1,0},{129,1},{3,2},{131,3},{5,4},{133,5},{7,6},{135,7},{9,8},{137... | collective-permute-start | bytes 1572872 | tf_op jit(solution)/shard_map/ppermute | solution.py:46
  10.6 14.5 %collective-permute-start.1 = (bf16[1024,256]{1,0:T(8,128)(2,1)}, bf16[1024,256]{1,0:T(8,128)(2,1)S(1)}, u32[]{:S(2)}, u32[]{:S(2)}) collective-permute-start(bf16[1024,256]{1,0:T(8,128)(2,1)} %param.19), channel_id=1, source_target_pairs={{0,0},{128,1},{2,2},{130,3},{4,4},{132,5},{6,6},{134,7},{8,8},{136... | collective-permute-start | bytes 1572872 | tf_op jit(solution)/shard_map/ppermute | solution.py:46
  13.7 11.4 %collective-permute-start = (s32[32]{0:T(128)}, s32[32]{0:T(128)S(1)}, u32[]{:S(2)}, u32[]{:S(2)}) collective-permute-start(s32[32]{0:T(128)} %param.16), channel_id=1, source_target_pairs={{48,0},{56,1},{112,2},{120,3},{176,4},{184,5},{240,6},{248,7},{0,8... | collective-permute-start | bytes 392 | tf_op jit(solution)/shard_map/ppermute | solution.py:46
  25.3 34.8 %copy-start.2 = (bf16[32,6,256]{2,0,1:T(8,128)(2,1)S(1)}, bf16[32,6,256]{2,0,1:T(8,128)(2,1)}, u32[]{:S(2)}) copy-start(bf16[32,6,256]{2,0,1:T(8,128)(2,1)} %param.17) | copy-start | bytes 294916
  27.0 20.5 %all-to-all-start = ((bf16[32,8,1024]{2,1,0:T(8,128)(2,1)}), bf16[32,8,1024]{2,1,0:T(8,128)(2,1)}, u32[]{:S(2)}, u32[]{:S(2)}) async-start(bf16[32,8,1024]{2,1,0:T(8,128)(2,1)} %broadcast_in_dim.80), calls=%async_computation | async-start | bytes 1048576 | tf_op jit(solution)/shard_map/all_to_all | solution.py:17
  35.9 24.3 %collective-permute-start.6 = (bf16[1024,256]{1,0:T(8,128)(2,1)S(1)}, bf16[1024,256]{1,0:T(8,128)(2,1)S(1)}, u32[]{:S(2)}, u32[]{:S(2)}) collective-permute-start(bf16[1024,256]{1,0:T(8,128)(2,1)S(1)} %get-tuple-element.52.refs_1_), channel_id=1, source_target_pairs={{2,0},{3,1},{4,2},{5,3},{6,4},{7,5},{0,6},{1,7},{10,8},{11,9},{12,... | collective-permute-start | bytes 1572872 | tf_op jit(solution)/shard_map/ppermute | solution.py:46
  38.2 22.0 %collective-permute-start.4 = (bf16[1024,256]{1,0:T(8,128)(2,1)S(1)}, bf16[1024,256]{1,0:T(8,128)(2,1)S(1)}, u32[]{:S(2)}, u32[]{:S(2)}) collective-permute-start(bf16[1024,256]{1,0:T(8,128)(2,1)S(1)} %get-tuple-element.52.refs_1_), channel_id=1, source_target_pairs={{6,0},{7,1},{0,2},{1,3},{2,4},{3,5},{4,6},{5,7},{14,8},{15,9},{8,1... | collective-permute-start | bytes 1572872 | tf_op jit(solution)/shard_map/ppermute | solution.py:46
  38.2 22.0 %collective-permute-start.5 = (bf16[1024,256]{1,0:T(8,128)(2,1)S(1)}, bf16[1024,256]{1,0:T(8,128)(2,1)}, u32[]{:S(2)}, u32[]{:S(2)}) collective-permute-start(bf16[1024,256]{1,0:T(8,128)(2,1)S(1)} %get-tuple-element.53.refs_0_), channel_id=1, source_target_pairs={{2,0},{3,1},{4,2},{5,3},{6,4},{7,5},{0,6},{1,7},{10,8},{11,9},{12,... | collective-permute-start | bytes 1572872 | tf_op jit(solution)/shard_map/ppermute | solution.py:46
  40.8 19.5 %collective-permute-start.3 = (bf16[1024,256]{1,0:T(8,128)(2,1)S(1)}, bf16[1024,256]{1,0:T(8,128)(2,1)S(1)}, u32[]{:S(2)}, u32[]{:S(2)}) collective-permute-start(bf16[1024,256]{1,0:T(8,128)(2,1)S(1)} %get-tuple-element.53.refs_0_), channel_id=1, source_target_pairs={{6,0},{7,1},{0,2},{1,3},{2,4},{3,5},{4,6},{5,7},{14,8},{15,9},{8,1... | collective-permute-start | bytes 1572872 | tf_op jit(solution)/shard_map/ppermute | solution.py:46
  49.6 15.8 %all-to-all-start.1 = ((bf16[8,32,256]{2,1,0:T(8,128)(2,1)}), bf16[8,32,256]{2,1,0:T(8,128)(2,1)S(1)}, u32[]{:S(2)}, u32[]{:S(2)}) async-start(bf16[8,32,256]{2,1,0:T(8,128)(2,1)} %bitcast.19), calls=%async_computation.1 | async-start | bytes 262144 | tf_op jit(solution)/shard_map/all_to_all | solution.py:222
  65.5 6.8 %collective-permute-start.7 = (bf16[32,256]{1,0:T(8,128)(2,1)S(1)}, bf16[32,256]{1,0:T(8,128)(2,1)S(1)}, u32[]{:S(2)}, u32[]{:S(2)}) collective-permute-start(bf16[32,256]{1,0:T(8,128)(2,1)S(1)} %add_convert_fusion.1), channel_id=1, source_target_pairs={{0,0},{128,1},{2,2},{130,3},{4,4},{132,5},{6,6},{134,7},{8,8},{136... | collective-permute-start | bytes 49160 | tf_op jit(solution)/shard_map/ppermute | solution.py:46
  73.0 16.6 %all-to-all-start.2 = ((bf16[16,32,256]{2,1,0:T(8,128)(2,1)}), bf16[16,32,256]{2,1,0:T(8,128)(2,1)S(1)}, u32[]{:S(2)}, u32[]{:S(2)}) async-start(bf16[16,32,256]{2,1,0:T(8,128)(2,1)} %broadcast_in_dim.81), calls=%async_computation.2 | async-start | bytes 524288 | tf_op jit(solution)/shard_map/all_to_all | solution.py:50
  80.3 92.0 %reduce-scatter.2.cloned.1.call-start = ((), (), s32[]{:S(2)}) async-start(), calls=%async_computation.9 | async-start | bytes 1769472 | tf_op jit(solution)/shard_map/reduce_scatter | solution.py:261
  80.3 9.7 %collective-permute-start.10 = (bf16[1024,256]{1,0:T(8,128)(2,1)S(1)}, bf16[1024,256]{1,0:T(8,128)(2,1)}, u32[]{:S(2)}, u32[]{:S(2)}) collective-permute-start(bf16[1024,256]{1,0:T(8,128)(2,1)S(1)} %collective-permute-done.6.refs_5_), channel_id=1, source_target_pairs={{2,0},{3,1},{4,2},{5,3},{6,4},{7,5},{0,6},{1,7},{10,8},{11,9},{12,... | collective-permute-start | bytes 1572872 | tf_op jit(solution)/shard_map/ppermute | solution.py:46
  80.5 10.7 %collective-permute-start.9 = (bf16[1024,256]{1,0:T(8,128)(2,1)S(1)}, bf16[1024,256]{1,0:T(8,128)(2,1)}, u32[]{:S(2)}, u32[]{:S(2)}) collective-permute-start(bf16[1024,256]{1,0:T(8,128)(2,1)S(1)} %collective-permute-done.3.refs_2_), channel_id=1, source_target_pairs={{6,0},{7,1},{0,2},{1,3},{2,4},{3,5},{4,6},{5,7},{14,8},{15,9},{8,1... | collective-permute-start | bytes 1572872 | tf_op jit(solution)/shard_map/ppermute | solution.py:46
  89.6 1.7 collective-permute-start.8
  116.2 1.6 collective-permute-start.11
  133.9 3.3 %collective-permute-start.12 = (bf16[16,32,256]{2,1,0:T(8,128)(2,1)S(1)}, bf16[16,32,256]{2,1,0:T(8,128)(2,1)S(1)}, u32[]{:S(2)}, u32[]{:S(2)}) collective-permute-start(bf16[16,32,256]{2,1,0:T(8,128)(2,1)S(1)} %all_to_all.36.own_ref), channel_id=1, source_target_pairs={{1,0},{0,1},{3,2},{2,3},{5,4},{4,5},{7,6},{6,7},{9,8},{8,9},{11,10... | collective-permute-start | bytes 786440 | tf_op jit(solution)/shard_map/ppermute | solution.py:46
  151.0 3.3 %collective-permute-start.13 = (bf16[16,32,256]{2,1,0:T(8,128)(2,1)S(1)}, bf16[16,32,256]{2,1,0:T(8,128)(2,1)S(1)}, u32[]{:S(2)}, u32[]{:S(2)}) collective-permute-start(bf16[16,32,256]{2,1,0:T(8,128)(2,1)S(1)} %all_to_all.37.own_ref), channel_id=1, source_target_pairs={{1,0},{0,1},{3,2},{2,3},{5,4},{4,5},{7,6},{6,7},{9,8},{8,9},{11,10... | collective-permute-start | bytes 786440 | tf_op jit(solution)/shard_map/ppermute | solution.py:46
  168.1 3.3 %collective-permute-start.14 = (bf16[16,32,256]{2,1,0:T(8,128)(2,1)S(1)}, bf16[16,32,256]{2,1,0:T(8,128)(2,1)S(1)}, u32[]{:S(2)}, u32[]{:S(2)}) collective-permute-start(bf16[16,32,256]{2,1,0:T(8,128)(2,1)S(1)} %all_to_all.38.own_ref), channel_id=1, source_target_pairs={{1,0},{0,1},{3,2},{2,3},{5,4},{4,5},{7,6},{6,7},{9,8},{8,9},{11,10... | collective-permute-start | bytes 786440 | tf_op jit(solution)/shard_map/ppermute | solution.py:46
  173.3 7.3 %collective-permute-start.15 = (bf16[5,32,256]{2,1,0:T(8,128)(2,1)S(1)}, bf16[5,32,256]{2,1,0:T(8,128)(2,1)S(1)}, u32[]{:S(2)}, u32[]{:S(2)}) collective-permute-start(bf16[5,32,256]{2,1,0:T(8,128)(2,1)S(1)} %draft_step.9), channel_id=1, source_target_pairs={{0,0},{128,1},{2,2},{130,3},{4,4},{132,5},{6,6},{134,7},{8,8},{136... | collective-permute-start | bytes 245768 | tf_op jit(solution)/shard_map/ppermute | solution.py:46
  (2 other events, 31.7 us)
Sparse Core Ops, SparseCore 0:
  26.3 82.5 all-gather.1
  116.3 31.2 reduce-scatter.1

commit v6 on v5

--- a/solution.py
+++ b/solution.py
@@ -259,7 +259,6 @@
         results.append(drafted)
     partial_out = jnp.dot(gathered, out_weight, preferred_element_type=jnp.float32)
     summed = lax.psum_scatter(partial_out, "tensor", scatter_dimension=0, tiled=True)
-    drafted, summed = lax.optimization_barrier((drafted, summed))
     verified = (residual.astype(jnp.float32) + summed.reshape(residual.shape)).astype(jnp.bfloat16)
     return (verified, move(drafted, SWAPPED))
 

time: 189 us -> 190 us (level)
  transfers between devices with their start and end apart: 21 -> 21, of which waited for: 12 -> 12; matrix products, arithmetic and copies ran while one was open for 5% -> 4% of each run, Pallas kernels for 4% -> 4%
where the time goes in v6:
time: 190 us; the launch traced here: 189 us
  starting transfers between devices  63.4 us (33%)
  blocking collectives  58.2 us (31%)
  waiting for transfers between devices  30.5 us (16%)
  between operations  14.4 us (8%)
  matrix products  8.99 us (5%)
  Pallas kernels  7.12 us (4%)
  local copies, waits for them, and re-layouts  4.51 us (2%)
    all_to_all x4, blocking collectives, exchange_copies(): lax.all_to_all(copies, 'dp', split_axis=0, concat_axis=0, tiled=True, axi...  58.2 us
    ppermute x16, starting transfers between devices, move(): return lax.ppermute(block, ('dp', 'tensor'), pairs)  36.9 us
    ppermute x16, waiting for transfers between devices, move(): return lax.ppermute(block, ('dp', 'tensor'), pairs)  11 us
    all_to_all x1, starting transfers between devices, per_device(): lax.all_to_all(picked_part.astype(jnp.bfloat16).reshape(tensor_size, bloc...  10.4 us
    all_to_all x1, starting transfers between devices, spread(): return lax.all_to_all(copies, axis, split_axis=0, concat_axis=0, tiled=True)  8.73 us
    all_to_all x1, waiting for transfers between devices, exchange_copies(): lax.all_to_all(copies, 'dp', split_axis=0, concat_axis=0, tiled=True, axi...  7.68 us
    all_to_all x1, starting transfers between devices, exchange_copies(): lax.all_to_all(copies, 'dp', split_axis=0, concat_axis=0, tiled=True, axi...  7.29 us
    pallas_call x5, Pallas kernels, draft_step(): pl.pallas_call(functools.partial(draft_kernel, last=last), out_shape=out_...  7.12 us
  transfers between devices with their start and end apart: 21, of which 12 were waited for; matrix products, arithmetic and copies ran while one was open for 4% of the time, Pallas kernels for 4%

profile of v6, /device:TPU:1, one launch (start us, length us, event | category | flops | bytes accessed | tf_op | source)
XLA Modules:
  0.0 188.7 jit_solution(11493734789158414299)
XLA Ops:
  7.2 3.3 %collective-permute-start.2 = (bf16[1024,256]{1,0:T(8,128)(2,1)}, bf16[1024,256]{1,0:T(8,128)(2,1)S(1)}, u32[]{:S(2)}, u32[]{:S(2)}) collective-permute-start(bf16[1024,256]{1,0:T(8,128)(2,1)} %param.19), channel_id=1, source_target_pairs={{1,0},{129,1},{3,2},{131,3},{5,4},{133,5},{7,6},{135,7},{9,8},{137... | collective-permute-start | bytes 1572872 | tf_op jit(solution)/shard_map/ppermute | solution.py:46
  10.6 3.1 %collective-permute-start.1 = (bf16[1024,256]{1,0:T(8,128)(2,1)}, bf16[1024,256]{1,0:T(8,128)(2,1)S(1)}, u32[]{:S(2)}, u32[]{:S(2)}) collective-permute-start(bf16[1024,256]{1,0:T(8,128)(2,1)} %param.19), channel_id=1, source_target_pairs={{0,0},{128,1},{2,2},{130,3},{4,4},{132,5},{6,6},{134,7},{8,8},{136... | collective-permute-start | bytes 1572872 | tf_op jit(solution)/shard_map/ppermute | solution.py:46
  13.7 7.4 %collective-permute-start = (s32[32]{0:T(128)}, s32[32]{0:T(128)S(1)}, u32[]{:S(2)}, u32[]{:S(2)}) collective-permute-start(s32[32]{0:T(128)} %param.16), channel_id=1, source_target_pairs={{48,0},{56,1},{112,2},{120,3},{176,4},{184,5},{240,6},{248,7},{0,8... | collective-permute-start | bytes 392 | tf_op jit(solution)/shard_map/ppermute | solution.py:46
  27.0 8.7 %all-to-all-start = ((bf16[32,8,1024]{2,1,0:T(8,128)(2,1)}), bf16[32,8,1024]{2,1,0:T(8,128)(2,1)}, u32[]{:S(2)}, u32[]{:S(2)}) async-start(bf16[32,8,1024]{2,1,0:T(8,128)(2,1)} %broadcast_in_dim.80), calls=%async_computation | async-start | bytes 1048576 | tf_op jit(solution)/shard_map/all_to_all | solution.py:17
  35.9 2.3 %collective-permute-start.6 = (bf16[1024,256]{1,0:T(8,128)(2,1)S(1)}, bf16[1024,256]{1,0:T(8,128)(2,1)S(1)}, u32[]{:S(2)}, u32[]{:S(2)}) collective-permute-start(bf16[1024,256]{1,0:T(8,128)(2,1)S(1)} %get-tuple-element.48.refs_1_), channel_id=1, source_target_pairs={{2,0},{3,1},{4,2},{5,3},{6,4},{7,5},{0,6},{1,7},{10,8},{11,9},{12,... | collective-permute-start | bytes 1572872 | tf_op jit(solution)/shard_map/ppermute | solution.py:46
  38.2 2.7 %collective-permute-start.5 = (bf16[1024,256]{1,0:T(8,128)(2,1)S(1)}, bf16[1024,256]{1,0:T(8,128)(2,1)}, u32[]{:S(2)}, u32[]{:S(2)}) collective-permute-start(bf16[1024,256]{1,0:T(8,128)(2,1)S(1)} %get-tuple-element.49.refs_0_), channel_id=1, source_target_pairs={{2,0},{3,1},{4,2},{5,3},{6,4},{7,5},{0,6},{1,7},{10,8},{11,9},{12,... | collective-permute-start | bytes 1572872 | tf_op jit(solution)/shard_map/ppermute | solution.py:46
  40.8 6.7 %all-to-all-done = bf16[32,8,1024]{2,1,0:T(8,128)(2,1)} async-done(((bf16[32,8,1024]{2,1,0:T(8,128)(2,1)}), bf16[32,8,1024]{2,1,0:T(8,128)(2,1)}, u32[]{:S(2)}, u32[]{:S(2)}) %all-to-all-start) | async-done | bytes 524320 | tf_op jit(solution)/shard_map/all_to_all | solution.py:17
  49.6 10.4 %all-to-all-start.1 = ((bf16[8,32,256]{2,1,0:T(8,128)(2,1)}), bf16[8,32,256]{2,1,0:T(8,128)(2,1)S(1)}, u32[]{:S(2)}, u32[]{:S(2)}) async-start(bf16[8,32,256]{2,1,0:T(8,128)(2,1)} %bitcast.19), calls=%async_computation.1 | async-start | bytes 262144 | tf_op jit(solution)/shard_map/all_to_all | solution.py:222
  60.3 5.1 %all-to-all-done.1 = bf16[8,32,256]{2,1,0:T(8,128)(2,1)S(1)} async-done(((bf16[8,32,256]{2,1,0:T(8,128)(2,1)}), bf16[8,32,256]{2,1,0:T(8,128)(2,1)S(1)}, u32[]{:S(2)}, u32[]{:S(2)}) %all-to-all-start.1) | async-done | bytes 131104 | tf_op jit(solution)/shard_map/all_to_all | solution.py:222
  65.5 5.4 %collective-permute-start.7 = (bf16[32,256]{1,0:T(8,128)(2,1)S(1)}, bf16[32,256]{1,0:T(8,128)(2,1)S(1)}, u32[]{:S(2)}, u32[]{:S(2)}) collective-permute-start(bf16[32,256]{1,0:T(8,128)(2,1)S(1)} %add_convert_fusion.1), channel_id=1, source_target_pairs={{0,0},{128,1},{2,2},{130,3},{4,4},{132,5},{6,6},{134,7},{8,8},{136... | collective-permute-start | bytes 49160 | tf_op jit(solution)/shard_map/ppermute | solution.py:46
  73.0 7.3 %all-to-all-start.2 = ((bf16[16,32,256]{2,1,0:T(8,128)(2,1)}), bf16[16,32,256]{2,1,0:T(8,128)(2,1)S(1)}, u32[]{:S(2)}, u32[]{:S(2)}) async-start(bf16[16,32,256]{2,1,0:T(8,128)(2,1)} %broadcast_in_dim.81), calls=%async_computation.2 | async-start | bytes 524288 | tf_op jit(solution)/shard_map/all_to_all | solution.py:50
  81.9 7.7 %all-to-all-done.2.own_ref = bf16[16,32,256]{2,1,0:T(8,128)(2,1)S(1)} async-done(((bf16[16,32,256]{2,1,0:T(8,128)(2,1)}), bf16[16,32,256]{2,1,0:T(8,128)(2,1)S(1)}, u32[]{:S(2)}, u32[]{:S(2)}) %all-to-all-start.2) | async-done | bytes 262176 | tf_op jit(solution)/shard_map/all_to_all | solution.py:50
  91.3 2.3 %draft_step.5 = (bf16[32,256]{1,0:T(8,128)(2,1)S(1)}, bf16[16,32,256]{2,1,0:T(8,128)(2,1)S(1)}) custom-call(bf16[16,32,256]{2,1,0:T(8,128)(2,1)S(1)} %all-to-all-done.2.own_ref, bf16[16,32,256]{2,1,0:T(8,128)(2,1)S(1)} %collective-permute-done.8.other_ref, bf16[1024,256]{1,0:T(8,128)(2,1)S(1)} %get-tuple-element.49.refs_0_, ...), custom_call_target="tpu_custom_call" | custom-call | flops 134217728 | bytes 4980736 | tf_op jit(solution)/shard_map/draft_step/pallas_call | solution.py:105
  93.5 18.6 %all_to_all.35.own_ref = bf16[16,32,256]{2,1,0:T(8,128)(2,1)S(1)} all-to-all(bf16[16,32,256]{2,1,0:T(8,128)(2,1)S(1)} %get-tuple-element.32), channel_id=1, replica_groups={{0,8,16,24,32,40,48,56,64,72,80,88,96,104,112,120},{128,136,144,152,160..., dimensions={0} | all-to-all | bytes 524288 | tf_op jit(solution)/shard_map/all_to_all | solution.py:50
  112.2 4.0 %fusion.19 = f32[1536,256]{1,0:T(8,128)} fusion(bf16[1536,1024]{1,0:T(8,128)(2,1)} %all-gather.2.cloned.1.call-done, bf16[1024,256]{1,0:T(8,128)(2,1)S(1)} %copy-done), kind=kOutput, calls=%fused_computation.42 | convolution fusion | flops 805306368 | bytes 5242880 | tf_op jit(solution)/shard_map/dot_general | solution.py:260
  117.8 2.3 %draft_step.6 = (bf16[32,256]{1,0:T(8,128)(2,1)S(1)}, bf16[16,32,256]{2,1,0:T(8,128)(2,1)S(1)}, bf16[1024,256]{1,0:T(8,128)(2,1)S(1)}, bf16[1024,256]{1,0:T(8,12...) custom-call(bf16[16,32,256]{2,1,0:T(8,128)(2,1)S(1)} %all_to_all.35.own_ref, ...), custom_call_target="tpu_custom_call" | custom-call | flops 134217728 | bytes 4980736 | tf_op jit(solution)/shard_map/draft_step/pallas_call | solution.py:105
  120.2 13.7 %all_to_all.36.own_ref = bf16[16,32,256]{2,1,0:T(8,128)(2,1)S(1)} all-to-all(bf16[16,32,256]{2,1,0:T(8,128)(2,1)S(1)} %get-tuple-element.35), channel_id=1, replica_groups={{0,8,16,24,32,40,48,56,64,72,80,88,96,104,112,120},{128,136,144,152,160..., dimensions={0} | all-to-all | bytes 524288 | tf_op jit(solution)/shard_map/all_to_all | solution.py:50
  133.9 2.2 %collective-permute-start.12 = (bf16[16,32,256]{2,1,0:T(8,128)(2,1)S(1)}, bf16[16,32,256]{2,1,0:T(8,128)(2,1)S(1)}, u32[]{:S(2)}, u32[]{:S(2)}) collective-permute-start(bf16[16,32,256]{2,1,0:T(8,128)(2,1)S(1)} %all_to_all.36.own_ref), channel_id=1, source_target_pairs={{1,0},{0,1},{3,2},{2,3},{5,4},{4,5},{7,6},{6,7},{9,8},{8,9},{11,10... | collective-permute-start | bytes 786440 | tf_op jit(solution)/shard_map/ppermute | solution.py:46
  138.1 13.0 %all_to_all.37.own_ref = bf16[16,32,256]{2,1,0:T(8,128)(2,1)S(1)} all-to-all(bf16[16,32,256]{2,1,0:T(8,128)(2,1)S(1)} %get-tuple-element.40), channel_id=1, replica_groups={{0,8,16,24,32,40,48,56,64,72,80,88,96,104,112,120},{128,136,144,152,160..., dimensions={0} | all-to-all | bytes 524288 | tf_op jit(solution)/shard_map/all_to_all | solution.py:50
  151.0 2.2 %collective-permute-start.13 = (bf16[16,32,256]{2,1,0:T(8,128)(2,1)S(1)}, bf16[16,32,256]{2,1,0:T(8,128)(2,1)S(1)}, u32[]{:S(2)}, u32[]{:S(2)}) collective-permute-start(bf16[16,32,256]{2,1,0:T(8,128)(2,1)S(1)} %all_to_all.37.own_ref), channel_id=1, source_target_pairs={{1,0},{0,1},{3,2},{2,3},{5,4},{4,5},{7,6},{6,7},{9,8},{8,9},{11,10... | collective-permute-start | bytes 786440 | tf_op jit(solution)/shard_map/ppermute | solution.py:46
  155.2 12.9 %all_to_all.38.own_ref = bf16[16,32,256]{2,1,0:T(8,128)(2,1)S(1)} all-to-all(bf16[16,32,256]{2,1,0:T(8,128)(2,1)S(1)} %get-tuple-element.41), channel_id=1, replica_groups={{0,8,16,24,32,40,48,56,64,72,80,88,96,104,112,120},{128,136,144,152,160..., dimensions={0} | all-to-all | bytes 524288 | tf_op jit(solution)/shard_map/all_to_all | solution.py:50
  168.1 2.2 %collective-permute-start.14 = (bf16[16,32,256]{2,1,0:T(8,128)(2,1)S(1)}, bf16[16,32,256]{2,1,0:T(8,128)(2,1)S(1)}, u32[]{:S(2)}, u32[]{:S(2)}) collective-permute-start(bf16[16,32,256]{2,1,0:T(8,128)(2,1)S(1)} %all_to_all.38.own_ref), channel_id=1, source_target_pairs={{1,0},{0,1},{3,2},{2,3},{5,4},{4,5},{7,6},{6,7},{9,8},{8,9},{11,10... | collective-permute-start | bytes 786440 | tf_op jit(solution)/shard_map/ppermute | solution.py:46
  172.3 4.2 %collective-permute-start.15 = (bf16[5,32,256]{2,1,0:T(8,128)(2,1)S(1)}, bf16[5,32,256]{2,1,0:T(8,128)(2,1)S(1)}, u32[]{:S(2)}, u32[]{:S(2)}) collective-permute-start(bf16[5,32,256]{2,1,0:T(8,128)(2,1)S(1)} %draft_step.9), channel_id=1, source_target_pairs={{0,0},{128,1},{2,2},{130,3},{4,4},{132,5},{6,6},{134,7},{8,8},{136... | collective-permute-start | bytes 245768 | tf_op jit(solution)/shard_map/ppermute | solution.py:46
  176.5 3.0 %collective-permute-done.15 = bf16[5,32,256]{2,1,0:T(8,128)(2,1)S(1)} collective-permute-done((bf16[5,32,256]{2,1,0:T(8,128)(2,1)S(1)}, bf16[5,32,256]{2,1,0:T(8,128)(2,1)S(1)}, u32[]{:S(2)}, u32[]{:S(2)}) %collective-permute-start.15) | collective-permute-done | bytes 81952 | tf_op jit(solution)/shard_map/ppermute | solution.py:46
  (66 shorter events, 23.7 us)
Async XLA Ops:
  7.2 40.4 %copy-start = (bf16[1024,256]{1,0:T(8,128)(2,1)S(1)}, bf16[1024,256]{1,0:T(8,128)(2,1)}, u32[]{:S(2)}) copy-start(bf16[1024,256]{1,0:T(8,128)(2,1)} %param.18) | copy-start | bytes 1572868
  7.2 18.1 %copy-start.1 = (bf16[8,256,128]{2,1,0:T(8,128)(2,1)S(1)}, bf16[8,256,128]{2,1,0:T(8,128)(2,1)}, u32[]{:S(2)}) copy-start(bf16[8,256,128]{2,1,0:T(8,128)(2,1)} %param.14) | copy-start | bytes 1572868
  7.2 105.0 %all-gather.2.cloned.1.call-start = ((), (), s32[]{:S(2)}) async-start(), calls=%async_computation.8 | async-start | bytes 3244032 | tf_op jit(solution)/shard_map/all_gather | solution.py:240
  7.2 17.9 %collective-permute-start.2 = (bf16[1024,256]{1,0:T(8,128)(2,1)}, bf16[1024,256]{1,0:T(8,128)(2,1)S(1)}, u32[]{:S(2)}, u32[]{:S(2)}) collective-permute-start(bf16[1024,256]{1,0:T(8,128)(2,1)} %param.19), channel_id=1, source_target_pairs={{1,0},{129,1},{3,2},{131,3},{5,4},{133,5},{7,6},{135,7},{9,8},{137... | collective-permute-start | bytes 1572872 | tf_op jit(solution)/shard_map/ppermute | solution.py:46
  10.6 14.5 %collective-permute-start.1 = (bf16[1024,256]{1,0:T(8,128)(2,1)}, bf16[1024,256]{1,0:T(8,128)(2,1)S(1)}, u32[]{:S(2)}, u32[]{:S(2)}) collective-permute-start(bf16[1024,256]{1,0:T(8,128)(2,1)} %param.19), channel_id=1, source_target_pairs={{0,0},{128,1},{2,2},{130,3},{4,4},{132,5},{6,6},{134,7},{8,8},{136... | collective-permute-start | bytes 1572872 | tf_op jit(solution)/shard_map/ppermute | solution.py:46
  13.7 11.4 %collective-permute-start = (s32[32]{0:T(128)}, s32[32]{0:T(128)S(1)}, u32[]{:S(2)}, u32[]{:S(2)}) collective-permute-start(s32[32]{0:T(128)} %param.16), channel_id=1, source_target_pairs={{48,0},{56,1},{112,2},{120,3},{176,4},{184,5},{240,6},{248,7},{0,8... | collective-permute-start | bytes 392 | tf_op jit(solution)/shard_map/ppermute | solution.py:46
  25.3 34.8 %copy-start.2 = (bf16[32,6,256]{2,0,1:T(8,128)(2,1)S(1)}, bf16[32,6,256]{2,0,1:T(8,128)(2,1)}, u32[]{:S(2)}) copy-start(bf16[32,6,256]{2,0,1:T(8,128)(2,1)} %param.17) | copy-start | bytes 294916
  27.0 20.5 %all-to-all-start = ((bf16[32,8,1024]{2,1,0:T(8,128)(2,1)}), bf16[32,8,1024]{2,1,0:T(8,128)(2,1)}, u32[]{:S(2)}, u32[]{:S(2)}) async-start(bf16[32,8,1024]{2,1,0:T(8,128)(2,1)} %broadcast_in_dim.80), calls=%async_computation | async-start | bytes 1048576 | tf_op jit(solution)/shard_map/all_to_all | solution.py:17
  35.9 24.3 %collective-permute-start.6 = (bf16[1024,256]{1,0:T(8,128)(2,1)S(1)}, bf16[1024,256]{1,0:T(8,128)(2,1)S(1)}, u32[]{:S(2)}, u32[]{:S(2)}) collective-permute-start(bf16[1024,256]{1,0:T(8,128)(2,1)S(1)} %get-tuple-element.48.refs_1_), channel_id=1, source_target_pairs={{2,0},{3,1},{4,2},{5,3},{6,4},{7,5},{0,6},{1,7},{10,8},{11,9},{12,... | collective-permute-start | bytes 1572872 | tf_op jit(solution)/shard_map/ppermute | solution.py:46
  38.2 22.0 %collective-permute-start.4 = (bf16[1024,256]{1,0:T(8,128)(2,1)S(1)}, bf16[1024,256]{1,0:T(8,128)(2,1)S(1)}, u32[]{:S(2)}, u32[]{:S(2)}) collective-permute-start(bf16[1024,256]{1,0:T(8,128)(2,1)S(1)} %get-tuple-element.48.refs_1_), channel_id=1, source_target_pairs={{6,0},{7,1},{0,2},{1,3},{2,4},{3,5},{4,6},{5,7},{14,8},{15,9},{8,1... | collective-permute-start | bytes 1572872 | tf_op jit(solution)/shard_map/ppermute | solution.py:46
  38.2 22.0 %collective-permute-start.5 = (bf16[1024,256]{1,0:T(8,128)(2,1)S(1)}, bf16[1024,256]{1,0:T(8,128)(2,1)}, u32[]{:S(2)}, u32[]{:S(2)}) collective-permute-start(bf16[1024,256]{1,0:T(8,128)(2,1)S(1)} %get-tuple-element.49.refs_0_), channel_id=1, source_target_pairs={{2,0},{3,1},{4,2},{5,3},{6,4},{7,5},{0,6},{1,7},{10,8},{11,9},{12,... | collective-permute-start | bytes 1572872 | tf_op jit(solution)/shard_map/ppermute | solution.py:46
  40.8 19.5 %collective-permute-start.3 = (bf16[1024,256]{1,0:T(8,128)(2,1)S(1)}, bf16[1024,256]{1,0:T(8,128)(2,1)S(1)}, u32[]{:S(2)}, u32[]{:S(2)}) collective-permute-start(bf16[1024,256]{1,0:T(8,128)(2,1)S(1)} %get-tuple-element.49.refs_0_), channel_id=1, source_target_pairs={{6,0},{7,1},{0,2},{1,3},{2,4},{3,5},{4,6},{5,7},{14,8},{15,9},{8,1... | collective-permute-start | bytes 1572872 | tf_op jit(solution)/shard_map/ppermute | solution.py:46
  49.6 15.8 %all-to-all-start.1 = ((bf16[8,32,256]{2,1,0:T(8,128)(2,1)}), bf16[8,32,256]{2,1,0:T(8,128)(2,1)S(1)}, u32[]{:S(2)}, u32[]{:S(2)}) async-start(bf16[8,32,256]{2,1,0:T(8,128)(2,1)} %bitcast.19), calls=%async_computation.1 | async-start | bytes 262144 | tf_op jit(solution)/shard_map/all_to_all | solution.py:222
  65.5 6.8 %collective-permute-start.7 = (bf16[32,256]{1,0:T(8,128)(2,1)S(1)}, bf16[32,256]{1,0:T(8,128)(2,1)S(1)}, u32[]{:S(2)}, u32[]{:S(2)}) collective-permute-start(bf16[32,256]{1,0:T(8,128)(2,1)S(1)} %add_convert_fusion.1), channel_id=1, source_target_pairs={{0,0},{128,1},{2,2},{130,3},{4,4},{132,5},{6,6},{134,7},{8,8},{136... | collective-permute-start | bytes 49160 | tf_op jit(solution)/shard_map/ppermute | solution.py:46
  73.0 16.6 %all-to-all-start.2 = ((bf16[16,32,256]{2,1,0:T(8,128)(2,1)}), bf16[16,32,256]{2,1,0:T(8,128)(2,1)S(1)}, u32[]{:S(2)}, u32[]{:S(2)}) async-start(bf16[16,32,256]{2,1,0:T(8,128)(2,1)} %broadcast_in_dim.81), calls=%async_computation.2 | async-start | bytes 524288 | tf_op jit(solution)/shard_map/all_to_all | solution.py:50
  80.3 99.3 %reduce-scatter.2.cloned.1.call-start = ((), (), s32[]{:S(2)}) async-start(), calls=%async_computation.9 | async-start | bytes 1769472 | tf_op jit(solution)/shard_map/reduce_scatter | solution.py:261
  80.3 9.7 %collective-permute-start.10 = (bf16[1024,256]{1,0:T(8,128)(2,1)S(1)}, bf16[1024,256]{1,0:T(8,128)(2,1)}, u32[]{:S(2)}, u32[]{:S(2)}) collective-permute-start(bf16[1024,256]{1,0:T(8,128)(2,1)S(1)} %collective-permute-done.6.refs_5_), channel_id=1, source_target_pairs={{2,0},{3,1},{4,2},{5,3},{6,4},{7,5},{0,6},{1,7},{10,8},{11,9},{12,... | collective-permute-start | bytes 1572872 | tf_op jit(solution)/shard_map/ppermute | solution.py:46
  80.5 10.7 %collective-permute-start.9 = (bf16[1024,256]{1,0:T(8,128)(2,1)S(1)}, bf16[1024,256]{1,0:T(8,128)(2,1)}, u32[]{:S(2)}, u32[]{:S(2)}) collective-permute-start(bf16[1024,256]{1,0:T(8,128)(2,1)S(1)} %collective-permute-done.3.refs_2_), channel_id=1, source_target_pairs={{6,0},{7,1},{0,2},{1,3},{2,4},{3,5},{4,6},{5,7},{14,8},{15,9},{8,1... | collective-permute-start | bytes 1572872 | tf_op jit(solution)/shard_map/ppermute | solution.py:46
  89.6 1.7 collective-permute-start.8
  116.2 1.6 collective-permute-start.11
  133.9 3.3 %collective-permute-start.12 = (bf16[16,32,256]{2,1,0:T(8,128)(2,1)S(1)}, bf16[16,32,256]{2,1,0:T(8,128)(2,1)S(1)}, u32[]{:S(2)}, u32[]{:S(2)}) collective-permute-start(bf16[16,32,256]{2,1,0:T(8,128)(2,1)S(1)} %all_to_all.36.own_ref), channel_id=1, source_target_pairs={{1,0},{0,1},{3,2},{2,3},{5,4},{4,5},{7,6},{6,7},{9,8},{8,9},{11,10... | collective-permute-start | bytes 786440 | tf_op jit(solution)/shard_map/ppermute | solution.py:46
  151.0 3.3 %collective-permute-start.13 = (bf16[16,32,256]{2,1,0:T(8,128)(2,1)S(1)}, bf16[16,32,256]{2,1,0:T(8,128)(2,1)S(1)}, u32[]{:S(2)}, u32[]{:S(2)}) collective-permute-start(bf16[16,32,256]{2,1,0:T(8,128)(2,1)S(1)} %all_to_all.37.own_ref), channel_id=1, source_target_pairs={{1,0},{0,1},{3,2},{2,3},{5,4},{4,5},{7,6},{6,7},{9,8},{8,9},{11,10... | collective-permute-start | bytes 786440 | tf_op jit(solution)/shard_map/ppermute | solution.py:46
  168.1 3.3 %collective-permute-start.14 = (bf16[16,32,256]{2,1,0:T(8,128)(2,1)S(1)}, bf16[16,32,256]{2,1,0:T(8,128)(2,1)S(1)}, u32[]{:S(2)}, u32[]{:S(2)}) collective-permute-start(bf16[16,32,256]{2,1,0:T(8,128)(2,1)S(1)} %all_to_all.38.own_ref), channel_id=1, source_target_pairs={{1,0},{0,1},{3,2},{2,3},{5,4},{4,5},{7,6},{6,7},{9,8},{8,9},{11,10... | collective-permute-start | bytes 786440 | tf_op jit(solution)/shard_map/ppermute | solution.py:46
  172.3 7.3 %collective-permute-start.15 = (bf16[5,32,256]{2,1,0:T(8,128)(2,1)S(1)}, bf16[5,32,256]{2,1,0:T(8,128)(2,1)S(1)}, u32[]{:S(2)}, u32[]{:S(2)}) collective-permute-start(bf16[5,32,256]{2,1,0:T(8,128)(2,1)S(1)} %draft_step.9), channel_id=1, source_target_pairs={{0,0},{128,1},{2,2},{130,3},{4,4},{132,5},{6,6},{134,7},{8,8},{136... | collective-permute-start | bytes 245768 | tf_op jit(solution)/shard_map/ppermute | solution.py:46
  (2 other events, 31.7 us)
Sparse Core Ops, SparseCore 0:
  26.3 82.5 all-gather.1
  116.3 31.2 reduce-scatter.1
